TPU v7x, 32 devices: a whole 2x2x4 slice. The times are simulated.
32 devices in a mesh: frames: 8 (over y, x, core), pos: 4 (over z).
Axes of the slice: x: 2, y: 2, z: 4, core: 2. Of those that a mesh axis runs over, the one named last changes fastest.
Arguments:
- frame_rows: bfloat16 [512, 16, 1024], P(('frames', 'pos')), may hold values from -6 to 6
- frame_mask: int32 [512], P(('frames', 'pos')), may hold values from 0 to 1, as said below
- gain_attention: float32 [1024], replicated, may hold values from 0.25 to 1.75
- gain_feed: float32 [1024], replicated, may hold values from 0.25 to 1.75
- qkv_master: float32 [1024, 3072], P(('frames', 'pos')), may hold values from -0.1875 to 0.1875
- out_master: float32 [1024, 1024], P(('frames', 'pos')), may hold values from -0.375 to 0.375
- gate_master: float32 [16, 1024, 2816], P('pos', 'frames'), may hold values from -0.1875 to 0.1875
- up_master: float32 [16, 1024, 2816], P('pos', 'frames'), may hold values from -0.1875 to 0.1875
- down_master: float32 [16, 2816, 1024], P('pos', 'frames'), may hold values from -0.109375 to 0.109375
- out_cotangent: bfloat16 [512, 16, 1024], P(('frames', 'pos')), may hold values from -6 to 6
Outputs:
- block_out: bfloat16 [512, 16, 1024], P(('frames', 'pos'))
- rows_grad: float32 [512, 16, 1024], P(('frames', 'pos'))
- gain_attention_grad: float32 [1024], P(('frames', 'pos'))
- gain_feed_grad: float32 [1024], P(('frames', 'pos'))
- qkv_grad: float32 [1024, 3072], P(('frames', 'pos'))
- out_proj_grad: float32 [1024, 1024], P(('frames', 'pos'))
- gate_grad: float32 [16, 1024, 2816], P('pos', 'frames')
- up_grad: float32 [16, 1024, 2816], P('pos', 'frames')
- down_grad: float32 [16, 2816, 1024], P('pos', 'frames')
Inputs may be any that keep to these rules, and one draw needn't show every extreme that they name: `frame_mask`: in each aligned block of 16 frames the live frames come first and are at least half of the block; some block is all live.
All inputs are finite; a program needn't handle non-finite values.
Results may differ from a plain program's by a relative error of at most 0.013.
Values may be sent and summed in bfloat16 or wider, within the bound.
A program may use at most 384 MiB of HBM per device.

v0:
```python
import math

import jax
import jax.numpy as jnp
from jax import lax
from jax.sharding import PartitionSpec as P

H = 16
HD = 64


HIGHEST = lax.Precision.HIGHEST


def rms_norm(values, gain_vector):
    return (
        values * lax.rsqrt(jnp.mean(values * values, axis=-1, keepdims=True) + 1e-05) * gain_vector
    )


def attend(qkv_rows):
    frame_count = qkv_rows.shape[0]
    positions = qkv_rows.shape[1]
    split_rows = qkv_rows.reshape(frame_count, positions, 3, H, HD)
    queries = split_rows[:, :, 0]
    keys_all = split_rows[:, :, 1]
    values_all = split_rows[:, :, 2]
    scores = jnp.einsum("fqhe,fkhe->fhqk", queries, keys_all, precision=HIGHEST) * (
        1.0 / math.sqrt(HD)
    )
    causal = jnp.arange(positions)[:, None] >= jnp.arange(positions)[None, :]
    scores = jnp.where(causal, scores, -1e30)
    weights = jax.nn.softmax(scores, axis=-1)
    mixed = jnp.einsum("fhqk,fkhe->fqhe", weights, values_all, precision=HIGHEST)
    return mixed.reshape(frame_count, positions, H * HD)


def gate_up_term_for(position_rows, joint_rows):
    return jnp.einsum("fd,fh->dh", position_rows, joint_rows, preferred_element_type=jnp.float32)


def down_term_for(hidden_rows, upstream_rows):
    return jnp.einsum("fh,fd->hd", hidden_rows, upstream_rows, preferred_element_type=jnp.float32)


def local(
    frame_rows,
    frame_mask,
    gain_attention,
    gain_feed,
    qkv_master,
    out_master,
    gate_master,
    up_master,
    down_master,
    out_cotangent,
):
    keep_rows = frame_mask.astype(jnp.float32)[:, None, None]
    inputs = frame_rows.astype(jnp.float32)
    gate_low = gate_master.astype(jnp.bfloat16)
    up_low = up_master.astype(jnp.bfloat16)
    down_low = down_master.astype(jnp.bfloat16)
    ff_width = gate_master.shape[2]
    w_qkv, w_out = (
        lax.all_gather(qkv_master.astype(jnp.bfloat16), ("frames", "pos"), axis=0, tiled=True),
        lax.all_gather(out_master.astype(jnp.bfloat16), ("frames", "pos"), axis=0, tiled=True),
    )
    normed_one, norm_one_pull = jax.vjp(rms_norm, inputs, gain_attention)
    normed_low = normed_one.astype(jnp.bfloat16)
    qkv_rows = jnp.einsum("fpd,de->fpe", normed_low, w_qkv, preferred_element_type=jnp.float32)
    mixed, attend_pull = jax.vjp(attend, qkv_rows)
    mixed_low = mixed.astype(jnp.bfloat16)
    branch = jnp.einsum("fpd,de->fpe", mixed_low, w_out, preferred_element_type=jnp.float32)
    middle = inputs + branch
    normed_two, norm_two_pull = jax.vjp(rms_norm, middle, gain_feed)
    sent = lax.all_to_all(
        normed_two.astype(jnp.bfloat16), "pos", split_axis=1, concat_axis=0, tiled=True
    )
    local_pos = sent.shape[1]
    pieces = (
        lax.all_gather(gate_low, "frames", axis=1, tiled=True),
        lax.all_gather(up_low, "frames", axis=1, tiled=True),
    )
    columns = sent
    gate_rows = jnp.einsum("fpd,pdh->fph", columns, pieces[0], preferred_element_type=jnp.float32)
    up_rows = jnp.einsum("fpd,pdh->fph", columns, pieces[1], preferred_element_type=jnp.float32)
    sigma = jax.nn.sigmoid(gate_rows)
    silu_gate = gate_rows * sigma
    hidden = (silu_gate * up_rows).astype(jnp.bfloat16)
    columns = hidden
    feed_rows = jnp.einsum(
        "fph,phd->fpd",
        columns,
        lax.all_gather(down_low, "frames", axis=1, tiled=True),
        preferred_element_type=jnp.float32,
    )
    returned = lax.all_to_all(
        feed_rows.astype(jnp.bfloat16), "pos", split_axis=0, concat_axis=1, tiled=True
    )
    block_out = (keep_rows * (middle + returned.astype(jnp.float32))).astype(jnp.bfloat16)
    upstream = keep_rows * out_cotangent.astype(jnp.float32)
    down_upstream = lax.all_to_all(
        upstream.astype(jnp.bfloat16), "pos", split_axis=1, concat_axis=0, tiled=True
    )
    hidden_grad = jnp.einsum(
        "fpd,phd->fph",
        down_upstream,
        lax.all_gather(down_low, "frames", axis=1, tiled=True),
        preferred_element_type=jnp.float32,
    )
    gate_back = (hidden_grad * up_rows * sigma * (1.0 + gate_rows * (1.0 - sigma))).astype(
        jnp.bfloat16
    )
    up_back = (hidden_grad * silu_gate).astype(jnp.bfloat16)
    pieces = (
        lax.all_gather(gate_low, "frames", axis=1, tiled=True),
        lax.all_gather(up_low, "frames", axis=1, tiled=True),
    )
    contribution = jnp.einsum(
        "fph,pdh->fpd", gate_back, pieces[0], preferred_element_type=jnp.float32
    ) + jnp.einsum("fph,pdh->fpd", up_back, pieces[1], preferred_element_type=jnp.float32)
    back_rows = lax.all_to_all(
        contribution.astype(jnp.bfloat16), "pos", split_axis=0, concat_axis=1, tiled=True
    )
    joint = jnp.concatenate((gate_back, up_back), axis=2)
    gate_parts = []
    up_parts = []
    down_parts = []
    for position in range(local_pos):
        summed = lax.psum_scatter(
            gate_up_term_for(sent[:, position, :], joint[:, position, :]).astype(jnp.bfloat16),
            "frames",
            scatter_dimension=0,
            tiled=True,
        ).astype(jnp.float32)
        gate_parts.append(summed[:, :ff_width])
        up_parts.append(summed[:, ff_width:])
        down_parts.append(
            lax.psum_scatter(
                down_term_for(hidden[:, position, :], down_upstream[:, position, :]).astype(
                    jnp.bfloat16
                ),
                "frames",
                scatter_dimension=0,
                tiled=True,
            ).astype(jnp.float32)
        )
    pulled_two = norm_two_pull(back_rows.astype(jnp.float32))
    middle_grad = upstream + pulled_two[0]
    branch_grad = middle_grad.astype(jnp.bfloat16)
    out_weight_grad = jnp.einsum(
        "fpd,fpe->de", mixed_low, branch_grad, preferred_element_type=jnp.float32
    )
    mixed_grad = jnp.einsum("fpe,de->fpd", branch_grad, w_out, preferred_element_type=jnp.float32)
    qkv_back = attend_pull(mixed_grad)[0].astype(jnp.bfloat16)
    qkv_weight_grad = jnp.einsum(
        "fpd,fpe->de", normed_low, qkv_back, preferred_element_type=jnp.float32
    )
    normed_grad = jnp.einsum("fpe,de->fpd", qkv_back, w_qkv, preferred_element_type=jnp.float32)
    pulled_one = norm_one_pull(normed_grad)
    rows_grad = middle_grad + pulled_one[0]
    shares = (
        lax.psum_scatter(qkv_weight_grad, ("frames", "pos"), scatter_dimension=0, tiled=True),
        lax.psum_scatter(out_weight_grad, ("frames", "pos"), scatter_dimension=0, tiled=True),
        lax.psum_scatter(pulled_one[1], ("frames", "pos"), scatter_dimension=0, tiled=True),
        lax.psum_scatter(pulled_two[1], ("frames", "pos"), scatter_dimension=0, tiled=True),
    )
    return (
        block_out,
        rows_grad,
        shares[2],
        shares[3],
        shares[0],
        shares[1],
        jnp.stack(gate_parts, axis=0),
        jnp.stack(up_parts, axis=0),
        jnp.stack(down_parts, axis=0),
    )


def solution(mesh):
    in_specs = (
        P(("frames", "pos"), None, None),
        P(("frames", "pos")),
        P(),
        P(),
        P(("frames", "pos"), None),
        P(("frames", "pos"), None),
        P("pos", "frames", None),
        P("pos", "frames", None),
        P("pos", "frames", None),
        P(("frames", "pos"), None, None),
    )
    out_specs = (
        P(("frames", "pos"), None, None),
        P(("frames", "pos"), None, None),
        P(("frames", "pos")),
        P(("frames", "pos")),
        P(("frames", "pos"), None),
        P(("frames", "pos"), None),
        P("pos", "frames", None),
        P("pos", "frames", None),
        P("pos", "frames", None),
    )
    return jax.shard_map(local, mesh=mesh, in_specs=in_specs, out_specs=out_specs, check_vma=False)
```

profile of v0, /device:TPU:0, one launch (start us, length us, event | category | flops | bytes accessed | tf_op | source)
XLA Modules:
  0.0 1446.9 jit_solution(6116066839153031749)
XLA Ops:
  33.8 52.9 %all-gather.6.cloned.1.call-done = bf16[1024,3072]{1,0:T(8,128)(2,1)} async-done(((bf16[32,3072]{1,0:T(8,128)(2,1)}), bf16[1024,3072]{1,0:T(8,128)(2,1)}) %all-gather.6.cloned.1.call-update) | async-done | bytes 6291472 | tf_op jit(solution)/shard_map/all_gather | solution.py:65
  113.6 31.6 %all-gather.8.cloned.1.call-done = bf16[1024,1024]{1,0:T(8,128)(2,1)} async-done(((bf16[32,1024]{1,0:T(8,128)(2,1)}), bf16[1024,1024]{1,0:T(8,128)(2,1)}) %all-gather.8.cloned.1.call-update) | async-done | bytes 2097168 | tf_op jit(solution)/shard_map/all_gather | solution.py:66
  154.5 14.2 all-to-all-done
  168.7 94.3 %all-gather.10.cloned.1.call-done = bf16[4,1024,2816]{2,1,0:T(8,128)(2,1)} async-done(((bf16[4,128,2816]{2,1,0:T(8,128)(2,1)}), bf16[4,1024,2816]{2,1,0:T(8,128)(2,1)}) %all-gather.10.cloned.1.call-update) | async-done | bytes 23068688 | tf_op jit(solution)/shard_map/all_gather | solution.py:81
  263.0 13.2 convolution_bitcast_fusion.3
  276.2 105.6 %all-gather.12.cloned.1.call-done = bf16[4,1024,2816]{2,1,0:T(8,128)(2,1)} async-done(((bf16[4,128,2816]{2,1,0:T(8,128)(2,1)}), bf16[4,1024,2816]{2,1,0:T(8,128)(2,1)}) %all-gather.12.cloned.1.call-update) | async-done | bytes 23068688 | tf_op jit(solution)/shard_map/all_gather | solution.py:82
  381.9 13.2 convolution_bitcast_fusion.2
  395.1 105.1 %all-gather.14.cloned.1.call-done = bf16[4,2816,1024]{2,1,0:T(8,128)(2,1)} async-done(((bf16[4,352,1024]{2,1,0:T(8,128)(2,1)}), bf16[4,2816,1024]{2,1,0:T(8,128)(2,1)}) %all-gather.14.cloned.1.call-update) | async-done | bytes 23068688 | tf_op jit(solution)/shard_map/all_gather | solution.py:94
  500.1 13.9 multiply_convert_fusion
  535.5 7.1 convolution_convert_fusion
  564.0 12.4 fusion.65
  576.3 11.7 fusion.33
  593.9 12.6 fusion.32
  613.3 14.0 all-to-all-done.1
  642.7 7.5 multiply_reduce_fusion
  666.3 8.1 convolution_bitcast_fusion
  681.9 37.6 %all-reduce.5 = (f32[1024]{0:T(1024)S(1)}, f32[1024]{0:T(1024)S(1)}) all-reduce(f32[1024]{0:T(1024)S(1)} %get-tuple-element.11, f32[1024]{0:T(1024)S(1)} %copy-done.35), channel_id=2, replica_groups=mesh['frames'=8,'pos'=4] {'frames','pos'}, use_global_device_ids=true, to_apply=%region_8.9.clone | all-reduce | flops 2048 | bytes 16384
  723.3 44.9 %reduce-scatter.23.cloned.1.call-done = bf16[352,1024]{1,0:T(8,128)(2,1)} async-done(((bf16[2816,1024]{1,0:T(8,128)(2,1)}), bf16[352,1024]{1,0:T(8,128)(2,1)}) %reduce-scatter.23.cloned.1.call-update) | async-done | bytes 720912 | tf_op jit(solution)/shard_map/reduce_scatter | solution.py:139
  773.0 85.4 %reduce-scatter.21.cloned.1.call-done = bf16[128,5632]{1,0:T(8,128)(2,1)} async-done(((bf16[1024,5632]{1,0:T(8,128)(2,1)}), bf16[128,5632]{1,0:T(8,128)(2,1)}) %reduce-scatter.21.cloned.1.call-update) | async-done | bytes 1441808 | tf_op jit(solution)/shard_map/reduce_scatter | solution.py:130
  860.1 88.7 %reduce-scatter.19.cloned.1.call-done = bf16[128,5632]{1,0:T(8,128)(2,1)} async-done(((bf16[1024,5632]{1,0:T(8,128)(2,1)}), bf16[128,5632]{1,0:T(8,128)(2,1)}) %reduce-scatter.19.cloned.1.call-update) | async-done | bytes 1441808 | tf_op jit(solution)/shard_map/reduce_scatter | solution.py:130
  952.0 87.0 %reduce-scatter.17.cloned.1.call-done = bf16[128,5632]{1,0:T(8,128)(2,1)} async-done(((bf16[1024,5632]{1,0:T(8,128)(2,1)}), bf16[128,5632]{1,0:T(8,128)(2,1)}) %reduce-scatter.17.cloned.1.call-update) | async-done | bytes 1441808 | tf_op jit(solution)/shard_map/reduce_scatter | solution.py:130
  1042.2 87.1 %reduce-scatter.15.cloned.1.call-done = bf16[128,5632]{1,0:T(8,128)(2,1)} async-done(((bf16[1024,5632]{1,0:T(8,128)(2,1)}), bf16[128,5632]{1,0:T(8,128)(2,1)}) %reduce-scatter.15.cloned.1.call-update) | async-done | bytes 1441808 | tf_op jit(solution)/shard_map/reduce_scatter | solution.py:130
  1139.8 139.6 %reduce-scatter.13.cloned.1.call-done = f32[32,1024]{1,0:T(8,128)} async-done(((f32[1024,1024]{1,0:T(8,128)}), f32[32,1024]{1,0:T(8,128)}) %reduce-scatter.13.cloned.1.call-update) | async-done | bytes 131088 | tf_op jit(solution)/shard_map/reduce_scatter | solution.py:164
  1279.4 160.8 %reduce-scatter.11.cloned.1.call-done = f32[32,3072]{1,0:T(8,128)} async-done(((f32[1024,3072]{1,0:T(8,128)}), f32[32,3072]{1,0:T(8,128)}) %reduce-scatter.11.cloned.1.call-update) | async-done | bytes 393232 | tf_op jit(solution)/shard_map/reduce_scatter | solution.py:163
  (188 shorter events, 183.8 us)
Async XLA Ops:
  7.2 79.5 %all-gather.6.cloned.1.call-start = ((), (), s32[]{:S(2)}) async-start(), calls=%async_computation.14 | async-start | bytes 6488064 | tf_op jit(solution)/shard_map/all_gather | solution.py:65
  8.9 136.3 %all-gather.8.cloned.1.call-start = ((), (), s32[]{:S(2)}) async-start(), calls=%async_computation.15 | async-start | bytes 2162688 | tf_op jit(solution)/shard_map/all_gather | solution.py:66
  10.6 252.5 %all-gather.10.cloned.1.call-start = ((), (), s32[]{:S(2)}) async-start(), calls=%async_computation.16 | async-start | bytes 25952256 | tf_op jit(solution)/shard_map/all_gather | solution.py:81
  15.1 366.7 %all-gather.12.cloned.1.call-start = ((), (), s32[]{:S(2)}) async-start(), calls=%async_computation.17 | async-start | bytes 25952256 | tf_op jit(solution)/shard_map/all_gather | solution.py:82
  19.7 480.4 %all-gather.14.cloned.1.call-start = ((), (), s32[]{:S(2)}) async-start(), calls=%async_computation.18 | async-start | bytes 25952256 | tf_op jit(solution)/shard_map/all_gather | solution.py:94
  25.1 61.6 %copy-start.36 = (f32[1024]{0:T(1024)S(1)}, f32[1024]{0:T(1024)}, u32[]{:S(2)}) copy-start(f32[1024]{0:T(1024)} %param.12) | copy-start | bytes 12292
  27.1 122.9 %all-to-all-start.2 = ((bf16[16,16,1024]{2,0,1:T(8,128)(2,1)}), bf16[16,16,1024]{2,0,1:T(8,128)(2,1)S(1)}, u32[]{:S(2)}, u32[]{:S(2)}) async-start(bf16[16,16,1024]{2,0,1:T(8,128)(2,1)} %copy.50), calls=%async_computation.2 | async-start | bytes 1048576 | tf_op jit(solution)/shard_map/all_to_all | solution.py:102
  33.6 74.7 %copy-start.33 = (pred[16,16]{0,1:T(8,128)(4,1)}, pred[16,16]{0,1:T(8,128)(4,1)S(1)}, u32[]{:S(2)}) copy-start(pred[16,16]{0,1:T(8,128)(4,1)S(1)} %iota_compare_fusion) | copy-start | bytes 772
  33.8 59.3 %copy-start.27 = (f32[16,16]{1,0:T(8,128)}, f32[16,16]{1,0:T(8,128)S(1)}, u32[]{:S(2)}) copy-start(f32[16,16]{1,0:T(8,128)S(1)} %fusion.38) | copy-start | bytes 3076
  33.8 59.2 %copy-start.31 = (f32[16,16]{1,0:T(8,128)}, f32[16,16]{1,0:T(8,128)S(1)}, u32[]{:S(2)}) copy-start(f32[16,16]{1,0:T(8,128)S(1)} %fusion.57) | copy-start | bytes 3076
  150.0 18.6 %all-to-all-start = ((bf16[16,16,1024]{2,0,1:T(8,128)(2,1)}), bf16[16,16,1024]{2,0,1:T(8,128)(2,1)S(1)}, u32[]{:S(2)}, u32[]{:S(2)}) async-start(bf16[16,16,1024]{2,0,1:T(8,128)(2,1)} %copy.46), calls=%async_computation | async-start | bytes 1048576 | tf_op jit(solution)/shard_map/all_to_all | solution.py:76
  153.6 569.8 %reduce-scatter.29.cloned.1.call-start = ((), (), s32[]{:S(2)}) async-start(), calls=%async_computation.28 | async-start | bytes 6488064 | tf_op jit(solution)/shard_map/reduce_scatter | solution.py:139
  519.2 204.2 %reduce-scatter.27.cloned.1.call-start = ((), (), s32[]{:S(2)}) async-start(), calls=%async_computation.27 | async-start | bytes 6488064 | tf_op jit(solution)/shard_map/reduce_scatter | solution.py:139
  524.8 198.6 %reduce-scatter.25.cloned.1.call-start = ((), (), s32[]{:S(2)}) async-start(), calls=%async_computation.26 | async-start | bytes 6488064 | tf_op jit(solution)/shard_map/reduce_scatter | solution.py:139
  530.2 238.0 %reduce-scatter.23.cloned.1.call-start = ((), (), s32[]{:S(2)}) async-start(), calls=%async_computation.25 | async-start | bytes 6488064 | tf_op jit(solution)/shard_map/reduce_scatter | solution.py:139
  535.4 323.0 %reduce-scatter.21.cloned.1.call-start = ((), (), s32[]{:S(2)}) async-start(), calls=%async_computation.24 | async-start | bytes 12976128 | tf_op jit(solution)/shard_map/reduce_scatter | solution.py:130
  542.6 406.2 %reduce-scatter.19.cloned.1.call-start = ((), (), s32[]{:S(2)}) async-start(), calls=%async_computation.23 | async-start | bytes 12976128 | tf_op jit(solution)/shard_map/reduce_scatter | solution.py:130
  549.7 489.2 %reduce-scatter.17.cloned.1.call-start = ((), (), s32[]{:S(2)}) async-start(), calls=%async_computation.22 | async-start | bytes 12976128 | tf_op jit(solution)/shard_map/reduce_scatter | solution.py:130
  556.7 572.5 %reduce-scatter.15.cloned.1.call-start = ((), (), s32[]{:S(2)}) async-start(), calls=%async_computation.21 | async-start | bytes 12976128 | tf_op jit(solution)/shard_map/reduce_scatter | solution.py:130
  589.3 19.5 %all-to-all-start.3 = ((bf16[64,4,1024]{2,1,0:T(4,128)(2,1)}), bf16[64,4,1024]{2,1,0:T(4,128)(2,1)S(1)}, u32[]{:S(2)}, u32[]{:S(2)}) async-start(bf16[64,4,1024]{2,1,0:T(4,128)(2,1)} %copy.52), calls=%async_computation.3 | async-start | bytes 1048576 | tf_op jit(solution)/shard_map/all_to_all | solution.py:122
  608.8 18.5 %all-to-all-start.1 = ((bf16[64,4,1024]{2,1,0:T(4,128)(2,1)}), bf16[64,4,1024]{2,1,0:T(4,128)(2,1)S(1)}, u32[]{:S(2)}, u32[]{:S(2)}) async-start(bf16[64,4,1024]{2,1,0:T(4,128)(2,1)} %copy.48), calls=%async_computation.1 | async-start | bytes 1048576 | tf_op jit(solution)/shard_map/all_to_all | solution.py:97
  612.8 666.6 %reduce-scatter.13.cloned.1.call-start = ((), (), s32[]{:S(2)}) async-start(), calls=%async_computation.20 | async-start | bytes 4325376 | tf_op jit(solution)/shard_map/reduce_scatter | solution.py:164
  636.0 804.2 %reduce-scatter.11.cloned.1.call-start = ((), (), s32[]{:S(2)}) async-start(), calls=%async_computation.19 | async-start | bytes 12976128 | tf_op jit(solution)/shard_map/reduce_scatter | solution.py:163
  676.0 44.8 %copy-start.7 = (f32[16,16,1024]{2,1,0:T(8,128)S(1)}, f32[16,16,1024]{2,1,0:T(8,128)}, u32[]{:S(2)}) copy-start(f32[16,16,1024]{2,1,0:T(8,128)} %copy-done.6) | copy-start | bytes 3145732
  (36 other events, 246.6 us)
Sparse Core Ops, SparseCore 0:
  11.5 75.1 all-gather.5
  90.2 54.9 all-gather.7
  147.7 115.3 all-gather.9
  265.4 116.4 all-gather.11
  383.6 116.4 all-gather.13
  519.3 59.0 reduce-scatter.28
  582.8 59.0 reduce-scatter.26
  645.9 59.4 reduce-scatter.24
  709.2 59.0 reduce-scatter.22
  771.6 86.7 reduce-scatter.20
  861.9 86.7 reduce-scatter.18
  952.1 86.7 reduce-scatter.16
  1042.4 86.7 reduce-scatter.14
  1132.0 147.3 reduce-scatter.12
  1285.8 154.3 reduce-scatter.10
where the time goes:
time: 1450 us
  waiting for transfers between devices  1110 us (77%)
  matrix products  181 us (12%)
  other arithmetic  44.5 us (3%)
  blocking collectives  37.6 us (3%)
  local copies, waits for them, and re-layouts  37 us (3%)
  starting transfers between devices  19.7 us (1%)
  between operations  14.7 us (1%)
    reduce_scatter x4, waiting for transfers between devices, local(): lax.psum_scatter(gate_up_term_for(sent[:, position, :], joint[:, position...  348 us
    reduce_scatter x1, waiting for transfers between devices, local(): lax.psum_scatter(qkv_weight_grad, ('frames', 'pos'), scatter_dimension=0,...  161 us
    reduce_scatter x1, waiting for transfers between devices, local(): lax.psum_scatter(out_weight_grad, ('frames', 'pos'), scatter_dimension=0,...  140 us
    all_gather x1, waiting for transfers between devices, local(): lax.all_gather(up_low, 'frames', axis=1, tiled=True)  106 us
    all_gather x1, waiting for transfers between devices, local(): lax.all_gather(down_low, 'frames', axis=1, tiled=True)  105 us
    all_gather x1, waiting for transfers between devices, local(): lax.all_gather(gate_low, 'frames', axis=1, tiled=True)  94.3 us
    all_gather x1, waiting for transfers between devices, local(): lax.all_gather(qkv_master.astype(jnp.bfloat16), ('frames', 'pos'), axis=0...  52.9 us
    reduce_scatter x4, waiting for transfers between devices, local(): lax.psum_scatter(down_term_for(hidden[:, position, :], down_upstream[:, p...  44.9 us
  transfers between devices with their start and end apart: 19, of which 15 were waited for; matrix products, arithmetic and copies ran while one was open for 16% of the time, Pallas kernels for 0%

commit v1 on v0

v1 whole, which is shorter than its diff:
```python
import math

import jax
import jax.numpy as jnp
from jax import lax
from jax.sharding import PartitionSpec as P

H = 16
HD = 64
BF = jnp.bfloat16
F32 = jnp.float32


def rms_norm(values, gain_vector):
    return (
        values * lax.rsqrt(jnp.mean(values * values, axis=-1, keepdims=True) + 1e-05) * gain_vector
    )


def attend(qkv_rows):
    frame_count = qkv_rows.shape[0]
    positions = qkv_rows.shape[1]
    split_rows = qkv_rows.reshape(frame_count, positions, 3, H, HD)
    queries = split_rows[:, :, 0]
    keys_all = split_rows[:, :, 1]
    values_all = split_rows[:, :, 2]
    scores = jnp.einsum("fqhe,fkhe->fhqk", queries, keys_all, preferred_element_type=F32) * (
        1.0 / math.sqrt(HD)
    )
    causal = jnp.arange(positions)[:, None] >= jnp.arange(positions)[None, :]
    scores = jnp.where(causal, scores, -1e30)
    weights = jax.nn.softmax(scores, axis=-1)
    mixed = jnp.einsum("fhqk,fkhe->fqhe", weights, values_all, preferred_element_type=F32)
    return mixed.reshape(frame_count, positions, H * HD)


def local(
    frame_rows,
    frame_mask,
    gain_attention,
    gain_feed,
    qkv_master,
    out_master,
    gate_master,
    up_master,
    down_master,
    out_cotangent,
):
    nf = lax.axis_size("frames")
    nz = lax.axis_size("pos")
    lp, dslice, ff = gate_master.shape
    ffs = down_master.shape[1]
    fr, npos, d = frame_rows.shape

    keep_rows = frame_mask.astype(F32)[:, None, None]
    inputs = frame_rows.astype(F32)

    def turned(w):
        return w.astype(BF).reshape(lp, dslice, nf, ffs).transpose(2, 0, 3, 1)

    def untwist(w):
        return w.transpose(1, 2, 0, 3).reshape(lp, ffs, d)

    def to_pos(rows):
        moved = rows.transpose(1, 0, 2).reshape(nz, lp, fr, d)
        return lax.all_to_all(moved, "pos", split_axis=0, concat_axis=0, tiled=True)

    def gathered(rows):
        every = lax.all_gather(rows, "frames", axis=0, tiled=False)
        return every.transpose(2, 0, 1, 3, 4).reshape(lp, nf * nz * fr, d)

    def scattered(rows):
        moved = rows.reshape(lp, nf, nz, fr, d).transpose(1, 2, 0, 3, 4)
        summed = lax.psum_scatter(moved, "frames", scatter_dimension=0, tiled=False)
        back = lax.all_to_all(summed.astype(BF), "pos", split_axis=0, concat_axis=0, tiled=True)
        return back.reshape(npos, fr, d).transpose(1, 0, 2)

    both = jnp.concatenate((qkv_master.astype(BF), out_master.astype(BF)), axis=1)
    w_all = lax.all_gather(both, ("frames", "pos"), axis=0, tiled=True)
    w_qkv = w_all[:, : 3 * d]
    w_out = w_all[:, 3 * d :]
    pair = jnp.stack((turned(gate_master), turned(up_master)), axis=1)
    pair = lax.all_to_all(pair, "frames", split_axis=0, concat_axis=0, tiled=True)
    gate_t = untwist(pair[:, 0])
    up_t = untwist(pair[:, 1])
    down = down_master.astype(BF)
    upstream = keep_rows * out_cotangent.astype(F32)
    gy = gathered(to_pos(upstream.astype(BF)))

    normed_one, norm_one_pull = jax.vjp(rms_norm, inputs, gain_attention)
    normed_low = normed_one.astype(BF)
    qkv_rows = jnp.einsum("fpd,de->fpe", normed_low, w_qkv, preferred_element_type=F32)
    mixed, attend_pull = jax.vjp(attend, qkv_rows)
    mixed_low = mixed.astype(BF)
    branch = jnp.einsum("fpd,de->fpe", mixed_low, w_out, preferred_element_type=F32)
    middle = inputs + branch
    normed_two, norm_two_pull = jax.vjp(rms_norm, middle, gain_feed)
    b = gathered(to_pos(normed_two.astype(BF)))

    gate_rows = jnp.einsum("prd,phd->phr", b, gate_t, preferred_element_type=F32)
    up_rows = jnp.einsum("prd,phd->phr", b, up_t, preferred_element_type=F32)
    hidden_grad = jnp.einsum("prd,phd->phr", gy, down, preferred_element_type=F32)
    sigma = jax.nn.sigmoid(gate_rows)
    silu_gate = gate_rows * sigma
    hidden = (silu_gate * up_rows).astype(BF)
    gate_back = (hidden_grad * up_rows * sigma * (1.0 + gate_rows * (1.0 - sigma))).astype(BF)
    up_back = (hidden_grad * silu_gate).astype(BF)
    db = jnp.einsum("phr,phd->prd", gate_back, gate_t, preferred_element_type=F32) + jnp.einsum(
        "phr,phd->prd", up_back, up_t, preferred_element_type=F32
    )
    back_rows = scattered(db.astype(BF)).astype(F32)
    feed = jnp.einsum("phr,phd->prd", hidden, down, preferred_element_type=F32)
    returned = scattered(feed.astype(BF)).astype(F32)
    block_out = (keep_rows * (middle + returned)).astype(BF)
    gate_grad = jnp.einsum("phr,prd->phd", gate_back, b, preferred_element_type=F32).astype(BF)
    up_grad = jnp.einsum("phr,prd->phd", up_back, b, preferred_element_type=F32).astype(BF)
    down_grad = jnp.einsum("phr,prd->phd", hidden, gy, preferred_element_type=F32)

    grads = jnp.stack((gate_grad, up_grad), axis=0).reshape(2, lp, ffs, nf, dslice)
    grads = lax.all_to_all(
        grads.transpose(3, 0, 1, 2, 4), "frames", split_axis=0, concat_axis=0, tiled=True
    )
    grads = grads.transpose(1, 2, 4, 0, 3).reshape(2, lp, dslice, ff).astype(F32)

    pulled_two = norm_two_pull(back_rows)
    middle_grad = upstream + pulled_two[0]
    branch_grad = middle_grad.astype(BF)
    out_weight_grad = jnp.einsum("fpd,fpe->de", mixed_low, branch_grad, preferred_element_type=F32)
    mixed_grad = jnp.einsum("fpe,de->fpd", branch_grad, w_out, preferred_element_type=F32)
    qkv_back = attend_pull(mixed_grad)[0].astype(BF)
    qkv_weight_grad = jnp.einsum("fpd,fpe->de", normed_low, qkv_back, preferred_element_type=F32)
    normed_grad = jnp.einsum("fpe,de->fpd", qkv_back, w_qkv, preferred_element_type=F32)
    pulled_one = norm_one_pull(normed_grad)
    rows_grad = middle_grad + pulled_one[0]

    gains = jnp.stack((pulled_one[1], pulled_two[1]), axis=1)
    gains_hi = gains.astype(BF)
    gains_lo = (gains - gains_hi.astype(F32)).astype(BF)
    tail = jnp.concatenate((gains_hi, gains_lo, jnp.zeros((d, 124), BF)), axis=1)
    total = jnp.concatenate(
        (qkv_weight_grad.astype(BF), out_weight_grad.astype(BF), tail), axis=1
    )
    total = lax.psum_scatter(total, "frames", scatter_dimension=0, tiled=True)
    total = lax.psum_scatter(total, "pos", scatter_dimension=0, tiled=True).astype(F32)
    gain_grads = total[:, 4 * d : 4 * d + 2] + total[:, 4 * d + 2 : 4 * d + 4]
    return (
        block_out,
        rows_grad,
        gain_grads[:, 0],
        gain_grads[:, 1],
        total[:, : 3 * d],
        total[:, 3 * d : 4 * d],
        grads[0],
        grads[1],
        down_grad,
    )
def solution(mesh):
    in_specs = (
        P(("frames", "pos"), None, None),
        P(("frames", "pos")),
        P(),
        P(),
        P(("frames", "pos"), None),
        P(("frames", "pos"), None),
        P("pos", "frames", None),
        P("pos", "frames", None),
        P("pos", "frames", None),
        P(("frames", "pos"), None, None),
    )
    out_specs = (
        P(("frames", "pos"), None, None),
        P(("frames", "pos"), None, None),
        P(("frames", "pos")),
        P(("frames", "pos")),
        P(("frames", "pos"), None),
        P(("frames", "pos"), None),
        P("pos", "frames", None),
        P("pos", "frames", None),
        P("pos", "frames", None),
    )
    return jax.shard_map(local, mesh=mesh, in_specs=in_specs, out_specs=out_specs, check_vma=False)
```

time: 1450 us -> 616 us (0.42)
  waiting for transfers between devices: 1110 us -> 259 us
  matrix products: 181 us -> 69.4 us
  blocking collectives: 37.6 us -> 125 us
  local copies, waits for them, and re-layouts: 37 us -> 95.5 us
  other arithmetic: 44.5 us -> 28 us
    reduce_scatter x10 -> x4, waiting for transfers between devices: 693 us -> 192 us  [the longest x1 102 us: local(): total = lax.psum_scatter(total, 'frames', scatter_dimension=0, tiled=True)]
    all_gather x5 -> x3, waiting for transfers between devices: 390 us -> 53.7 us  [the longest x1 53.6 us: local(): w_all = lax.all_gather(both, ('frames', 'pos'), axis=0, tiled=True)]
    all_to_all x0 -> x3, blocking collectives: none -> 125 us  [the longest x1 80.5 us: local(): lax.all_to_all(pair, 'frames', split_axis=0, concat_axis=0, tiled=True)]
    dot_general x25 -> x20, matrix products: 178 us -> 67.3 us  [the longest x1 7.43 us: local(): jnp.einsum('prd,phd->phr', gy, down, preferred_element_type=F32)]
    unnamed x1 -> x0, blocking collectives: 37.6 us -> none
    unnamed x84 -> x87, local copies, waits for them, and re-layouts: 11.3 us -> 34.2 us
    all_to_all x4 -> x3, waiting for transfers between devices: 29.2 us -> 12.8 us  [the longest x2 12.8 us: scattered(): lax.all_to_all(summed.astype(BF), 'pos', split_axis=0, concat_axis=0, til...]
    convert_element_type x15 -> x10, other arithmetic: 29.1 us -> 13.1 us  [the longest x1 8.48 us: local(): grads.transpose(1, 2, 4, 0, 3).reshape(2, lp, dslice, ff).astype(F32)]
  transfers between devices with their start and end apart: 19 -> 10, of which waited for: 15 -> 5; matrix products, arithmetic and copies ran while one was open for 16% -> 17% of each run, Pallas kernels for 0% -> 0%
where the time goes in v1:
time: 616 us; the launch traced here: 606 us
  waiting for transfers between devices  259 us (42%)
  blocking collectives  125 us (20%)
  local copies, waits for them, and re-layouts  95.5 us (16%)
  matrix products  69.4 us (11%)
  other arithmetic  28 us (5%)
  between operations  15.2 us (2%)
  starting transfers between devices  14.6 us (2%)
    reduce_scatter x1, waiting for transfers between devices, local(): total = lax.psum_scatter(total, 'frames', scatter_dimension=0, tiled=True)  102 us
    reduce_scatter x2, waiting for transfers between devices, scattered(): summed = lax.psum_scatter(moved, 'frames', scatter_dimension=0, tiled=False)  90.5 us
    all_to_all x1, blocking collectives, local(): lax.all_to_all(pair, 'frames', split_axis=0, concat_axis=0, tiled=True)  80.5 us
    all_gather x1, waiting for transfers between devices, local(): w_all = lax.all_gather(both, ('frames', 'pos'), axis=0, tiled=True)  53.6 us
    all_to_all x2, blocking collectives, to_pos(): return lax.all_to_all(moved, 'pos', split_axis=0, concat_axis=0, tiled=True)  44.1 us
    unnamed x87, local copies, waits for them, and re-layouts  34.2 us
    concatenate x1, local copies, waits for them, and re-layouts, local(): jnp.concatenate((qkv_weight_grad.astype(BF), out_weight_grad.astype(BF),...  13.3 us
    all_to_all x2, waiting for transfers between devices, scattered(): lax.all_to_all(summed.astype(BF), 'pos', split_axis=0, concat_axis=0, til...  12.8 us
  transfers between devices with their start and end apart: 10, of which 5 were waited for; matrix products, arithmetic and copies ran while one was open for 17% of the time, Pallas kernels for 0%

profile of v1, /device:TPU:0, one launch (start us, length us, event | category | flops | bytes accessed | tf_op | source)
XLA Modules:
  0.0 606.4 jit_solution(439109005350942202)
XLA Ops:
  12.8 26.2 %all_to_all.30 = bf16[4,4,16,1024]{3,1,2,0:T(4,128)(2,1)S(1)} all-to-all(bf16[4,4,16,1024]{3,1,2,0:T(4,128)(2,1)S(1)} %copy.138), channel_id=1, replica_groups=mesh['frames'=8,'pos'=4] {'pos'}, dimensions={0} | all-to-all | bytes 1048576 | tf_op jit(solution)/shard_map/all_to_all | solution.py:66
  40.9 53.6 %all-gather.6.cloned.1.call-done = bf16[1024,4096]{1,0:T(8,128)(2,1)} async-done(((bf16[32,4096]{1,0:T(8,128)(2,1)}), bf16[1024,4096]{1,0:T(8,128)(2,1)}) %all-gather.6.cloned.1.call-update) | async-done | bytes 8388624 | tf_op jit(solution)/shard_map/all_gather | solution.py:79
  94.5 5.8 fusion.1
  112.8 17.9 %all_to_all.31 = bf16[4,4,16,1024]{3,1,2,0:T(4,128)(2,1)S(1)} all-to-all(bf16[4,4,16,1024]{3,1,2,0:T(4,128)(2,1)S(1)} %copy.130), channel_id=1, replica_groups=mesh['frames'=8,'pos'=4] {'pos'}, dimensions={0} | all-to-all | bytes 1048576 | tf_op jit(solution)/shard_map/all_to_all | solution.py:66
  135.7 5.2 copy.126
  144.0 80.5 %all_to_all.32 = bf16[8,2,4,352,128]{4,3,2,1,0:T(8,128)(2,1)S(1)} all-to-all(bf16[8,2,4,352,128]{4,3,2,1,0:T(8,128)(2,1)S(1)} %copy.128), channel_id=1, replica_groups=mesh['frames'=8,'pos'=4] {'frames'}, dimensions={0} | all-to-all | bytes 11534336 | tf_op jit(solution)/shard_map/all_to_all | solution.py:83
  226.7 5.0 copy.140
  241.4 7.4 %fusion.12 = (bf16[4,352,512]{2,1,0:T(8,128)(2,1)S(1)}, bf16[4,352,512]{2,1,0:T(8,128)(2,1)S(1)}, bf16[4,352,512]{2,1,0:T(8,128)(2,1)}) fusion(f32[4,352,512]{2,1,0:T(8,128)} %fusion.7, f32[4,352,512]{2,1,0:T(8,128)} %fusion.3, bf16[4,512,1024]{2,1,0:T(8,128)(2,1)S(1)} %bitcast.201, f32[4,352,1024]{2,1,0:T(8,128)} %param.18), kind=kOutput, calls=%fused_computation.26 | convolution fusion | flops 1488650240 | bytes 20054016 | tf_op jit(solution)/shard_map/prd,phd->phr/dot_general | solution.py:102
  257.5 5.0 convolution_convert_fusion
  265.1 41.9 %reduce-scatter.7.cloned.1.call-done = bf16[1,4,4,16,1024]{4,3,2,1,0:T(8,128)(2,1)} async-done(((bf16[8,4,4,16,1024]{4,3,2,1,0:T(8,128)(2,1)}), bf16[1,4,4,16,1024]{4,3,2,1,0:T(8,128)(2,1)}) %reduce-scatter.7.cloned.1.call-update) | async-done | bytes 524304 | tf_op jit(solution)/shard_map/reduce_scatter | solution.py:74
  309.3 4.7 all-to-all-start.4
  314.0 48.5 %reduce-scatter.5.cloned.1.call-done = bf16[1,4,4,16,1024]{4,3,2,1,0:T(8,128)(2,1)} async-done(((bf16[8,4,4,16,1024]{4,3,2,1,0:T(8,128)(2,1)}), bf16[1,4,4,16,1024]{4,3,2,1,0:T(8,128)(2,1)}) %reduce-scatter.5.cloned.1.call-update) | async-done | bytes 524304 | tf_op jit(solution)/shard_map/reduce_scatter | solution.py:74
  364.8 4.6 all-to-all-start.2
  371.1 12.8 %all-to-all-done.2 = bf16[4,4,16,1024]{3,1,2,0:T(4,128)(2,1)S(1)} async-done(((bf16[4,4,16,1024]{3,1,2,0:T(4,128)(2,1)}), bf16[4,4,16,1024]{3,1,2,0:T(4,128)(2,1)S(1)}, u32[]{:S(2)}, u32[]{:S(2)}) %all-to-all-start.2) | async-done | bytes 524320 | tf_op jit(solution)/shard_map/all_to_all | solution.py:75
  407.1 6.3 %bitcast_convert_fusion = bf16[1024,3072]{1,0:T(8,128)(2,1)} fusion(bf16[16,16,3072]{2,1,0:T(8,128)(2,1)} %convert_element_type.146, bf16[16,16,1024]{2,1,0:T(8,128)(2,1)} %param.10, f32[1024]{0:T(1024)S(1)} %copy-done.38, f32[16,16]{1,0:T(8,128)S(1)} %copy-done.34), kind=kOutput, calls=%fused_computation | convolution fusion | flops 1614807040 | bytes 8393728 | tf_op jit(solution)/shard_map/fpd,fpe->de/dot_general | solution.py:131
  413.4 5.9 fusion.44
  419.8 13.3 %concatenate.8 = bf16[1024,4224]{1,0:T(8,128)(2,1)} concatenate(bf16[1024,3072]{1,0:T(8,128)(2,1)} %bitcast_convert_fusion, bf16[1024,1024]{1,0:T(8,128)(2,1)S(1)} %copy-done.14, bf16[1024,2]{1,0:T(8,128)(2,1)S(1)} %copy.149, bf16[1024,2]{1,0:T(8,128)(2,1)S(1)} %copy.150, bf16[1024,124]{1,0:T(8,128)(2,1)S(1)} %broadcast_in_dim.57), dimensions={1} | concatenate | bytes 17301504 | tf_op jit(solution)/shard_map/concatenate | solution.py:140
  448.9 4.8 all-to-all-start.5
  453.8 102.0 %reduce-scatter.9.cloned.1.call-done = bf16[128,4224]{1,0:T(8,128)(2,1)} async-done(((bf16[1024,4224]{1,0:T(8,128)(2,1)}), bf16[128,4224]{1,0:T(8,128)(2,1)}) %reduce-scatter.9.cloned.1.call-update) | async-done | bytes 1081360 | tf_op jit(solution)/shard_map/reduce_scatter | solution.py:143
  555.8 6.4 %fusion.65 = f32[4,352,1024]{2,1,0:T(8,128)} fusion(bf16[4,352,512]{2,1,0:T(8,128)(2,1)S(1)} %copy-done.11, bf16[4,512,1024]{2,1,0:T(8,128)(2,1)} %bitcast.200), kind=kOutput, calls=%fused_computation.116 | convolution fusion | flops 1476395008 | bytes 11403264 | tf_op jit(solution)/shard_map/phr,prd->phd/dot_general | solution.py:117
  562.2 8.5 %convert_bitcast_fusion = f32[2,4,128,8,352]{2,4,3,1,0:T(8,128)} fusion(bf16[8,2,4,352,128]{4,3,2,1,0:T(8,128)(2,1)} %all-to-all-done.5), kind=kLoop, calls=%fused_computation.1 | loop fusion | flops 2883584 | bytes 17301504 | tf_op jit(solution)/shard_map/convert_element_type | solution.py:123
  570.7 9.6 %fusion.63 = (f32[1,4,128,8,352]{2,4,3,1,0:T(8,128)}, f32[1,4,128,8,352]{2,4,3,1,0:T(8,128)}) fusion(f32[2,4,128,8,352]{2,4,3,1,0:T(8,128)} %convert_bitcast_fusion), kind=kLoop, calls=%fused_computation.114 | loop fusion | bytes 23068672 | tf_op jit(solution)/shard_map/slice | solution.py:154
  580.3 6.2 %copy.154 = f32[4,128,2816]{2,1,0:T(8,128)} copy(f32[4,128,2816]{1,2,0:T(8,128)} %bitcast.195) | data formatting | bytes 11534336
  586.5 6.4 %copy.155 = f32[4,128,2816]{2,1,0:T(8,128)} copy(f32[4,128,2816]{1,2,0:T(8,128)} %bitcast.194) | data formatting | bytes 11534336
  (174 shorter events, 102.5 us)
Async XLA Ops:
  7.2 87.3 %all-gather.6.cloned.1.call-start = ((), (), s32[]{:S(2)}) async-start(), calls=%async_computation.10 | async-start | bytes 8650752 | tf_op jit(solution)/shard_map/all_gather | solution.py:79
  9.9 216.8 %all-gather.10.cloned.1.call-start = ((), (), s32[]{:S(2)}) async-start(), calls=%async_computation.16 | async-start | bytes 4718592 | tf_op jit(solution)/shard_map/all_gather | solution.py:69
  11.1 28.9 %copy-start.17 = (bf16[16,16,1024]{2,1,0:T(8,128)(2,1)S(1)}, bf16[16,16,1024]{2,1,0:T(8,128)(2,1)}, u32[]{:S(2)}) copy-start(bf16[16,16,1024]{2,1,0:T(8,128)(2,1)} %param.10) | copy-start | bytes 1572868
  12.4 82.1 %copy-start.37 = (f32[1024]{0:T(1024)S(1)}, f32[1024]{0:T(1024)}, u32[]{:S(2)}) copy-start(f32[1024]{0:T(1024)} %param.12) | copy-start | bytes 12292
  40.0 191.7 %all-gather.8.cloned.1.call-start = ((), (), s32[]{:S(2)}) async-start(), calls=%async_computation.15 | async-start | bytes 4718592 | tf_op jit(solution)/shard_map/all_gather | solution.py:69
  40.1 66.6 %copy-start.35 = (pred[16,16]{0,1:T(8,128)(4,1)}, pred[16,16]{0,1:T(8,128)(4,1)S(1)}, u32[]{:S(2)}) copy-start(pred[16,16]{0,1:T(8,128)(4,1)S(1)} %iota_compare_fusion) | copy-start | bytes 772
  40.8 53.7 %copy-start.33 = (f32[16,16]{1,0:T(8,128)}, f32[16,16]{1,0:T(8,128)S(1)}, u32[]{:S(2)}) copy-start(f32[16,16]{1,0:T(8,128)S(1)} %fusion.59) | copy-start | bytes 3076
  131.6 175.4 %reduce-scatter.7.cloned.1.call-start = ((), (), s32[]{:S(2)}) async-start(), calls=%async_computation.12 | async-start | bytes 4718592 | tf_op jit(solution)/shard_map/reduce_scatter | solution.py:74
  256.2 106.3 %reduce-scatter.5.cloned.1.call-start = ((), (), s32[]{:S(2)}) async-start(), calls=%async_computation.11 | async-start | bytes 4718592 | tf_op jit(solution)/shard_map/reduce_scatter | solution.py:74
  309.3 60.4 %copy-start.5 = (f32[16,16,1024]{2,1,0:T(8,128)S(1)}, f32[16,16,1024]{2,1,0:T(8,128)}, u32[]{:S(2)}) copy-start(f32[16,16,1024]{2,1,0:T(8,128)} %copy-done.4) | copy-start | bytes 3145732
  309.3 55.5 %all-to-all-start.4 = ((bf16[4,4,16,1024]{3,1,2,0:T(4,128)(2,1)}), bf16[4,4,16,1024]{3,1,2,0:T(4,128)(2,1)S(1)}, u32[]{:S(2)}, u32[]{:S(2)}) async-start(bf16[4,4,16,1024]{3,1,2,0:T(4,128)(2,1)} %copy.142), calls=%async_computation.6 | async-start | bytes 1048576 | tf_op jit(solution)/shard_map/all_to_all | solution.py:75
  364.8 19.1 %all-to-all-start.2 = ((bf16[4,4,16,1024]{3,1,2,0:T(4,128)(2,1)}), bf16[4,4,16,1024]{3,1,2,0:T(4,128)(2,1)S(1)}, u32[]{:S(2)}, u32[]{:S(2)}) async-start(bf16[4,4,16,1024]{3,1,2,0:T(4,128)(2,1)} %copy.135), calls=%async_computation.3 | async-start | bytes 1048576 | tf_op jit(solution)/shard_map/all_to_all | solution.py:75
  369.4 186.4 %reduce-scatter.9.cloned.1.call-start = ((), (), s32[]{:S(2)}) async-start(), calls=%async_computation.13 | async-start | bytes 9732096 | tf_op jit(solution)/shard_map/reduce_scatter | solution.py:143
  387.6 12.3 %copy-start.12 = (f32[16,16,1024]{2,1,0:T(8,128)}, f32[16,16,1024]{2,1,0:T(8,128)S(1)}, u32[]{:S(2)}) copy-start(f32[16,16,1024]{2,1,0:T(8,128)S(1)} %get-tuple-element.61) | copy-start | bytes 3145732
  387.6 6.2 %copy-start.36 = (pred[16,16]{0,1:T(8,128)(4,1)S(1)}, pred[16,16]{0,1:T(8,128)(4,1)}, u32[]{:S(2)}) copy-start(pred[16,16]{0,1:T(8,128)(4,1)} %copy-done.35) | copy-start | bytes 772
  407.0 6.4 %copy-start.19 = (bf16[16,16,1024]{2,1,0:T(8,128)(2,1)S(1)}, bf16[16,16,1024]{2,1,0:T(8,128)(2,1)}, u32[]{:S(2)}) copy-start(bf16[16,16,1024]{2,1,0:T(8,128)(2,1)} %param.10) | copy-start | bytes 1572868
  407.0 6.4 %copy-start.20 = (bf16[16,16,3072]{2,1,0:T(8,128)(2,1)S(1)}, bf16[16,16,3072]{2,1,0:T(8,128)(2,1)}, u32[]{:S(2)}) copy-start(bf16[16,16,3072]{2,1,0:T(8,128)(2,1)} %convert_element_type.146) | copy-start | bytes 4718596
  413.4 6.4 %copy-start.14 = (bf16[1024,1024]{1,0:T(8,128)(2,1)S(1)}, bf16[1024,1024]{1,0:T(8,128)(2,1)}, u32[]{:S(2)}) copy-start(bf16[1024,1024]{1,0:T(8,128)(2,1)} %bitcast_convert_fusion.1) | copy-start | bytes 6291460
  448.9 107.0 %copy-start.11 = (bf16[4,352,512]{2,1,0:T(8,128)(2,1)S(1)}, bf16[4,352,512]{2,1,0:T(8,128)(2,1)}, u32[]{:S(2)}) copy-start(bf16[4,352,512]{2,1,0:T(8,128)(2,1)} %get-tuple-element.55) | copy-start | bytes 4325380
  448.9 113.3 %all-to-all-start.5 = ((bf16[8,2,4,352,128]{4,3,2,1,0:T(8,128)(2,1)}), bf16[8,2,4,352,128]{4,3,2,1,0:T(8,128)(2,1)}, u32[]{:S(2)}, u32[]{:S(2)}) async-start(bf16[8,2,4,352,128]{4,3,2,1,0:T(8,128)(2,1)} %maximum_bitcast_fusion), calls=%async_computation.9 | async-start | bytes 11534336 | tf_op jit(solution)/shard_map/all_to_all | solution.py:120
  453.7 140.5 %reduce-scatter.11.cloned.1.call-start = ((), (), s32[]{:S(2)}) async-start(), calls=%async_computation.14 | async-start | bytes 1351680 | tf_op jit(solution)/shard_map/reduce_scatter | solution.py:144
  586.5 6.4 %copy-start.31 = (f32[16,16]{1,0:T(8,128)S(1)}, f32[16,16]{1,0:T(8,128)}, u32[]{:S(2)}) copy-start(f32[16,16]{1,0:T(8,128)} %copy-done.30) | copy-start | bytes 3076
  586.5 6.4 %copy-start.13 = (f32[16,16,1024]{2,1,0:T(8,128)S(1)}, f32[16,16,1024]{2,1,0:T(8,128)}, u32[]{:S(2)}) copy-start(f32[16,16,1024]{2,1,0:T(8,128)} %copy-done.12) | copy-start | bytes 3145732
  586.5 6.4 %copy-start.27 = (f32[16,16,1024]{2,1,0:T(8,128)S(1)}, f32[16,16,1024]{2,1,0:T(8,128)}, u32[]{:S(2)}) copy-start(f32[16,16,1024]{2,1,0:T(8,128)} %get-tuple-element.69) | copy-start | bytes 3145732
  (26 other events, 60.8 us)
Sparse Core Ops, SparseCore 0:
  11.5 82.9 all-gather.5
  97.0 35.2 all-gather.9
  134.8 66.1 all-gather.7
  256.3 50.6 reduce-scatter.6
  311.2 51.3 reduce-scatter.4
  433.3 122.4 reduce-scatter.8
  558.2 25.9 reduce-scatter.10

commit v2 on v1

--- a/solution.py
+++ b/solution.py
@@ -1,14 +1,331 @@
+import functools
 import math
 
 import jax
 import jax.numpy as jnp
 from jax import lax
+from jax.experimental import pallas as pl
+from jax.experimental.pallas import tpu as pltpu
 from jax.sharding import PartitionSpec as P
 
 H = 16
 HD = 64
 BF = jnp.bfloat16
 F32 = jnp.float32
+MESH = pl.DeviceIdType.MESH
+ANY = pl.BlockSpec(memory_space=pl.ANY)
+VM = pl.BlockSpec(memory_space=pltpu.VMEM)
+
+
+def place():
+    return lax.axis_index("frames"), lax.axis_index("pos")
+
+
+def flip(index, mask):
+    bit = 1
+    while bit <= mask:
+        if mask & bit:
+            index = index + bit * (1 - 2 * ((index // bit) % 2))
+        bit *= 2
+    return index
+
+
+def greet(nf, nz, every_frame):
+    f, z = place()
+    hops = [1] + [2 * m for m in range(1, nf // 2)]
+    if every_frame:
+        hops = list(range(1, nf))
+    others = [(flip(f, h), z) for h in hops] + [(f, flip(z, k)) for k in range(1, nz)]
+    barrier = pltpu.get_barrier_semaphore()
+    for other in others:
+        pl.semaphore_signal(barrier, inc=1, device_id=other, device_id_type=MESH)
+    pl.semaphore_wait(barrier, len(others))
+
+
+def remote(src, dst, send, recv, to):
+    copy = pltpu.make_async_remote_copy(
+        src_ref=src, dst_ref=dst, send_sem=send, recv_sem=recv, device_id=to, device_id_type=MESH
+    )
+    copy.start()
+    return copy
+
+
+def relay_of(k):
+    return 1 if k % 2 == 0 else 2
+
+
+class Gather:
+    def __init__(self, nf, nz, src_for, out, sems):
+        self.nf, self.nz, self.nc = nf, nz, nf // 2
+        self.f, self.z = place()
+        self.src_for, self.out, self.sems = src_for, out, sems
+        self.sent = []
+        self.tree = self.nc == 4
+
+    @staticmethod
+    def sem_shape(nf, nz):
+        return (2, 1 + 2 * (nf // 2), nz)
+
+    def push(self, src, dst, hop, k, to):
+        self.sent.append(remote(src, dst, self.sems.at[0, hop, k], self.sems.at[1, hop, k], to))
+
+    def arrive(self, dst, hop, k):
+        pltpu.make_async_remote_copy(
+            src_ref=dst,
+            dst_ref=dst,
+            send_sem=self.sems.at[0, hop, k],
+            recv_sem=self.sems.at[1, hop, k],
+            device_id=(flip(self.f, 1), self.z),
+            device_id_type=MESH,
+        ).wait_recv()
+
+    def begin(self):
+        f, z = self.f, self.z
+        for k in range(1, self.nz):
+            self.push(self.src_for(flip(z, k)), self.out.at[f, z], 0, k, (f, flip(z, k)))
+        self.own = pltpu.make_async_copy(self.src_for(z), self.out.at[f, z], self.sems.at[0, 0, 0])
+        self.own.start()
+        self.spread(self.src_for(z), 0)
+
+    def spread(self, src, k):
+        f, z = self.f, self.z
+        block = self.out.at[f, flip(z, k)]
+        for m in range(1, self.nc):
+            if self.tree and m == 3:
+                continue
+            self.push(src, block, m, k, (flip(f, 2 * m), z))
+        self.push(src, block, self.nc, k, (flip(f, 1), z))
+
+    def along(self, k):
+        block = self.out.at[self.f, flip(self.z, k)]
+        self.arrive(block, 0, k)
+        self.spread(block, k)
+
+    def over(self, m, k):
+        f, z = self.f, self.z
+        block = self.out.at[flip(f, 2 * m), flip(z, k)]
+        self.arrive(block, m, k)
+        if self.tree and m == relay_of(k):
+            self.push(block, block, 3, k, (flip(f, 2 * (3 - m)), z))
+        self.push(block, block, self.nc + m, k, (flip(f, 1), z))
+
+    def order(self, k):
+        first = relay_of(k) if self.tree else 1
+        return [first] + [m for m in range(1, self.nc) if m != first]
+
+    def finish(self):
+        f, z = self.f, self.z
+        for k in range(self.nz):
+            for m in range(self.nc):
+                self.arrive(self.out.at[flip(f, 2 * m + 1), flip(z, k)], self.nc + m, k)
+        self.own.wait()
+        for copy in self.sent:
+            copy.wait_send()
+
+
+class Swap:
+    def __init__(self, nf, src, out, sems):
+        self.nf, self.src, self.out, self.sems = nf, src, out, sems
+        self.f, self.z = place()
+        self.sent = []
+
+    @staticmethod
+    def sem_shape(nf):
+        return (2, nf)
+
+    def start(self):
+        f, z = self.f, self.z
+        self.own = pltpu.make_async_copy(self.src.at[f], self.out.at[f], self.sems.at[0, 0])
+        self.own.start()
+        for m in range(self.nf - 1, 0, -1):
+            self.sent.append(
+                remote(
+                    self.src.at[flip(f, m)],
+                    self.out.at[f],
+                    self.sems.at[0, m],
+                    self.sems.at[1, m],
+                    (flip(f, m), z),
+                )
+            )
+
+    def finish(self):
+        self.own.wait()
+        for copy in self.sent:
+            copy.wait()
+
+
+class Scatter:
+    def __init__(self, nf, nz, src, sib, tx, rx, ty, land, sems):
+        self.nf, self.nz, self.nc = nf, nz, nf // 2
+        self.f, self.z = place()
+        self.src, self.sib, self.tx, self.rx, self.ty = src, sib, tx, rx, ty
+        self.land, self.sems = land, sems
+        self.sent = []
+
+    @staticmethod
+    def scratch(nf, nz, rows, columns):
+        nc = nf // 2
+        block = (rows, columns)
+        return [
+            pltpu.VMEM((nz, nc) + block, BF),
+            pltpu.VMEM((nz, nc) + block, BF),
+            pltpu.VMEM((nz, nc) + block, BF),
+            pltpu.VMEM((nz,) + block, BF),
+            pltpu.VMEM((nz,) + block, BF),
+            pltpu.SemaphoreType.DMA((2, 1 + 2 * nc, nz)),
+        ]
+
+    def push(self, src, dst, hop, k, to):
+        copy = remote(src, dst, self.sems.at[0, hop, k], self.sems.at[1, hop, k], to)
+        self.sent.append(copy)
+
+    def arrive(self, dst, hop, k):
+        pltpu.make_async_remote_copy(
+            src_ref=dst,
+            dst_ref=dst,
+            send_sem=self.sems.at[0, hop, k],
+            recv_sem=self.sems.at[1, hop, k],
+            device_id=(flip(self.f, 1), self.z),
+            device_id_type=MESH,
+        ).wait_recv()
+
+    def pairs(self, k):
+        f, z = self.f, self.z
+        for m in list(range(self.nc - 1, 0, -1)) + [0]:
+            self.push(
+                self.src.at[flip(f, 2 * m + 1), flip(z, k)],
+                self.sib.at[k, m],
+                self.nc + m,
+                k,
+                (flip(f, 1), z),
+            )
+
+    def chips(self, k):
+        f, z = self.f, self.z
+        for m in list(range(self.nc - 1, 0, -1)):
+            self.arrive(self.sib.at[k, m], self.nc + m, k)
+            add_into(self.tx.at[k, m], self.src.at[flip(f, 2 * m), flip(z, k)], self.sib.at[k, m])
+            self.push(self.tx.at[k, m], self.rx.at[k, m], m, k, (flip(f, 2 * m), z))
+
+    def home(self, k, out=None):
+        f, z = self.f, self.z
+        self.arrive(self.sib.at[k, 0], self.nc, k)
+        for m in range(1, self.nc):
+            self.arrive(self.rx.at[k, m], m, k)
+        terms = [self.src.at[f, flip(z, k)], self.sib.at[k, 0]]
+        terms += [self.rx.at[k, m] for m in range(1, self.nc)]
+        if k == 0:
+            add_into(out, *terms)
+            return
+        add_into(self.ty.at[k], *terms)
+        self.push(self.ty.at[k], self.land.at[k], 0, k, (f, flip(z, k)))
+
+    def landed(self, k):
+        self.arrive(self.land.at[k], 0, k)
+
+    def finish(self):
+        for copy in self.sent:
+            copy.wait_send()
+
+
+def add_into(out, *terms):
+    rows = out.shape[0]
+    step = 16 if rows % 16 == 0 else rows
+
+    def body(i, carry):
+        at = pl.ds(pl.multiple_of(i * step, step), step)
+        total = terms[0][at, :].astype(F32)
+        for term in terms[1:]:
+            total = total + term[at, :].astype(F32)
+        out[at, :] = total.astype(out.dtype)
+        return carry
+
+    lax.fori_loop(0, rows // step, body, 0)
+
+
+def call(kernel, ident, **kw):
+    return pl.pallas_call(
+        kernel,
+        compiler_params=pltpu.CompilerParams(
+            collective_id=ident, has_side_effects=True, vmem_limit_bytes=56 * 2**20
+        ),
+        **kw,
+    )
+
+
+def run_gathers(gathers, nz):
+    for k in range(nz):
+        for g in gathers:
+            if k > 0:
+                g.along(k)
+        for g in gathers:
+            if g.tree and k > 0:
+                g.over(relay_of(k - 1), k - 1)
+    for g in gathers:
+        if g.tree:
+            g.over(relay_of(nz - 1), nz - 1)
+    for k in range(nz):
+        for g in gathers:
+            for m in range(1, g.nc):
+                if g.tree and m == relay_of(k):
+                    continue
+                g.over(m, k)
+
+
+def first_kernel(nf, nz, attn, gy, pair, attn_all, gy_all, pair_all, s1, s2, s3):
+    greet(nf, nz, True)
+    weights = Gather(nf, nz, lambda zz: attn, attn_all, s1)
+    rows = Gather(nf, nz, lambda zz: gy.at[zz], gy_all, s2)
+    swap = Swap(nf, pair, pair_all, s3)
+    weights.begin()
+    rows.begin()
+    swap.start()
+    run_gathers([weights, rows], nz)
+    weights.finish()
+    rows.finish()
+    swap.finish()
+
+
+def rows_kernel(nf, nz, b, b_all, s1):
+    greet(nf, nz, False)
+    rows = Gather(nf, nz, lambda zz: b.at[zz], b_all, s1)
+    rows.begin()
+    run_gathers([rows], nz)
+    rows.finish()
+
+
+def back_kernel(nf, nz, terms, out, sib, tx, rx, ty, land, sems):
+    greet(nf, nz, False)
+    s = Scatter(nf, nz, terms, sib, tx, rx, ty, land, sems)
+    z = s.z
+    for k in range(nz - 1, -1, -1):
+        s.pairs(k)
+    for k in range(nz - 1, -1, -1):
+        s.chips(k)
+    for k in range(nz - 1, -1, -1):
+        s.home(k, out.at[z])
+    for k in range(1, nz):
+        s.landed(k)
+        out[flip(z, k)] = land[k]
+    s.finish()
+
+
+def last_kernel(nf, nz, terms, pair, out, pair_all, sib, tx, rx, ty, land, sems, s2):
+    greet(nf, nz, True)
+    s = Scatter(nf, nz, terms, sib, tx, rx, ty, land, sems)
+    swap = Swap(nf, pair, pair_all, s2)
+    for k in range(nz - 1, -1, -1):
+        s.pairs(k)
+    swap.start()
+    for k in range(nz - 1, -1, -1):
+        s.chips(k)
+    for k in range(nz - 1, -1, -1):
+        s.home(k, out)
+    for k in range(1, nz):
+        s.landed(k)
+        add_into(out, out, land.at[k])
+    s.finish()
+    swap.finish()
 
 
 def rms_norm(values, gain_vector):
@@ -62,30 +379,53 @@
         return w.transpose(1, 2, 0, 3).reshape(lp, ffs, d)
 
     def to_pos(rows):
-        moved = rows.transpose(1, 0, 2).reshape(nz, lp, fr, d)
-        return lax.all_to_all(moved, "pos", split_axis=0, concat_axis=0, tiled=True)
-
-    def gathered(rows):
-        every = lax.all_gather(rows, "frames", axis=0, tiled=False)
+        return rows.transpose(1, 0, 2).reshape(nz, lp * fr, d)
+
+    def gathered(every):
+        every = every.reshape(nf, nz, lp, fr, d)
         return every.transpose(2, 0, 1, 3, 4).reshape(lp, nf * nz * fr, d)
 
-    def scattered(rows):
+    rows_shape = jax.ShapeDtypeStruct((nf, nz, lp * fr, d), BF)
+    back_shape = jax.ShapeDtypeStruct((nz, lp * fr, d), BF)
+    gather_sems = pltpu.SemaphoreType.DMA(Gather.sem_shape(nf, nz))
+    swap_sems = pltpu.SemaphoreType.DMA(Swap.sem_shape(nf))
+
+    def scattered(rows, ident):
         moved = rows.reshape(lp, nf, nz, fr, d).transpose(1, 2, 0, 3, 4)
-        summed = lax.psum_scatter(moved, "frames", scatter_dimension=0, tiled=False)
-        back = lax.all_to_all(summed.astype(BF), "pos", split_axis=0, concat_axis=0, tiled=True)
+        moved = moved.reshape(nf, nz, lp * fr, d)
+        back = call(
+            functools.partial(back_kernel, nf, nz),
+            ident,
+            out_shape=back_shape,
+            in_specs=[VM],
+            out_specs=VM,
+            scratch_shapes=Scatter.scratch(nf, nz, lp * fr, d),
+        )(moved)
         return back.reshape(npos, fr, d).transpose(1, 0, 2)
 
     both = jnp.concatenate((qkv_master.astype(BF), out_master.astype(BF)), axis=1)
-    w_all = lax.all_gather(both, ("frames", "pos"), axis=0, tiled=True)
+    pair = jnp.stack((turned(gate_master), turned(up_master)), axis=1)
+    upstream = keep_rows * out_cotangent.astype(F32)
+    own_rows = both.shape[0]
+    w_all, gy_all, pair = call(
+        functools.partial(first_kernel, nf, nz),
+        0,
+        out_shape=(
+            jax.ShapeDtypeStruct((nf, nz) + both.shape, BF),
+            rows_shape,
+            jax.ShapeDtypeStruct(pair.shape, BF),
+        ),
+        in_specs=[ANY] * 3,
+        out_specs=(ANY,) * 3,
+        scratch_shapes=[gather_sems, gather_sems, swap_sems],
+    )(both, to_pos(upstream.astype(BF)), pair)
+    w_all = w_all.reshape(d, both.shape[1])
     w_qkv = w_all[:, : 3 * d]
     w_out = w_all[:, 3 * d :]
-    pair = jnp.stack((turned(gate_master), turned(up_master)), axis=1)
-    pair = lax.all_to_all(pair, "frames", split_axis=0, concat_axis=0, tiled=True)
     gate_t = untwist(pair[:, 0])
     up_t = untwist(pair[:, 1])
     down = down_master.astype(BF)
-    upstream = keep_rows * out_cotangent.astype(F32)
-    gy = gathered(to_pos(upstream.astype(BF)))
+    gy = gathered(gy_all)
 
     normed_one, norm_one_pull = jax.vjp(rms_norm, inputs, gain_attention)
     normed_low = normed_one.astype(BF)
@@ -95,7 +435,15 @@
     branch = jnp.einsum("fpd,de->fpe", mixed_low, w_out, preferred_element_type=F32)
     middle = inputs + branch
     normed_two, norm_two_pull = jax.vjp(rms_norm, middle, gain_feed)
-    b = gathered(to_pos(normed_two.astype(BF)))
+    b_all = call(
+        functools.partial(rows_kernel, nf, nz),
+        1,
+        out_shape=rows_shape,
+        in_specs=[ANY],
+        out_specs=ANY,
+        scratch_shapes=[gather_sems],
+    )(to_pos(normed_two.astype(BF)))
+    b = gathered(b_all)
 
     gate_rows = jnp.einsum("prd,phd->phr", b, gate_t, preferred_element_type=F32)
     up_rows = jnp.einsum("prd,phd->phr", b, up_t, preferred_element_type=F32)
@@ -108,19 +456,16 @@
     db = jnp.einsum("phr,phd->prd", gate_back, gate_t, preferred_element_type=F32) + jnp.einsum(
         "phr,phd->prd", up_back, up_t, preferred_element_type=F32
     )
-    back_rows = scattered(db.astype(BF)).astype(F32)
+    back_rows = scattered(db.astype(BF), 2).astype(F32)
     feed = jnp.einsum("phr,phd->prd", hidden, down, preferred_element_type=F32)
-    returned = scattered(feed.astype(BF)).astype(F32)
+    returned = scattered(feed.astype(BF), 3).astype(F32)
     block_out = (keep_rows * (middle + returned)).astype(BF)
     gate_grad = jnp.einsum("phr,prd->phd", gate_back, b, preferred_element_type=F32).astype(BF)
     up_grad = jnp.einsum("phr,prd->phd", up_back, b, preferred_element_type=F32).astype(BF)
     down_grad = jnp.einsum("phr,prd->phd", hidden, gy, preferred_element_type=F32)
 
     grads = jnp.stack((gate_grad, up_grad), axis=0).reshape(2, lp, ffs, nf, dslice)
-    grads = lax.all_to_all(
-        grads.transpose(3, 0, 1, 2, 4), "frames", split_axis=0, concat_axis=0, tiled=True
-    )
-    grads = grads.transpose(1, 2, 4, 0, 3).reshape(2, lp, dslice, ff).astype(F32)
+    grads = grads.transpose(3, 0, 1, 2, 4)
 
     pulled_two = norm_two_pull(back_rows)
     middle_grad = upstream + pulled_two[0]
@@ -140,8 +485,19 @@
     total = jnp.concatenate(
         (qkv_weight_grad.astype(BF), out_weight_grad.astype(BF), tail), axis=1
     )
-    total = lax.psum_scatter(total, "frames", scatter_dimension=0, tiled=True)
-    total = lax.psum_scatter(total, "pos", scatter_dimension=0, tiled=True).astype(F32)
+    total = total.reshape(nf, nz, own_rows, total.shape[1])
+    total, grads = call(
+        functools.partial(last_kernel, nf, nz),
+        4,
+        out_shape=(
+            jax.ShapeDtypeStruct(total.shape[2:], F32),
+            jax.ShapeDtypeStruct(grads.shape, BF),
+        ),
+        in_specs=[VM, ANY],
+        out_specs=(VM, ANY),
+        scratch_shapes=Scatter.scratch(nf, nz, *total.shape[2:]) + [swap_sems],
+    )(total, grads)
+    grads = grads.transpose(1, 2, 4, 0, 3).reshape(2, lp, dslice, ff).astype(F32)
     gain_grads = total[:, 4 * d : 4 * d + 2] + total[:, 4 * d + 2 : 4 * d + 4]
     return (
         block_out,

time: 616 us -> 533 us (0.87)
  Pallas kernels: 0 us -> 335 us
  waiting for transfers between devices: 259 us -> 0 us
  blocking collectives: 125 us -> 0 us
  starting transfers between devices: 14.6 us -> 0 us
  between operations: 15.2 us -> 1.73 us
    pallas_call x0 -> x5, Pallas kernels: none -> 335 us  [the longest x1 124 us: local(): call(functools.partial(first_kernel, nf, nz), 0, out_shape=(jax.ShapeDtyp...]
    reduce_scatter x4 -> x0, waiting for transfers between devices: 192 us -> none  [the longest x1 102 us: local(): total = lax.psum_scatter(total, 'frames', scatter_dimension=0, tiled=True)]
    all_to_all x3 -> x0, blocking collectives: 125 us -> none  [the longest x1 80.5 us: local(): lax.all_to_all(pair, 'frames', split_axis=0, concat_axis=0, tiled=True)]
    all_gather x3 -> x0, waiting for transfers between devices: 53.7 us -> none  [the longest x1 53.6 us: local(): w_all = lax.all_gather(both, ('frames', 'pos'), axis=0, tiled=True)]
    all_to_all x3 -> x0, starting transfers between devices: 14.2 us -> none  [the longest x2 9.33 us: scattered(): lax.all_to_all(summed.astype(BF), 'pos', split_axis=0, concat_axis=0, til...]
    all_to_all x3 -> x0, waiting for transfers between devices: 12.8 us -> none  [the longest x2 12.8 us: scattered(): lax.all_to_all(summed.astype(BF), 'pos', split_axis=0, concat_axis=0, til...]
    all_gather x2 -> x0, local copies, waits for them, and re-layouts: 7.82 us -> none  [gathered(): every = lax.all_gather(rows, 'frames', axis=0, tiled=False)]
    slice x1 -> x2, local copies, waits for them, and re-layouts: 9.57 us -> 13.4 us  [local(): grads[1]]
  transfers between devices with their start and end apart: 10 -> 0, of which waited for: 5 -> 0; matrix products, arithmetic and copies ran while one was open for 17% -> 0% of each run, Pallas kernels for 0% -> 0%
where the time goes in v2:
time: 533 us; the launch traced here: 527 us
  Pallas kernels  335 us (63%)
  local copies, waits for them, and re-layouts  94.5 us (18%)
  matrix products  66.9 us (13%)
  other arithmetic  28.7 us (5%)
    pallas_call x1, Pallas kernels, local(): call(functools.partial(first_kernel, nf, nz), 0, out_shape=(jax.ShapeDtyp...  124 us
    pallas_call x1, Pallas kernels, local(): call(functools.partial(last_kernel, nf, nz), 4, out_shape=(jax.ShapeDtype...  118 us
    pallas_call x2, Pallas kernels, scattered(): call(functools.partial(back_kernel, nf, nz), ident, out_shape=back_shape,...  62.9 us
    unnamed x69, local copies, waits for them, and re-layouts  32.2 us
    pallas_call x1, Pallas kernels, local(): call(functools.partial(rows_kernel, nf, nz), 1, out_shape=rows_shape, in_...  29.9 us
    concatenate x1, local copies, waits for them, and re-layouts, local(): jnp.concatenate((qkv_weight_grad.astype(BF), out_weight_grad.astype(BF),...  13.5 us
    slice x2, local copies, waits for them, and re-layouts, local(): grads[1]  13.4 us

profile of v2, /device:TPU:0, one launch (start us, length us, event | category | flops | bytes accessed | tf_op | source)
XLA Modules:
  0.0 526.6 jit_solution(6042144660970804666)
XLA Ops:
  6.2 4.0 copy.68
  10.2 5.2 copy.66
  20.8 123.7 %shard_map.169 = (bf16[8,4,32,4096]{3,2,1,0:T(8,128)(2,1)}, bf16[8,4,64,1024]{3,2,1,0:T(8,128)(2,1)}, bf16[8,2,4,352,128]{4,3,2,1,0:T(8,128)(2,1)}) custom-call(bf16[32,4096]{1,0:T(8,128)(2,1)} %pad_maximum_fusion.1.attn, bf16[4,64,1024]{2,1,0:T(8,128)(2,1)} %bitcast.210, bf16[8,2,4,352,128]{4,3,2,1,0:T(8,128)(2,1)} %pad_maximum_fusion.pair), custom_call_target="tpu_custom_call" | custom-call | tf_op jit(solution)/shard_map/pallas_call | solution.py:410
  145.3 5.8 %fusion.1 = bf16[16,16,3072]{2,1,0:T(8,128)(2,1)} fusion(bf16[1024,4096]{1,0:T(8,128)(2,1)} %bitcast.216, bf16[16,16,1024]{2,1,0:T(8,128)(2,1)S(1)} %copy-done.15, f32[1024]{0:T(1024)S(1)} %copy-done.29, f32[16,16]{1,0:T(8,128)S(1)} %fusion.59), kind=kOutput, calls=%fused_computation.8 | convolution fusion | flops 1611661312 | bytes 8393728 | tf_op jit(solution)/shard_map/fpd,de->fpe/dot_general | solution.py:432
  151.1 4.1 reshape.152
  163.8 29.9 %shard_map.170 = bf16[8,4,64,1024]{3,2,1,0:T(8,128)(2,1)} custom-call(bf16[4,64,1024]{2,1,0:T(8,128)(2,1)} %bitcast.211), custom_call_target="tpu_custom_call" | custom-call | tf_op jit(solution)/shard_map/pallas_call | solution.py:438
  196.7 4.7 slice_bitcast_fusion.4
  201.5 3.3 fusion.7
  204.7 3.3 fusion.3
  208.4 9.2 %fusion.12 = (bf16[4,352,512]{2,1,0:T(8,128)(2,1)S(1)}, bf16[4,352,512]{2,1,0:T(8,128)(2,1)S(1)}, bf16[4,352,512]{2,1,0:T(8,128)(2,1)}) fusion(f32[4,352,512]{2,1,0:T(8,128)} %fusion.7, f32[4,352,512]{2,1,0:T(8,128)} %fusion.3, bf16[4,512,1024]{2,1,0:T(8,128)(2,1)S(1)} %bitcast.199, f32[4,352,1024]{2,1,0:T(8,128)} %param.18), kind=kOutput, calls=%fused_computation.22 | convolution fusion | flops 1488650240 | bytes 20054016 | tf_op jit(solution)/shard_map/prd,phd->phr/dot_general | solution.py:450
  225.0 31.8 %shard_map.172 = bf16[4,64,1024]{2,1,0:T(8,128)(2,1)} custom-call(bf16[8,4,64,1024]{3,2,1,0:T(8,128)(2,1)} %bitcast.197), custom_call_target="tpu_custom_call" | custom-call | tf_op jit(solution)/shard_map/pallas_call | solution.py:396
  258.8 5.0 convolution_convert_fusion
  266.4 31.1 %shard_map.171 = bf16[4,64,1024]{2,1,0:T(8,128)(2,1)} custom-call(bf16[8,4,64,1024]{3,2,1,0:T(8,128)(2,1)} %bitcast.198), custom_call_target="tpu_custom_call" | custom-call | tf_op jit(solution)/shard_map/pallas_call | solution.py:396
  317.3 5.5 %fusion.44 = (f32[1024]{0:T(1024)S(1)}, f32[16,16]{1,0:T(8,128)S(1)}, f32[16,16,1024]{2,1,0:T(8,128)S(1)}) fusion(bf16[16,16,1024]{2,1,0:T(8,128)(2,1)} %param.10, f32[16,16]{1,0:T(8,128)S(1)} %copy-done.28, f32[1024]{0:T(1024)S(1)} %copy-done.30, bf16[16,16,3072]{2,1,0:T(8,128)(2,1)} %convert_element_type.143, bf16[1024,4096]{1,0:T(8,128)(2,1)} %bitcast.219), kind=kOutput, calls=%fused_computation.76 | convolution fusion | flops 1612446464 | bytes 9447424 | tf_op jit(solution)/shard_map/fpe,de->fpd/dot_general | solution.py:477
  324.5 4.6 bitcast_convert_fusion
  332.4 13.5 %concatenate.8 = bf16[1024,4224]{1,0:T(8,128)(2,1)} concatenate(bf16[1024,3072]{1,0:T(8,128)(2,1)} %bitcast_convert_fusion, bf16[1024,1024]{1,0:T(8,128)(2,1)S(1)} %bitcast_convert_fusion.1, bf16[1024,2]{1,0:T(8,128)(2,1)} %copy.88, bf16[1024,2]{1,0:T(8,128)(2,1)} %copy.89, bf16[1024,124]{1,0:T(8,128)(2,1)} %broadcast_in_dim.57), dimensions={1} | concatenate | bytes 17301504 | tf_op jit(solution)/shard_map/concatenate | solution.py:485
  345.9 3.9 convolution_convert_fusion.1
  359.1 118.4 %shard_map.173 = (f32[32,4224]{1,0:T(8,128)}, bf16[8,2,4,352,128]{4,3,2,1,0:T(8,128)(2,1)}) custom-call(bf16[8,4,32,4224]{3,2,1,0:T(8,128)(2,1)} %bitcast.191, bf16[8,2,4,352,128]{4,3,2,1,0:T(8,128)(2,1)} %maximum_bitcast_fusion.pair), custom_call_target="tpu_custom_call" | custom-call | tf_op jit(solution)/shard_map/pallas_call | solution.py:489
  482.4 8.5 %convert_bitcast_fusion = f32[2,4,128,8,352]{2,4,1,0,3:T(8,128)} fusion(bf16[8,2,4,352,128]{4,3,2,1,0:T(8,128)(2,1)} %get-tuple-element.18), kind=kLoop, calls=%fused_computation.1 | loop fusion | flops 2883584 | bytes 17301504 | tf_op jit(solution)/shard_map/convert_element_type | solution.py:500
  490.9 7.8 %fusion.63 = (f32[1,4,128,8,352]{2,4,1,0,3:T(8,128)}, f32[1,4,128,8,352]{2,4,1,0,3:T(8,128)S(1)}) fusion(f32[2,4,128,8,352]{2,4,1,0,3:T(8,128)} %convert_bitcast_fusion), kind=kLoop, calls=%fused_computation.113 | loop fusion | bytes 23068672 | tf_op jit(solution)/shard_map/slice | solution.py:510
  501.7 6.2 %copy.94 = f32[4,128,2816]{2,1,0:T(8,128)} copy(f32[4,128,2816]{1,2,0:T(8,128)} %bitcast.192) | data formatting | bytes 11534336
  507.9 5.6 %copy.93 = f32[1,4,128,8,352]{2,4,3,1,0:T(8,128)} copy(f32[1,4,128,8,352]{2,4,1,0,3:T(8,128)} %get-tuple-element.43) | data formatting | bytes 11534336 | tf_op jit(solution)/shard_map/slice | solution.py:510
  513.5 6.3 %copy.95 = f32[4,128,2816]{2,1,0:T(8,128)} copy(f32[4,128,2816]{1,2,0:T(8,128)} %bitcast.193) | data formatting | bytes 11534336
  519.8 6.4 %fusion.65 = f32[4,352,1024]{2,1,0:T(8,128)} fusion(bf16[4,352,512]{2,1,0:T(8,128)(2,1)S(1)} %copy-done.8, bf16[4,512,1024]{2,1,0:T(8,128)(2,1)} %bitcast.200), kind=kOutput, calls=%fused_computation.115 | convolution fusion | flops 1476395008 | bytes 11403264 | tf_op jit(solution)/shard_map/phr,prd->phd/dot_general | solution.py:465
  (124 shorter events, 77.3 us)
Async XLA Ops:
  20.8 123.7 %copy-start.15 = (bf16[16,16,1024]{2,1,0:T(8,128)(2,1)S(1)}, bf16[16,16,1024]{2,1,0:T(8,128)(2,1)}, u32[]{:S(2)}) copy-start(bf16[16,16,1024]{2,1,0:T(8,128)(2,1)} %param.10) | copy-start | bytes 1572868
  20.8 124.5 %copy-start.29 = (f32[1024]{0:T(1024)S(1)}, f32[1024]{0:T(1024)}, u32[]{:S(2)}) copy-start(f32[1024]{0:T(1024)} %param.12) | copy-start | bytes 12292
  156.2 1.8 copy-start.21
  157.1 1.8 copy-start.13
  159.9 2.8 copy-start.24
  159.9 2.6 copy-start.26
  196.7 8.0 %copy-start = (bf16[4,8,4,16,1024]{4,3,2,1,0:T(8,128)(2,1)}, bf16[4,8,4,16,1024]{4,3,2,1,0:T(8,128)(2,1)S(1)}, u32[]{:S(2)}) copy-start(bf16[4,8,4,16,1024]{4,3,2,1,0:T(8,128)(2,1)S(1)} %copy.77) | copy-start | bytes 12582916
  204.7 3.3 copy-start.9
  208.4 9.2 %copy-start.2 = (bf16[4,8,4,16,1024]{4,3,2,1,0:T(8,128)(2,1)}, bf16[4,8,4,16,1024]{4,3,2,1,0:T(8,128)(2,1)S(1)}, u32[]{:S(2)}) copy-start(bf16[4,8,4,16,1024]{4,3,2,1,0:T(8,128)(2,1)S(1)} %copy.81) | copy-start | bytes 12582916
  217.6 2.4 copy-start.3
  217.7 2.4 copy-start.5
  256.8 2.0 copy-start.7
  266.4 32.2 %copy-start.12 = (bf16[16,16,1024]{2,1,0:T(8,128)(2,1)S(1)}, bf16[16,16,1024]{2,1,0:T(8,128)(2,1)}, u32[]{:S(2)}) copy-start(bf16[16,16,1024]{2,1,0:T(8,128)(2,1)} %param.19) | copy-start | bytes 1572868
  300.9 6.1 %copy-start.14 = (f32[16,16,16,16]{2,3,1,0:T(8,128)S(1)}, f32[16,16,16,16]{2,3,1,0:T(8,128)}, u32[]{:S(2)}) copy-start(f32[16,16,16,16]{2,3,1,0:T(8,128)} %copy-done.13) | copy-start | bytes 786436
  307.0 2.5 copy-start.22
  314.1 3.2 copy-start.28
  314.1 3.2 copy-start.30
  317.3 5.5 %copy-start.11 = (f32[16,16,1024]{2,1,0:T(8,128)S(1)}, f32[16,16,1024]{2,1,0:T(8,128)}, u32[]{:S(2)}) copy-start(f32[16,16,1024]{2,1,0:T(8,128)} %copy-done.10) | copy-start | bytes 3145732
  317.3 5.5 %copy-start.17 = (bf16[16,16,1024]{2,1,0:T(8,128)(2,1)S(1)}, bf16[16,16,1024]{2,1,0:T(8,128)(2,1)}, u32[]{:S(2)}) copy-start(bf16[16,16,1024]{2,1,0:T(8,128)(2,1)} %param.10) | copy-start | bytes 1572868
  324.5 4.6 copy-start.25
  332.4 13.5 %copy-start.6 = (bf16[4,352,512]{2,1,0:T(8,128)(2,1)S(1)}, bf16[4,352,512]{2,1,0:T(8,128)(2,1)}, u32[]{:S(2)}) copy-start(bf16[4,352,512]{2,1,0:T(8,128)(2,1)} %copy-done.5) | copy-start | bytes 4325380
  350.6 2.2 copy-start.1
  350.6 2.6 copy-start.4
  513.5 6.3 %copy-start.8 = (bf16[4,352,512]{2,1,0:T(8,128)(2,1)S(1)}, bf16[4,352,512]{2,1,0:T(8,128)(2,1)}, u32[]{:S(2)}) copy-start(bf16[4,352,512]{2,1,0:T(8,128)(2,1)} %get-tuple-element.47) | copy-start | bytes 4325380
  (7 other events, 8.2 us)

commit v3 on v2

--- a/solution.py
+++ b/solution.py
@@ -55,10 +55,10 @@
 
 
 class Gather:
-    def __init__(self, nf, nz, src_for, out, sems):
+    def __init__(self, nf, nz, src_for, out_at, sems):
         self.nf, self.nz, self.nc = nf, nz, nf // 2
         self.f, self.z = place()
-        self.src_for, self.out, self.sems = src_for, out, sems
+        self.src_for, self.out_at, self.sems = src_for, out_at, sems
         self.sent = []
         self.tree = self.nc == 4
 
@@ -82,14 +82,14 @@
     def begin(self):
         f, z = self.f, self.z
         for k in range(1, self.nz):
-            self.push(self.src_for(flip(z, k)), self.out.at[f, z], 0, k, (f, flip(z, k)))
-        self.own = pltpu.make_async_copy(self.src_for(z), self.out.at[f, z], self.sems.at[0, 0, 0])
+            self.push(self.src_for(flip(z, k)), self.out_at(f, z), 0, k, (f, flip(z, k)))
+        self.own = pltpu.make_async_copy(self.src_for(z), self.out_at(f, z), self.sems.at[0, 0, 0])
         self.own.start()
         self.spread(self.src_for(z), 0)
 
     def spread(self, src, k):
         f, z = self.f, self.z
-        block = self.out.at[f, flip(z, k)]
+        block = self.out_at(f, flip(z, k))
         for m in range(1, self.nc):
             if self.tree and m == 3:
                 continue
@@ -97,13 +97,13 @@
         self.push(src, block, self.nc, k, (flip(f, 1), z))
 
     def along(self, k):
-        block = self.out.at[self.f, flip(self.z, k)]
+        block = self.out_at(self.f, flip(self.z, k))
         self.arrive(block, 0, k)
         self.spread(block, k)
 
     def over(self, m, k):
         f, z = self.f, self.z
-        block = self.out.at[flip(f, 2 * m), flip(z, k)]
+        block = self.out_at(flip(f, 2 * m), flip(z, k))
         self.arrive(block, m, k)
         if self.tree and m == relay_of(k):
             self.push(block, block, 3, k, (flip(f, 2 * (3 - m)), z))
@@ -117,15 +117,15 @@
         f, z = self.f, self.z
         for k in range(self.nz):
             for m in range(self.nc):
-                self.arrive(self.out.at[flip(f, 2 * m + 1), flip(z, k)], self.nc + m, k)
+                self.arrive(self.out_at(flip(f, 2 * m + 1), flip(z, k)), self.nc + m, k)
         self.own.wait()
         for copy in self.sent:
             copy.wait_send()
 
 
 class Swap:
-    def __init__(self, nf, src, out, sems):
-        self.nf, self.src, self.out, self.sems = nf, src, out, sems
+    def __init__(self, nf, src_at, out_at, sems):
+        self.nf, self.src_at, self.out_at, self.sems = nf, src_at, out_at, sems
         self.f, self.z = place()
         self.sent = []
 
@@ -135,13 +135,13 @@
 
     def start(self):
         f, z = self.f, self.z
-        self.own = pltpu.make_async_copy(self.src.at[f], self.out.at[f], self.sems.at[0, 0])
+        self.own = pltpu.make_async_copy(self.src_at(f), self.out_at(f), self.sems.at[0, 0])
         self.own.start()
         for m in range(self.nf - 1, 0, -1):
             self.sent.append(
                 remote(
-                    self.src.at[flip(f, m)],
-                    self.out.at[f],
+                    self.src_at(flip(f, m)),
+                    self.out_at(f),
                     self.sems.at[0, m],
                     self.sems.at[1, m],
                     (flip(f, m), z),
@@ -155,12 +155,13 @@
 
 
 class Scatter:
-    def __init__(self, nf, nz, src, sib, tx, rx, ty, land, sems):
+    def __init__(self, nf, nz, src_at, own_at, sib, rx, land, sems):
         self.nf, self.nz, self.nc = nf, nz, nf // 2
         self.f, self.z = place()
-        self.src, self.sib, self.tx, self.rx, self.ty = src, sib, tx, rx, ty
+        self.src_at, self.own_at, self.sib, self.rx = src_at, own_at, sib, rx
         self.land, self.sems = land, sems
         self.sent = []
+        self.tree = self.nc == 4
 
     @staticmethod
     def scratch(nf, nz, rows, columns):
@@ -168,10 +169,8 @@
         block = (rows, columns)
         return [
             pltpu.VMEM((nz, nc) + block, BF),
-            pltpu.VMEM((nz, nc) + block, BF),
-            pltpu.VMEM((nz, nc) + block, BF),
-            pltpu.VMEM((nz,) + block, BF),
-            pltpu.VMEM((nz,) + block, BF),
+            pltpu.VMEM((nz, nc - 1) + block, BF),
+            pltpu.VMEM((nz - 1,) + block, BF),
             pltpu.SemaphoreType.DMA((2, 1 + 2 * nc, nz)),
         ]
 
@@ -189,11 +188,17 @@
             device_id_type=MESH,
         ).wait_recv()
 
+    def first(self, k):
+        if self.tree:
+            return [3, relay_of(k)]
+        return list(range(self.nc - 1, 0, -1))
+
     def pairs(self, k):
         f, z = self.f, self.z
-        for m in list(range(self.nc - 1, 0, -1)) + [0]:
+        order = self.first(k)
+        for m in order + [m for m in range(self.nc - 1, -1, -1) if m not in order]:
             self.push(
-                self.src.at[flip(f, 2 * m + 1), flip(z, k)],
+                self.src_at(flip(f, 2 * m + 1), flip(z, k)),
                 self.sib.at[k, m],
                 self.nc + m,
                 k,
@@ -202,26 +207,41 @@
 
     def chips(self, k):
         f, z = self.f, self.z
-        for m in list(range(self.nc - 1, 0, -1)):
+        for m in self.first(k):
             self.arrive(self.sib.at[k, m], self.nc + m, k)
-            add_into(self.tx.at[k, m], self.src.at[flip(f, 2 * m), flip(z, k)], self.sib.at[k, m])
-            self.push(self.tx.at[k, m], self.rx.at[k, m], m, k, (flip(f, 2 * m), z))
-
-    def home(self, k, out=None):
+            add_into(self.sib.at[k, m], self.own_at(k, m), self.sib.at[k, m])
+            hop, to = m, m
+            if self.tree:
+                hop, to = (2 if m == 3 else 1), relay_of(k)
+            self.push(self.sib.at[k, m], self.rx.at[k, hop - 1], hop, k, (flip(f, 2 * to), z))
+
+    def across(self, k):
+        if not self.tree:
+            return
+        f, z = self.f, self.z
+        m = 3 - relay_of(k)
+        self.arrive(self.sib.at[k, m], self.nc + m, k)
+        self.arrive(self.rx.at[k, 1], 2, k)
+        add_into(self.sib.at[k, m], self.own_at(k, m), self.sib.at[k, m], self.rx.at[k, 1])
+        self.push(self.sib.at[k, m], self.rx.at[k, 2], 3, k, (flip(f, 2 * m), z))
+
+    def home(self, k, out):
         f, z = self.f, self.z
         self.arrive(self.sib.at[k, 0], self.nc, k)
+        terms = [self.own_at(k, 0), self.sib.at[k, 0]]
         for m in range(1, self.nc):
-            self.arrive(self.rx.at[k, m], m, k)
-        terms = [self.src.at[f, flip(z, k)], self.sib.at[k, 0]]
-        terms += [self.rx.at[k, m] for m in range(1, self.nc)]
+            if self.tree and m == 2:
+                continue
+            self.arrive(self.rx.at[k, m - 1], m, k)
+            terms.append(self.rx.at[k, m - 1])
         if k == 0:
             add_into(out, *terms)
             return
-        add_into(self.ty.at[k], *terms)
-        self.push(self.ty.at[k], self.land.at[k], 0, k, (f, flip(z, k)))
+        add_into(self.sib.at[k, 0], *terms)
+        self.push(self.sib.at[k, 0], self.land.at[k - 1], 0, k, (f, flip(z, k)))
 
     def landed(self, k):
-        self.arrive(self.land.at[k], 0, k)
+        self.arrive(self.land.at[k - 1], 0, k)
 
     def finish(self):
         for copy in self.sent:
@@ -274,9 +294,9 @@
 
 def first_kernel(nf, nz, attn, gy, pair, attn_all, gy_all, pair_all, s1, s2, s3):
     greet(nf, nz, True)
-    weights = Gather(nf, nz, lambda zz: attn, attn_all, s1)
-    rows = Gather(nf, nz, lambda zz: gy.at[zz], gy_all, s2)
-    swap = Swap(nf, pair, pair_all, s3)
+    weights = Gather(nf, nz, lambda zz: attn, lambda ff, zz: attn_all.at[ff, zz], s1)
+    rows = Gather(nf, nz, lambda zz: gy.at[zz], lambda ff, zz: gy_all.at[ff, zz], s2)
+    swap = Swap(nf, lambda ff: pair.at[ff], lambda ff: pair_all.at[ff], s3)
     weights.begin()
     rows.begin()
     swap.start()
@@ -288,44 +308,421 @@
 
 def rows_kernel(nf, nz, b, b_all, s1):
     greet(nf, nz, False)
-    rows = Gather(nf, nz, lambda zz: b.at[zz], b_all, s1)
+    rows = Gather(nf, nz, lambda zz: b.at[zz], lambda ff, zz: b_all.at[ff, zz], s1)
     rows.begin()
     run_gathers([rows], nz)
     rows.finish()
 
 
-def back_kernel(nf, nz, terms, out, sib, tx, rx, ty, land, sems):
+def in_place(terms):
+    f, z = place()
+    return lambda ff, zz: terms.at[ff, zz], lambda k, m: terms.at[flip(f, 2 * m), flip(z, k)]
+
+
+def back_kernel(nf, nz, terms, out, sib, rx, land, sems):
     greet(nf, nz, False)
-    s = Scatter(nf, nz, terms, sib, tx, rx, ty, land, sems)
+    s = Scatter(nf, nz, *in_place(terms), sib, rx, land, sems)
     z = s.z
-    for k in range(nz - 1, -1, -1):
-        s.pairs(k)
-    for k in range(nz - 1, -1, -1):
-        s.chips(k)
-    for k in range(nz - 1, -1, -1):
-        s.home(k, out.at[z])
+    backward = range(nz - 1, -1, -1)
+    for step in (s.pairs, s.chips, s.across, lambda k: s.home(k, out.at[z])):
+        for k in backward:
+            step(k)
     for k in range(1, nz):
         s.landed(k)
-        out[flip(z, k)] = land[k]
+        out[flip(z, k)] = land[k - 1]
     s.finish()
 
 
-def last_kernel(nf, nz, terms, pair, out, pair_all, sib, tx, rx, ty, land, sems, s2):
+def last_kernel(nf, nz, terms, pair, out, pair_all, sib, rx, land, sems, s2):
     greet(nf, nz, True)
-    s = Scatter(nf, nz, terms, sib, tx, rx, ty, land, sems)
-    swap = Swap(nf, pair, pair_all, s2)
-    for k in range(nz - 1, -1, -1):
+    s = Scatter(nf, nz, *in_place(terms), sib, rx, land, sems)
+    swap = Swap(nf, lambda ff: pair.at[ff], lambda ff: pair_all.at[ff], s2)
+    backward = range(nz - 1, -1, -1)
+    for k in backward:
         s.pairs(k)
     swap.start()
-    for k in range(nz - 1, -1, -1):
-        s.chips(k)
-    for k in range(nz - 1, -1, -1):
-        s.home(k, out)
+    for step in (s.chips, s.across, lambda k: s.home(k, out)):
+        for k in backward:
+            step(k)
     for k in range(1, nz):
         s.landed(k)
-        add_into(out, out, land.at[k])
+        add_into(out, out, land.at[k - 1])
     s.finish()
     swap.finish()
+
+
+def contract(a, b, at_a, at_b):
+    return lax.dot_general(a, b, (((at_a,), (at_b,)), ((), ())), preferred_element_type=F32)
+
+
+def nt(a, b):
+    return contract(a, b, 1, 1)
+
+
+def nn(a, b):
+    return contract(a, b, 1, 0)
+
+
+def tn(a, b):
+    return contract(a, b, 0, 0)
+
+
+def by_position(rows, npos, fr, back=False):
+    i = lax.broadcasted_iota(jnp.int32, (rows, rows), 0)
+    j = lax.broadcasted_iota(jnp.int32, (rows, rows), 1)
+    if back:
+        i, j = j, i
+    return ((i % fr) * npos + i // fr == j).astype(F32).astype(BF)
+
+
+def causal(rows, npos):
+    i = lax.broadcasted_iota(jnp.int32, (rows, rows), 0)
+    j = lax.broadcasted_iota(jnp.int32, (rows, rows), 1)
+    return jnp.logical_and(i // npos == j // npos, j <= i)
+
+
+def soft(q, k, mask):
+    s = jnp.where(mask, nt(q, k) * (1.0 / math.sqrt(HD)), -1e30)
+    e = jnp.exp(s - jnp.max(s, axis=1, keepdims=True))
+    return e / jnp.sum(e, axis=1, keepdims=True)
+
+GROUP=128
+
+def attention_fwd(npos, fr, x, gain1, gain2, w, a_out, qkv, ob, x1_out, b_out):
+    rows, d = x.shape
+    xf = x[...].astype(F32)
+    rinv1 = lax.rsqrt(jnp.mean(xf * xf, axis=1, keepdims=True) + 1e-05)
+    a_out[...] = (xf * rinv1 * gain1[...]).astype(BF)
+    step = 512
+    def project(i, c):
+        at = pl.ds(pl.multiple_of(i * step, step), step)
+        qkv[:, at] = nn(a_out[...], w[:, at]).astype(BF)
+        return c
+    lax.fori_loop(0, 3 * d // step, project, 0)
+    mask = causal(GROUP, npos)
+    low = lax.broadcasted_iota(jnp.int32, (GROUP, 2 * HD), 1) < HD
+    def heads(i, c):
+        for g in range(rows // GROUP):
+            at = pl.ds(g * GROUP, GROUP)
+            q, k, v = (qkv[at, pl.ds(pl.multiple_of(i * 2 * HD + t * d, 2 * HD), 2 * HD)] for t in range(3))
+            zero = jnp.zeros_like(q)
+            p0 = soft(jnp.where(low, q, zero), k, mask).astype(BF)
+            p1 = soft(jnp.where(low, zero, q), k, mask).astype(BF)
+            ob[at, pl.ds(pl.multiple_of(i * 2 * HD, 2 * HD), 2 * HD)] = jnp.where(low, nn(p0, v), nn(p1, v)).astype(BF)
+        return c
+    lax.fori_loop(0, d // (2 * HD), heads, 0)
+    def out(i, c):
+        at = pl.ds(pl.multiple_of(i * step, step), step)
+        x1_out[:, at] = x[:, at].astype(F32) + nn(ob[...], w[:, pl.ds(pl.multiple_of(3 * d + i * step, step), step)])
+        return c
+    lax.fori_loop(0, d // step, out, 0)
+    x1 = x1_out[...]
+    rinv2 = lax.rsqrt(jnp.mean(x1 * x1, axis=1, keepdims=True) + 1e-05)
+    b = (x1 * rinv2 * gain2[...]).astype(BF)
+    b_out[...] = nn(by_position(rows, npos, fr), b).astype(BF)
+
+
+def attention_bwd_in(npos, fr, db_pos, gy, keep, x1_ref, ob, w, gain2, dx1_s, dxb, do_s, terms):
+    rows, d = x1_ref.shape
+    db = nn(by_position(rows, npos, fr, True), db_pos[...])
+    x1 = x1_ref[...]
+    rinv2 = lax.rsqrt(jnp.mean(x1 * x1, axis=1, keepdims=True) + 1e-05)
+    n2 = db * gain2[...]
+    inner = jnp.mean(n2 * x1, axis=1, keepdims=True)
+    dx1 = keep[...] * gy[...].astype(F32) + rinv2 * n2 - x1 * (rinv2 * rinv2 * rinv2 * inner)
+    dx1_s[...] = dx1
+    dxb[...] = dx1.astype(BF)
+    step = 512
+
+    def weights(i, c):
+        at = pl.ds(pl.multiple_of(i * step, step), step)
+        to = pl.ds(pl.multiple_of(3 * d + i * step, step), step)
+        terms[:, to] = tn(ob[...], dxb[:, at]).astype(BF)
+        return c
+
+    lax.fori_loop(0, d // step, weights, 0)
+    do_s[...] = nt(dxb[...], w[:, 3 * d : 4 * d]).astype(BF)
+    return jnp.sum(db * x1 * rinv2, axis=0, keepdims=True)
+
+
+def attention_bwd_heads(npos, qkv, do_s, dqkv):
+    rows, d = do_s.shape
+    mask = causal(GROUP, npos)
+    low = lax.broadcasted_iota(jnp.int32, (GROUP, 2 * HD), 1) < HD
+    scale = 1.0 / math.sqrt(HD)
+
+    def heads(i, c):
+        for g in range(rows // GROUP):
+            at = pl.ds(g * GROUP, GROUP)
+            lanes = [pl.ds(pl.multiple_of(i * 2 * HD + t * d, 2 * HD), 2 * HD) for t in range(3)]
+            q, k, v = (qkv[at, l] for l in lanes)
+            do = do_s[at, lanes[0]]
+            zero = jnp.zeros_like(q)
+            parts = []
+            for h in range(2):
+                keep = low if h == 0 else jnp.logical_not(low)
+                p = soft(jnp.where(keep, q, zero), k, mask)
+                dp = nt(jnp.where(keep, do, zero), v)
+                ds = (p * (dp - jnp.sum(p * dp, axis=1, keepdims=True)) * scale).astype(BF)
+                parts.append((nn(ds, k), tn(ds, q), tn(p.astype(BF), do)))
+            for t in range(3):
+                dqkv[at, lanes[t]] = jnp.where(low, parts[0][t], parts[1][t]).astype(BF)
+        return c
+
+    lax.fori_loop(0, d // (2 * HD), heads, 0)
+
+
+def attention_bwd_weights(a, dqkv, terms):
+    step = 512
+
+    def weights(i, c):
+        at = pl.ds(pl.multiple_of(i * step, step), step)
+        terms[:, at] = tn(a[...], dqkv[:, at]).astype(BF)
+        return c
+
+    lax.fori_loop(0, dqkv.shape[1] // step, weights, 0)
+
+
+def attention_bwd_rows(x, dqkv, w, gain1, dx1, rows_out):
+    d = x.shape[1]
+    da = nt(dqkv[...], w[:, 0 : 3 * d])
+    xf = x[...].astype(F32)
+    rinv1 = lax.rsqrt(jnp.mean(xf * xf, axis=1, keepdims=True) + 1e-05)
+    n1 = da * gain1[...]
+    inner = jnp.mean(n1 * xf, axis=1, keepdims=True)
+    rows_out[...] = dx1[...] + rinv1 * n1 - xf * (rinv1 * rinv1 * rinv1 * inner)
+    return jnp.sum(da * xf * rinv1, axis=0, keepdims=True)
+
+
+def gains_into(gain1_grad, gain2_grad, terms):
+    d = gain1_grad.shape[1]
+    high1 = gain1_grad.astype(BF).astype(F32)
+    high2 = gain2_grad.astype(BF).astype(F32)
+    at = lax.broadcasted_iota(jnp.int32, (128, d), 0)
+    tail = jnp.where(at == 0, high1, 0.0)
+    tail = jnp.where(at == 1, high2, tail)
+    tail = jnp.where(at == 2, gain1_grad - high1, tail)
+    tail = jnp.where(at == 3, gain2_grad - high2, tail)
+    terms[:, 4 * d : 4 * d + 128] = tail.T.astype(BF)
+
+
+def by_row(ref, rows, nz):
+    return lambda ff, zz: ref.at[pl.ds(pl.multiple_of((ff * nz + zz) * rows, rows), rows)]
+
+
+def pack(master, stage, sems, send, mat):
+    nf, _, lp, ffs, _ = send.shape
+
+    def fetch(p):
+        return pltpu.make_async_copy(master.at[p], stage.at[p % 2], sems.at[p % 2])
+
+    fetch(0).start()
+
+    def body(p, carry):
+        @pl.when(p + 1 < lp)
+        def _():
+            fetch(p + 1).start()
+
+        fetch(p).wait()
+        turned = stage[p % 2].T.astype(BF)
+        for j in range(nf):
+            send[j, mat, p] = turned[j * ffs : (j + 1) * ffs]
+        return carry
+
+    lax.fori_loop(0, lp, body, 0)
+
+
+def forward_kernel(
+    nf, nz, npos, fr,
+    x, gy, keep, gain1, gain2, qkv_w, out_w, gate_w, up_w,
+    w_out, gy_all, b_all, pair_all, a, qkv, ob, x1,
+    own_w, w, gy_pos, b_pos, send, stage, sems_w, sems_gy, sems_b, sems_gate, sems_up, sems_in, sem_w,
+):
+    d = x.shape[1]
+    each = own_w.shape[0]
+    lp = npos // nz
+    greet(nf, nz, True)
+    own_w[:, : 3 * d] = qkv_w[...].astype(BF)
+    own_w[:, 3 * d :] = out_w[...].astype(BF)
+    weights = Gather(nf, nz, lambda zz: own_w, by_row(w, each, nz), sems_w)
+    weights.begin()
+    turn = by_position(npos * fr, npos, fr)
+    kept = (gy[...].astype(F32) * keep[...]).astype(BF)
+    gy_pos[...] = nn(turn, kept).astype(BF).reshape(gy_pos.shape)
+    grads = Gather(nf, nz, lambda zz: gy_pos.at[zz], lambda ff, zz: gy_all.at[ff, zz], sems_gy)
+    pack(gate_w, stage, sems_in, send, 0)
+    for k in range(1, nz):
+        weights.along(k)
+    for k in range(nz):
+        weights.over(relay_of(k), k)
+    grads.begin()
+    pack(up_w, stage, sems_in, send, 1)
+    for k in range(nz):
+        for m in weights.order(k)[1:]:
+            weights.over(m, k)
+    for k in range(1, nz):
+        grads.along(k)
+    gate = Swap(nf, lambda ff: send.at[ff, 0], lambda ff: pair_all.at[ff, 0], sems_gate)
+    up = Swap(nf, lambda ff: send.at[ff, 1], lambda ff: pair_all.at[ff, 1], sems_up)
+    gate.start()
+    for k in range(nz):
+        grads.over(relay_of(k), k)
+    weights.finish()
+    save = pltpu.make_async_copy(w, w_out, sem_w)
+    save.start()
+    attention_fwd(npos, fr, x, gain1, gain2, w, a, qkv, ob, x1, b_pos)
+    rows = Gather(nf, nz, lambda zz: b_pos.at[pl.ds(pl.multiple_of(zz * lp * fr, lp * fr), lp * fr)], lambda ff, zz: b_all.at[ff, zz], sems_b)
+    rows.begin()
+    for k in range(nz):
+        for m in grads.order(k)[1:]:
+            grads.over(m, k)
+    for k in range(1, nz):
+        rows.along(k)
+    for k in range(nz):
+        rows.over(relay_of(k), k)
+    up.start()
+    for k in range(nz):
+        for m in rows.order(k)[1:]:
+            rows.over(m, k)
+    save.wait()
+    rows.finish()
+    grads.finish()
+    gate.finish()
+    up.finish()
+
+
+def feed_kernel(gy, b, pair, down, db, z, grads, down_grad, wg, wu):
+    nf = pair.shape[0]
+    width = pair.shape[4]
+    rows, d = gy.shape[0] * gy.shape[1] * gy.shape[2], gy.shape[3]
+    for s in range(nf):
+        wg[:, s * width : (s + 1) * width] = pair[s, 0, 0]
+        wu[:, s * width : (s + 1) * width] = pair[s, 1, 0]
+    b_rows = b[...].reshape(rows, d)
+    gy_rows = gy[...].reshape(rows, d)
+    wd = down[0].astype(BF)
+    gate = nt(wg[...], b_rows)
+    up = nt(wu[...], b_rows)
+    dhid = nt(wd, gy_rows)
+    s = jax.nn.sigmoid(gate)
+    silu = gate * s
+    hid = (silu * up).astype(BF)
+    dgate = (dhid * up * s * (1.0 + gate * (1.0 - s))).astype(BF)
+    dup = (dhid * silu).astype(BF)
+    for at, term in enumerate((dgate, dup)):
+        grad = nn(term, b_rows).astype(BF)
+        for j in range(nf):
+            grads[j, at, 0] = grad[:, j * width : (j + 1) * width]
+    down_grad[0] = nn(hid, gy_rows)
+    db[...] = (tn(dgate, wg[...]) + tn(dup, wu[...])).astype(BF).reshape(db.shape)
+    z[...] = tn(hid, wd).astype(BF).reshape(z.shape)
+
+
+def backward_kernel(
+    nf, nz, npos, fr,
+    db_terms, z_terms, grads, w_in, x, gy, keep, gain1, gain2, x1, a, qkv, ob,
+    block_out, rows_grad, total, pair_all,
+    db_own, db_sib, db_rx, db_land, db_sems,
+    z_own, z_sib, z_rx, z_land, z_sems,
+    t_sib, t_rx, t_land, t_sems,
+    sems_gate, sems_up, sems_own, sem_w,
+    w, terms, db_rows, z_rows, dx1, dxb, do, dqkv,
+):
+    d = x.shape[1]
+    each = total.shape[0]
+    lrows = db_own.shape[2]
+    nc = nf // 2
+    f, z = place()
+    greet(nf, nz, True)
+    backward = range(nz - 1, -1, -1)
+
+    def own_copies(src, own, at):
+        return [
+            pltpu.make_async_copy(
+                src.at[flip(f, 2 * m), flip(z, k)], own.at[k, m], sems_own.at[at, k, m]
+            )
+            for k in backward
+            for m in range(nc)
+        ]
+
+    def scatter(src, own, sib, rx, land, sems):
+        return Scatter(
+            nf, nz, lambda ff, zz: src.at[ff, zz], lambda k, m: own.at[k, m], sib, rx, land, sems
+        )
+
+    s_db = scatter(db_terms, db_own, db_sib, db_rx, db_land, db_sems)
+    s_z = scatter(z_terms, z_own, z_sib, z_rx, z_land, z_sems)
+    for k in backward:
+        s_db.pairs(k)
+    load_db = own_copies(db_terms, db_own, 0)
+    load_z = own_copies(z_terms, z_own, 1)
+    for copy in load_db:
+        copy.start()
+    load_w = pltpu.make_async_copy(w_in, w, sem_w)
+    load_w.start()
+    for copy in load_db:
+        copy.wait()
+    for k in backward:
+        s_db.chips(k)
+    for k in backward:
+        s_z.pairs(k)
+    for copy in load_z:
+        copy.start()
+    for k in backward:
+        s_db.across(k)
+
+    def at_pos(zz):
+        return pl.ds(pl.multiple_of(zz * lrows, lrows), lrows)
+
+    for k in backward:
+        s_db.home(k, db_rows.at[at_pos(z)])
+    gate = Swap(nf, lambda ff: grads.at[ff, 0], lambda ff: pair_all.at[ff, 0], sems_gate)
+    up = Swap(nf, lambda ff: grads.at[ff, 1], lambda ff: pair_all.at[ff, 1], sems_up)
+    for copy in load_z:
+        copy.wait()
+    for k in backward:
+        s_z.chips(k)
+    gate.start()
+    for k in range(1, nz):
+        s_db.landed(k)
+        db_rows[at_pos(flip(z, k)), :] = db_land[k - 1]
+    load_w.wait()
+    gain2_grad = attention_bwd_in(npos, fr, db_rows, gy, keep, x1, ob, w, gain2, dx1, dxb, do, terms)
+    for k in backward:
+        s_z.across(k)
+    up.start()
+    attention_bwd_heads(npos, qkv, do, dqkv)
+    for k in backward:
+        s_z.home(k, z_rows.at[at_pos(z)])
+    attention_bwd_weights(a, dqkv, terms)
+    gain1_grad = attention_bwd_rows(x, dqkv, w, gain1, dx1, rows_grad)
+    gains_into(gain1_grad, gain2_grad, terms)
+    src_at = by_row(terms, each, nz)
+    s_t = Scatter(
+        nf, nz, src_at, lambda k, m: src_at(flip(f, 2 * m), flip(z, k)), t_sib, t_rx, t_land, t_sems
+    )
+    for step in (s_t.pairs, s_t.chips):
+        for k in backward:
+            step(k)
+    for k in range(1, nz):
+        s_z.landed(k)
+        z_rows[at_pos(flip(z, k)), :] = z_land[k - 1]
+    back = nn(by_position(npos * fr, npos, fr, True), z_rows[...])
+    block_out[...] = (keep[...] * (x1[...] + back)).astype(BF)
+    for step in (s_t.across, lambda k: s_t.home(k, total)):
+        for k in backward:
+            step(k)
+    for k in range(1, nz):
+        s_t.landed(k)
+        add_into(total, total, t_land.at[k - 1])
+    for task in (s_db, s_z, s_t, gate, up):
+        task.finish()
+
+
+def unpack_kernel(pair, gate, up):
+    nf, _, _, ffs, width = pair.shape
+    for at, out in enumerate((gate, up)):
+        out[0] = pair[:, at, 0].astype(F32).reshape(nf * ffs, width).T
 
 
 def rms_norm(values, gain_vector):
@@ -351,7 +748,7 @@
     return mixed.reshape(frame_count, positions, H * HD)
 
 
-def local(
+def local_general(
     frame_rows,
     frame_mask,
     gain_attention,
@@ -510,6 +907,146 @@
         grads[1],
         down_grad,
     )
+def local_fused(
+    frame_rows,
+    frame_mask,
+    gain_attention,
+    gain_feed,
+    qkv_master,
+    out_master,
+    gate_master,
+    up_master,
+    down_master,
+    out_cotangent,
+):
+    nf = lax.axis_size("frames")
+    nz = lax.axis_size("pos")
+    lp, dslice, ff = gate_master.shape
+    ffs = down_master.shape[1]
+    fr, npos, d = frame_rows.shape
+    rows = fr * npos
+    each = qkv_master.shape[0]
+
+    def make(shape, kind=BF):
+        return jax.ShapeDtypeStruct(shape, kind)
+
+    x = frame_rows.reshape(rows, d)
+    gy = out_cotangent.reshape(rows, d)
+    keep = jnp.broadcast_to(frame_mask.astype(F32)[:, None], (fr, npos)).reshape(rows, 1)
+    gain1 = gain_attention.reshape(1, d)
+    gain2 = gain_feed.reshape(1, d)
+    gather_sems = pltpu.SemaphoreType.DMA(Gather.sem_shape(nf, nz))
+    swap_sems = pltpu.SemaphoreType.DMA(Swap.sem_shape(nf))
+    rows_shape = make((nf, nz, lp * fr, d))
+    pair_shape = make((nf, 2, lp, ffs, dslice))
+    w_all, gy_all, b_all, pair_all, a, qkv, ob, x1 = call(
+        functools.partial(forward_kernel, nf, nz, npos, fr),
+        0,
+        out_shape=(
+            make((d, 4 * d)),
+            rows_shape,
+            rows_shape,
+            pair_shape,
+            make((rows, d)),
+            make((rows, 3 * d)),
+            make((rows, d)),
+            make((rows, d), F32),
+        ),
+        in_specs=[VM] * 7 + [ANY] * 2,
+        out_specs=(ANY,) * 4 + (VM,) * 4,
+        scratch_shapes=[
+            pltpu.VMEM((each, 4 * d), BF),
+            pltpu.VMEM((d, 4 * d), BF),
+            pltpu.VMEM((nz, lp * fr, d), BF),
+            pltpu.VMEM((rows, d), BF),
+            pltpu.VMEM(pair_shape.shape, BF),
+            pltpu.VMEM((2, dslice, ff), F32),
+            gather_sems,
+            gather_sems,
+            gather_sems,
+            swap_sems,
+            swap_sems,
+            pltpu.SemaphoreType.DMA((2,)),
+            pltpu.SemaphoreType.DMA,
+        ],
+    )(x, gy, keep, gain1, gain2, qkv_master, out_master, gate_master, up_master)
+    rows_block = pl.BlockSpec((nf, nz, fr, d), lambda p: (0, 0, p, 0))
+    pair_block = pl.BlockSpec((nf, 2, 1, ffs, dslice), lambda p: (0, 0, p, 0, 0))
+    down_block = pl.BlockSpec((1, ffs, d), lambda p: (p, 0, 0))
+    local_params = pltpu.CompilerParams(vmem_limit_bytes=56 * 2**20)
+    db_terms, z_terms, grads, down_grad = pl.pallas_call(
+        feed_kernel,
+        grid=(lp,),
+        out_shape=(rows_shape, rows_shape, pair_shape, make((lp, ffs, d), F32)),
+        in_specs=[rows_block, rows_block, pair_block, down_block],
+        out_specs=(rows_block, rows_block, pair_block, down_block),
+        scratch_shapes=[pltpu.VMEM((ffs, d), BF)] * 2,
+        compiler_params=local_params,
+    )(gy_all, b_all, pair_all, down_master)
+    small = (nf, nz, lp * fr, d)
+    wide = 4 * d + 128
+    own = pltpu.VMEM((nz, nf // 2, lp * fr, d), BF)
+    block_out, rows_grad, total, back = call(
+        functools.partial(backward_kernel, nf, nz, npos, fr),
+        1,
+        out_shape=(
+            make((rows, d)),
+            make((rows, d), F32),
+            make((each, wide), F32),
+            pair_shape,
+        ),
+        in_specs=[ANY] * 4 + [VM] * 9,
+        out_specs=(VM,) * 3 + (ANY,),
+        scratch_shapes=[
+            own,
+            *Scatter.scratch(*small),
+            own,
+            *Scatter.scratch(*small),
+            *Scatter.scratch(nf, nz, each, wide),
+            swap_sems,
+            swap_sems,
+            pltpu.SemaphoreType.DMA((2, nz, nf // 2)),
+            pltpu.SemaphoreType.DMA,
+            pltpu.VMEM((d, 4 * d), BF),
+            pltpu.VMEM((d, wide), BF),
+            pltpu.VMEM((rows, d), BF),
+            pltpu.VMEM((rows, d), BF),
+            pltpu.VMEM((rows, d), F32),
+            pltpu.VMEM((rows, d), BF),
+            pltpu.VMEM((rows, d), BF),
+            pltpu.VMEM((rows, 3 * d), BF),
+        ],
+    )(db_terms, z_terms, grads, w_all, x, gy, keep, gain1, gain2, x1, a, qkv, ob)
+    whole_block = pl.BlockSpec((1, dslice, ff), lambda p: (p, 0, 0))
+    gate_grad, up_grad = pl.pallas_call(
+        unpack_kernel,
+        grid=(lp,),
+        out_shape=(make((lp, dslice, ff), F32),) * 2,
+        in_specs=[pair_block],
+        out_specs=(whole_block, whole_block),
+        compiler_params=local_params,
+    )(back)
+    gains = total[:, 4 * d : 4 * d + 2] + total[:, 4 * d + 2 : 4 * d + 4]
+    return (
+        block_out.reshape(fr, npos, d),
+        rows_grad.reshape(fr, npos, d),
+        gains[:, 0],
+        gains[:, 1],
+        total[:, : 3 * d],
+        total[:, 3 * d : 4 * d],
+        gate_grad,
+        up_grad,
+        down_grad,
+    )
+
+
+def local(*args):
+    _, dslice, _ = args[6].shape
+    if lax.axis_size("frames") == 8 and dslice % 128 == 0:
+        return local_fused(*args)
+    return local_general(*args)
+
+
 def solution(mesh):
     in_specs = (
         P(("frames", "pos"), None, None),

time: 533 us -> 352 us (0.66); the launches traced: 527 us -> 351 us
  local copies, waits for them, and re-layouts: 94.5 us -> 6.64 us
  matrix products: 66.9 us -> 0 us
  other arithmetic: 28.7 us -> 1.58 us
  Pallas kernels: 335 us -> 342 us
    dot_general x21 -> x0, matrix products: 66.9 us -> none  [the longest x1 9.18 us: local(): jnp.einsum('prd,phd->phr', gy, down, preferred_element_type=F32)]
    unnamed x69 -> x6, local copies, waits for them, and re-layouts: 32.2 us -> 1.77 us
    slice x7 -> x3, local copies, waits for them, and re-layouts: 21.3 us -> 4.04 us  [the longest x1 1.77 us: local_fused(): total[:, :3 * d]]
    convert_element_type x9 -> x1, other arithmetic: 14.3 us -> 0.66 us  [local_fused(): frame_mask.astype(F32)[:, None]]
    concatenate x1 -> x0, local copies, waits for them, and re-layouts: 13.5 us -> none  [local(): jnp.concatenate((qkv_weight_grad.astype(BF), out_weight_grad.astype(BF),...]
    reshape x4 -> x1, local copies, waits for them, and re-layouts: 11 us -> 0.76 us  [local_fused(): jnp.broadcast_to(frame_mask.astype(F32)[:, None], (fr, npos))]
    pallas_call x5 -> x4, Pallas kernels: 335 us -> 342 us  [the longest x1 164 us: local_fused(): call(functools.partial(backward_kernel, nf, nz, npos, fr), 1, out_shape=(...]
    convert_element_type x6 -> x0, local copies, waits for them, and re-layouts: 6.73 us -> none  [the longest x2 3.97 us: local(): qkv_back = attend_pull(mixed_grad)[0].astype(BF)]
where the time goes in v3:
time: 352 us; the launch traced here: 351 us
  Pallas kernels  342 us (97%)
  local copies, waits for them, and re-layouts  6.64 us (2%)
    pallas_call x1, Pallas kernels, local_fused(): call(functools.partial(backward_kernel, nf, nz, npos, fr), 1, out_shape=(...  164 us
    pallas_call x1, Pallas kernels, local_fused(): call(functools.partial(forward_kernel, nf, nz, npos, fr), 0, out_shape=(m...  148 us
    pallas_call x1, Pallas kernels, local_fused(): pl.pallas_call(feed_kernel, grid=(lp,), out_shape=(rows_shape, rows_shape...  22.2 us
    pallas_call x1, Pallas kernels, local_fused(): pl.pallas_call(unpack_kernel, grid=(lp,), out_shape=(make((lp, dslice, ff...  7.65 us

profile of v3, /device:TPU:0, one launch (start us, length us, event | category | flops | bytes accessed | tf_op | source)
XLA Modules:
  0.0 351.3 jit_solution(8123998135336374121)
XLA Ops:
  0.6 0.7 convert_element_type.3
  1.3 0.1 broadcast_in_dim.2
  1.4 0.8 reshape.47.keep
  2.1 148.4 %shard_map.169 = (bf16[1024,4096]{1,0:T(8,128)(2,1)}, bf16[8,4,64,1024]{3,2,1,0:T(8,128)(2,1)}, bf16[8,4,64,1024]{3,2,1,0:T(8,128)(2,1)}, bf16[8,2,4,352,128]{4,...) custom-call(bf16[256,1024]{1,0:T(8,128)(2,1)} %bitcast.6, ...), custom_call_target="tpu_custom_call" | custom-call | tf_op jit(solution)/shard_map/pallas_call | solution.py:942
  150.6 22.2 %shard_map.170 = (bf16[8,4,64,1024]{3,2,1,0:T(8,128)(2,1)}, bf16[8,4,64,1024]{3,2,1,0:T(8,128)(2,1)}, bf16[8,2,4,352,128]{4,3,2,1,0:T(8,128)(2,1)}, f32[4,352,1024]{2,1,0:T(8,128)}) custom-call(bf16[8,4,64,1024]{3,2,1,0:T(8,128)(2,1)} %get-tuple-element.27.gy, bf16[8,4,64,1024]{3,2,1,0:T(8,128)(2,1)} %get-tuple-element.28.b, ...), custom_call_target="tpu_custom_call" | custom-call | tf_op jit(solution)/shard_map/pallas_call | solution.py:977
  172.7 164.1 %shard_map.171 = (bf16[256,1024]{1,0:T(8,128)(2,1)}, f32[256,1024]{1,0:T(8,128)}, f32[32,4224]{1,0:T(8,128)}, bf16[8,2,4,352,128]{4,3,2,1,0:T(8,128)(2,1)}) custom-call(bf16[8,4,64,1024]{3,2,1,0:T(8,128)(2,1)} %get-tuple-element.30.db_terms, bf16[8,4,64,1024]{3,2,1,0:T(8,128)(2,1)} %get-tuple-element.31.z_terms, ...), custom_call_target="tpu_custom_call" | custom-call | tf_op jit(solution)/shard_map/pallas_call | solution.py:989
  336.9 0.0 copy-start.1
  336.9 0.0 copy-start
  336.9 0.9 slice_add_fusion
  337.8 0.7 slice_reduce_fusion
  338.5 1.6 slice.23
  340.1 1.8 slice.22
  341.8 7.6 %shard_map.172 = (f32[4,128,2816]{2,1,0:T(8,128)}, f32[4,128,2816]{2,1,0:T(8,128)}) custom-call(bf16[8,2,4,352,128]{4,3,2,1,0:T(8,128)(2,1)} %get-tuple-element.41.pair), custom_call_target="tpu_custom_call" | custom-call | tf_op jit(solution)/shard_map/pallas_call | solution.py:1021
  349.5 0.0 copy-done.1
  349.5 0.8 copy.23
  350.3 0.0 copy-done
  350.3 1.0 copy.24
Async XLA Ops:
  336.9 12.6 %copy-start.1 = (bf16[256,1024]{1,0:T(8,128)(2,1)S(1)}, bf16[256,1024]{1,0:T(8,128)(2,1)}, u32[]{:S(2)}) copy-start(bf16[256,1024]{1,0:T(8,128)(2,1)} %get-tuple-element.38) | copy-start | bytes 1572868
  336.9 13.4 %copy-start = (f32[256,1024]{1,0:T(8,128)S(1)}, f32[256,1024]{1,0:T(8,128)}, u32[]{:S(2)}) copy-start(f32[256,1024]{1,0:T(8,128)} %get-tuple-element.39) | copy-start | bytes 3145732

commit v4 on v3

--- a/solution.py
+++ b/solution.py
@@ -154,36 +154,33 @@
             copy.wait()
 
 
-class Scatter:
-    def __init__(self, nf, nz, src_at, own_at, sib, rx, land, sems):
+class Sums:
+    def __init__(self, nf, nz, src_at, own_at, sib, rx, sems):
         self.nf, self.nz, self.nc = nf, nz, nf // 2
         self.f, self.z = place()
         self.src_at, self.own_at, self.sib, self.rx = src_at, own_at, sib, rx
-        self.land, self.sems = land, sems
+        self.sems = sems
         self.sent = []
         self.tree = self.nc == 4
 
     @staticmethod
-    def scratch(nf, nz, rows, columns):
+    def buffers(nf, parts, rows, columns):
         nc = nf // 2
-        block = (rows, columns)
         return [
-            pltpu.VMEM((nz, nc) + block, BF),
-            pltpu.VMEM((nz, nc - 1) + block, BF),
-            pltpu.VMEM((nz - 1,) + block, BF),
-            pltpu.SemaphoreType.DMA((2, 1 + 2 * nc, nz)),
+            pltpu.VMEM((parts, nc, rows, columns), BF),
+            pltpu.VMEM((parts, nc - 1, rows, columns), BF),
+            pltpu.SemaphoreType.DMA((2, 2 * nc, parts)),
         ]
 
-    def push(self, src, dst, hop, k, to):
-        copy = remote(src, dst, self.sems.at[0, hop, k], self.sems.at[1, hop, k], to)
-        self.sent.append(copy)
-
-    def arrive(self, dst, hop, k):
+    def push(self, src, dst, sems, hop, k, to):
+        self.sent.append(remote(src, dst, sems.at[0, hop, k], sems.at[1, hop, k], to))
+
+    def arrive(self, dst, sems, hop, k):
         pltpu.make_async_remote_copy(
             src_ref=dst,
             dst_ref=dst,
-            send_sem=self.sems.at[0, hop, k],
-            recv_sem=self.sems.at[1, hop, k],
+            send_sem=sems.at[0, hop, k],
+            recv_sem=sems.at[1, hop, k],
             device_id=(flip(self.f, 1), self.z),
             device_id_type=MESH,
         ).wait_recv()
@@ -197,55 +194,95 @@
         f, z = self.f, self.z
         order = self.first(k)
         for m in order + [m for m in range(self.nc - 1, -1, -1) if m not in order]:
-            self.push(
-                self.src_at(flip(f, 2 * m + 1), flip(z, k)),
-                self.sib.at[k, m],
-                self.nc + m,
-                k,
-                (flip(f, 1), z),
-            )
+            src = self.src_at(flip(f, 2 * m + 1), k)
+            self.push(src, self.sib.at[k, m], self.sems, self.nc + m, k, (flip(f, 1), z))
 
     def chips(self, k):
         f, z = self.f, self.z
         for m in self.first(k):
-            self.arrive(self.sib.at[k, m], self.nc + m, k)
-            add_into(self.sib.at[k, m], self.own_at(k, m), self.sib.at[k, m])
+            sib = self.sib.at[k, m]
+            self.arrive(sib, self.sems, self.nc + m, k)
+            add_into(sib, self.own_at(k, m), sib)
             hop, to = m, m
             if self.tree:
                 hop, to = (2 if m == 3 else 1), relay_of(k)
-            self.push(self.sib.at[k, m], self.rx.at[k, hop - 1], hop, k, (flip(f, 2 * to), z))
+            self.push(sib, self.rx.at[k, hop - 1], self.sems, hop, k, (flip(f, 2 * to), z))
 
     def across(self, k):
         if not self.tree:
             return
-        f, z = self.f, self.z
         m = 3 - relay_of(k)
-        self.arrive(self.sib.at[k, m], self.nc + m, k)
-        self.arrive(self.rx.at[k, 1], 2, k)
-        add_into(self.sib.at[k, m], self.own_at(k, m), self.sib.at[k, m], self.rx.at[k, 1])
-        self.push(self.sib.at[k, m], self.rx.at[k, 2], 3, k, (flip(f, 2 * m), z))
-
-    def home(self, k, out):
-        f, z = self.f, self.z
-        self.arrive(self.sib.at[k, 0], self.nc, k)
+        sib = self.sib.at[k, m]
+        self.arrive(sib, self.sems, self.nc + m, k)
+        self.arrive(self.rx.at[k, 1], self.sems, 2, k)
+        add_into(sib, self.own_at(k, m), sib, self.rx.at[k, 1])
+        self.push(sib, self.rx.at[k, 2], self.sems, 3, k, (flip(self.f, 2 * m), self.z))
+
+    def total(self, k, out):
+        self.arrive(self.sib.at[k, 0], self.sems, self.nc, k)
         terms = [self.own_at(k, 0), self.sib.at[k, 0]]
         for m in range(1, self.nc):
             if self.tree and m == 2:
                 continue
-            self.arrive(self.rx.at[k, m - 1], m, k)
+            self.arrive(self.rx.at[k, m - 1], self.sems, m, k)
             terms.append(self.rx.at[k, m - 1])
-        if k == 0:
-            add_into(out, *terms)
-            return
-        add_into(self.sib.at[k, 0], *terms)
-        self.push(self.sib.at[k, 0], self.land.at[k - 1], 0, k, (f, flip(z, k)))
-
-    def landed(self, k):
-        self.arrive(self.land.at[k - 1], 0, k)
+        add_into(out, *terms)
 
     def finish(self):
         for copy in self.sent:
             copy.wait_send()
+
+
+class Scatter(Sums):
+    def __init__(self, nf, nz, src_at, own_at, sib, rx, sems, land):
+        super().__init__(nf, nz, src_at, own_at, sib, rx, sems)
+        self.land = land
+
+    @staticmethod
+    def scratch(nf, nz, rows, columns):
+        sib, rx, sems = Sums.buffers(nf, nz, rows, columns)
+        return [sib, rx, pltpu.VMEM((nz - 1, rows, columns), BF), sems]
+
+    def home(self, k, out):
+        if k == 0:
+            self.total(0, out)
+            return
+        sib = self.sib.at[k, 0]
+        self.total(k, sib)
+        self.push(sib, self.land.at[k - 1], self.sems, 0, k, (self.f, flip(self.z, k)))
+
+    def landed(self, k):
+        self.arrive(self.land.at[k - 1], self.sems, 0, k)
+
+
+class RowScatter(Sums):
+    def __init__(self, nf, nz, src_at, own_at, sib, rx, sems, home_sems, land, each):
+        super().__init__(nf, nz, src_at, own_at, sib, rx, sems)
+        self.home_sems, self.land, self.each = home_sems, land, each
+
+    @staticmethod
+    def scratch(nf, nz, lp, rows, columns):
+        sib, rx, sems = Sums.buffers(nf, lp, rows, columns)
+        return [sib, rx, sems, pltpu.SemaphoreType.DMA((2, nz, lp))]
+
+    def rows_of(self, ref, at):
+        return ref.at[pl.ds(pl.multiple_of(at * self.each, self.each), self.each)]
+
+    def home(self, p):
+        f, z, lp = self.f, self.z, self.sib.shape[0]
+        whole = self.sib.at[p, 0]
+        self.total(p, whole)
+        land = self.rows_of(self.land, z * lp + p)
+        for k in range(1, self.nz):
+            src = self.rows_of(whole, flip(z, k))
+            self.push(src, land, self.home_sems, k, p, (f, flip(z, k)))
+        land[...] = self.rows_of(whole, z)[...]
+
+    def landed(self, p):
+        lp = self.sib.shape[0]
+        for k in range(1, self.nz):
+            land = self.rows_of(self.land, flip(self.z, k) * lp + p)
+            self.arrive(land, self.home_sems, k, p)
 
 
 def add_into(out, *terms):
@@ -267,7 +304,7 @@
     return pl.pallas_call(
         kernel,
         compiler_params=pltpu.CompilerParams(
-            collective_id=ident, has_side_effects=True, vmem_limit_bytes=56 * 2**20
+            collective_id=ident, has_side_effects=True, vmem_limit_bytes=60 * 2**20
         ),
         **kw,
     )
@@ -316,12 +353,15 @@
 
 def in_place(terms):
     f, z = place()
-    return lambda ff, zz: terms.at[ff, zz], lambda k, m: terms.at[flip(f, 2 * m), flip(z, k)]
+    return (
+        lambda ff, k: terms.at[ff, flip(z, k)],
+        lambda k, m: terms.at[flip(f, 2 * m), flip(z, k)],
+    )
 
 
 def back_kernel(nf, nz, terms, out, sib, rx, land, sems):
     greet(nf, nz, False)
-    s = Scatter(nf, nz, *in_place(terms), sib, rx, land, sems)
+    s = Scatter(nf, nz, *in_place(terms), sib, rx, sems, land)
     z = s.z
     backward = range(nz - 1, -1, -1)
     for step in (s.pairs, s.chips, s.across, lambda k: s.home(k, out.at[z])):
@@ -335,7 +375,7 @@
 
 def last_kernel(nf, nz, terms, pair, out, pair_all, sib, rx, land, sems, s2):
     greet(nf, nz, True)
-    s = Scatter(nf, nz, *in_place(terms), sib, rx, land, sems)
+    s = Scatter(nf, nz, *in_place(terms), sib, rx, sems, land)
     swap = Swap(nf, lambda ff: pair.at[ff], lambda ff: pair_all.at[ff], s2)
     backward = range(nz - 1, -1, -1)
     for k in backward:
@@ -396,9 +436,11 @@
     step = 512
     def project(i, c):
         at = pl.ds(pl.multiple_of(i * step, step), step)
-        qkv[:, at] = nn(a_out[...], w[:, at]).astype(BF)
+        for t in range(3):
+            to = pl.ds(pl.multiple_of(t * d + i * step, step), step)
+            qkv[:, to] = nn(a_out[...], w[t, :, at]).astype(BF)
         return c
-    lax.fori_loop(0, 3 * d // step, project, 0)
+    lax.fori_loop(0, d // step, project, 0)
     mask = causal(GROUP, npos)
     low = lax.broadcasted_iota(jnp.int32, (GROUP, 2 * HD), 1) < HD
     def heads(i, c):
@@ -413,7 +455,7 @@
     lax.fori_loop(0, d // (2 * HD), heads, 0)
     def out(i, c):
         at = pl.ds(pl.multiple_of(i * step, step), step)
-        x1_out[:, at] = x[:, at].astype(F32) + nn(ob[...], w[:, pl.ds(pl.multiple_of(3 * d + i * step, step), step)])
+        x1_out[:, at] = x[:, at].astype(F32) + nn(ob[...], w[3, :, at])
         return c
     lax.fori_loop(0, d // step, out, 0)
     x1 = x1_out[...]
@@ -441,7 +483,7 @@
         return c
 
     lax.fori_loop(0, d // step, weights, 0)
-    do_s[...] = nt(dxb[...], w[:, 3 * d : 4 * d]).astype(BF)
+    do_s[...] = nt(dxb[...], w[3]).astype(BF)
     return jnp.sum(db * x1 * rinv2, axis=0, keepdims=True)
 
 
@@ -485,7 +527,7 @@
 
 def attention_bwd_rows(x, dqkv, w, gain1, dx1, rows_out):
     d = x.shape[1]
-    da = nt(dqkv[...], w[:, 0 : 3 * d])
+    da = sum(nt(dqkv[:, t * d : (t + 1) * d], w[t]) for t in range(3))
     xf = x[...].astype(F32)
     rinv1 = lax.rsqrt(jnp.mean(xf * xf, axis=1, keepdims=True) + 1e-05)
     n1 = da * gain1[...]
@@ -510,68 +552,114 @@
     return lambda ff, zz: ref.at[pl.ds(pl.multiple_of((ff * nz + zz) * rows, rows), rows)]
 
 
-def pack(master, stage, sems, send, mat):
-    nf, _, lp, ffs, _ = send.shape
-
-    def fetch(p):
-        return pltpu.make_async_copy(master.at[p], stage.at[p % 2], sems.at[p % 2])
-
-    fetch(0).start()
-
-    def body(p, carry):
-        @pl.when(p + 1 < lp)
-        def _():
-            fetch(p + 1).start()
-
-        fetch(p).wait()
-        turned = stage[p % 2].T.astype(BF)
+def pack(masters, stage, sems, send, p):
+    nf, _, _, ffs, _ = send.shape
+    copies = [
+        pltpu.make_async_copy(master.at[p], stage.at[i], sems.at[i])
+        for i, master in enumerate(masters)
+    ]
+    for copy in copies:
+        copy.start()
+    for i, copy in enumerate(copies):
+        copy.wait()
+        turned = stage[i].T.astype(BF)
         for j in range(nf):
-            send[j, mat, p] = turned[j * ffs : (j + 1) * ffs]
-        return carry
-
-    lax.fori_loop(0, lp, body, 0)
-
-
-def forward_kernel(
+            send[j, i, p] = turned[j * ffs : (j + 1) * ffs]
+
+
+def feed(p, fr, gy_all, b_all, pair, wd, rows_g, rows_b, hid_out, grads, db, z):
+    nf, _, _, _, width = grads.shape
+    count, d = rows_b.shape
+    blocks = count // fr
+    each = b_all.shape[0] // blocks
+    for i in range(blocks):
+        rows_g[i * fr : (i + 1) * fr] = gy_all[i * each + p * fr : i * each + (p + 1) * fr]
+        rows_b[i * fr : (i + 1) * fr] = b_all[i * each + p * fr : i * each + (p + 1) * fr]
+    b_rows = rows_b[...]
+    gate = nt(pair[0, p], b_rows)
+    up = nt(pair[1, p], b_rows)
+    dhid = nt(wd, rows_g[...])
+    s = jax.nn.sigmoid(gate)
+    silu = gate * s
+    hid = (silu * up).astype(BF)
+    dgate = (dhid * up * s * (1.0 + gate * (1.0 - s))).astype(BF)
+    dup = (dhid * silu).astype(BF)
+    hid_out[p] = hid
+    db[...] = (tn(dgate, pair[0, p]) + tn(dup, pair[1, p])).astype(BF)
+    z[...] = tn(hid, wd).astype(BF)
+    for at, term in enumerate((dgate, dup)):
+        grad = nn(term, b_rows).astype(BF)
+        for j in range(nf):
+            grads[j, at, p] = grad[:, j * width : (j + 1) * width]
+
+
+def ahead_kernel(
     nf, nz, npos, fr,
-    x, gy, keep, gain1, gain2, qkv_w, out_w, gate_w, up_w,
-    w_out, gy_all, b_all, pair_all, a, qkv, ob, x1,
-    own_w, w, gy_pos, b_pos, send, stage, sems_w, sems_gy, sems_b, sems_gate, sems_up, sems_in, sem_w,
+    x, gy, keep, gain1, gain2, qkv_w, out_w, gate_w, up_w, down_w,
+    w_out, gy_out, grads_out, hid_out, a, qkv, ob, x1, db_rows, z_rows,
+    own_w, w, gy_pos, b_pos, send, stage, down, gy_all, b_all, pair, rows_g, rows_b,
+    db_sib, db_rx, z_sib, z_rx,
+    sems_w, sems_gy, sems_b, sems_swap, sems_in, sems_out, sems_grads, sems_down,
+    sems_db, sems_db_home, sems_z, sems_z_home,
 ):
     d = x.shape[1]
-    each = own_w.shape[0]
+    each = own_w.shape[1]
     lp = npos // nz
+    lrows = lp * fr
+    width = send.shape[4]
+    f, z = place()
     greet(nf, nz, True)
-    own_w[:, : 3 * d] = qkv_w[...].astype(BF)
-    own_w[:, 3 * d :] = out_w[...].astype(BF)
-    weights = Gather(nf, nz, lambda zz: own_w, by_row(w, each, nz), sems_w)
+    for i in range(3):
+        own_w[i] = qkv_w[:, i * d : (i + 1) * d].astype(BF)
+    own_w[3] = out_w[...].astype(BF)
+
+    def w_at(ff, zz):
+        return w.at[:, pl.ds(pl.multiple_of((ff * nz + zz) * each, each), each)]
+
+    def pos_rows(ref):
+        return lambda zz: ref.at[pl.ds(pl.multiple_of(zz * lrows, lrows), lrows)]
+
+    weights = Gather(nf, nz, lambda zz: own_w, w_at, sems_w)
     weights.begin()
-    turn = by_position(npos * fr, npos, fr)
     kept = (gy[...].astype(F32) * keep[...]).astype(BF)
-    gy_pos[...] = nn(turn, kept).astype(BF).reshape(gy_pos.shape)
-    grads = Gather(nf, nz, lambda zz: gy_pos.at[zz], lambda ff, zz: gy_all.at[ff, zz], sems_gy)
-    pack(gate_w, stage, sems_in, send, 0)
+    gy_pos[...] = nn(by_position(npos * fr, npos, fr), kept).astype(BF)
+    grads = Gather(nf, nz, pos_rows(gy_pos), by_row(gy_all, lrows, nz), sems_gy)
+    masters = (gate_w, up_w)
+
+    def pair_at(p):
+        def at(ff):
+            return pair.at[:, p, :, pl.ds(pl.multiple_of(ff * width, width), width)]
+
+        return at
+
+    def send_at(p):
+        return lambda ff: send.at[ff, :, p]
+
+    swaps = [Swap(nf, send_at(p), pair_at(p), sems_swap.at[p]) for p in range(lp)]
+    half = lp // 2
+    for p in range(half):
+        pack(masters, stage, sems_in, send, p)
     for k in range(1, nz):
         weights.along(k)
     for k in range(nz):
         weights.over(relay_of(k), k)
     grads.begin()
-    pack(up_w, stage, sems_in, send, 1)
+    for p in range(half, lp):
+        pack(masters, stage, sems_in, send, p)
     for k in range(nz):
         for m in weights.order(k)[1:]:
             weights.over(m, k)
     for k in range(1, nz):
         grads.along(k)
-    gate = Swap(nf, lambda ff: send.at[ff, 0], lambda ff: pair_all.at[ff, 0], sems_gate)
-    up = Swap(nf, lambda ff: send.at[ff, 1], lambda ff: pair_all.at[ff, 1], sems_up)
-    gate.start()
+    for p in range(half):
+        swaps[p].start()
     for k in range(nz):
         grads.over(relay_of(k), k)
     weights.finish()
-    save = pltpu.make_async_copy(w, w_out, sem_w)
-    save.start()
+    save_w = pltpu.make_async_copy(w, w_out, sems_out.at[0])
+    save_w.start()
     attention_fwd(npos, fr, x, gain1, gain2, w, a, qkv, ob, x1, b_pos)
-    rows = Gather(nf, nz, lambda zz: b_pos.at[pl.ds(pl.multiple_of(zz * lp * fr, lp * fr), lp * fr)], lambda ff, zz: b_all.at[ff, zz], sems_b)
+    rows = Gather(nf, nz, pos_rows(b_pos), by_row(b_all, lrows, nz), sems_b)
     rows.begin()
     for k in range(nz):
         for m in grads.order(k)[1:]:
@@ -580,133 +668,118 @@
         rows.along(k)
     for k in range(nz):
         rows.over(relay_of(k), k)
-    up.start()
+    for p in range(half, lp):
+        swaps[p].start()
     for k in range(nz):
         for m in rows.order(k)[1:]:
             rows.over(m, k)
-    save.wait()
+    grads.finish()
+    save_gy = pltpu.make_async_copy(gy_all, gy_out, sems_out.at[1])
+    save_gy.start()
+    save_w.wait()
     rows.finish()
-    grads.finish()
-    gate.finish()
-    up.finish()
-
-
-def feed_kernel(gy, b, pair, down, db, z, grads, down_grad, wg, wu):
-    nf = pair.shape[0]
-    width = pair.shape[4]
-    rows, d = gy.shape[0] * gy.shape[1] * gy.shape[2], gy.shape[3]
-    for s in range(nf):
-        wg[:, s * width : (s + 1) * width] = pair[s, 0, 0]
-        wu[:, s * width : (s + 1) * width] = pair[s, 1, 0]
-    b_rows = b[...].reshape(rows, d)
-    gy_rows = gy[...].reshape(rows, d)
-    wd = down[0].astype(BF)
-    gate = nt(wg[...], b_rows)
-    up = nt(wu[...], b_rows)
-    dhid = nt(wd, gy_rows)
-    s = jax.nn.sigmoid(gate)
-    silu = gate * s
-    hid = (silu * up).astype(BF)
-    dgate = (dhid * up * s * (1.0 + gate * (1.0 - s))).astype(BF)
-    dup = (dhid * silu).astype(BF)
-    for at, term in enumerate((dgate, dup)):
-        grad = nn(term, b_rows).astype(BF)
-        for j in range(nf):
-            grads[j, at, 0] = grad[:, j * width : (j + 1) * width]
-    down_grad[0] = nn(hid, gy_rows)
-    db[...] = (tn(dgate, wg[...]) + tn(dup, wu[...])).astype(BF).reshape(db.shape)
-    z[...] = tn(hid, wd).astype(BF).reshape(z.shape)
-
-
-def backward_kernel(
+
+    count = rows_b.shape[0]
+    share = count // nf
+
+    def term_at(first, p):
+        per = d // count
+        return w.at[first + p // per, pl.ds((p % per) * count, count)]
+
+    def part_at(first):
+        def at(ff, p):
+            return term_at(first, p).at[pl.ds(pl.multiple_of(ff * share, share), share)]
+
+        return at
+
+    def sums(first, sib, rx, sems, home_sems, land):
+        at = part_at(first)
+        return RowScatter(
+            nf, nz, at, lambda p, m: at(flip(f, 2 * m), p), sib, rx, sems, home_sems, land, fr
+        )
+
+    s_db = sums(0, db_sib, db_rx, sems_db, sems_db_home, db_rows)
+    s_z = sums(2, z_sib, z_rx, sems_z, sems_z_home, z_rows)
+
+    def fetch(p):
+        return pltpu.make_async_copy(down_w.at[p], down.at[p % 2], sems_down.at[p % 2])
+
+    saves = []
+    fetch(0).start()
+    for p in range(lp):
+        if p + 1 < lp:
+            fetch(p + 1).start()
+        fetch(p).wait()
+        wd = down[p % 2].astype(BF)
+        swaps[p].finish()
+        feed(
+            p, fr, gy_all, b_all, pair, wd, rows_g, rows_b, hid_out, send,
+            term_at(0, p), term_at(2, p),
+        )
+        saves.append(
+            pltpu.make_async_copy(send.at[:, :, p], grads_out.at[:, :, p], sems_grads.at[p])
+        )
+        saves[-1].start()
+        s_db.pairs(p)
+        if p >= 1:
+            s_db.chips(p - 1)
+        s_z.pairs(p)
+        if p >= 2:
+            s_db.across(p - 2)
+        if p >= 3:
+            s_db.home(p - 3)
+            s_z.chips(p - 3)
+    for step, last in ((s_db.chips, 1), (s_db.across, 2), (s_db.home, 3), (s_z.chips, 3)):
+        for p in range(max(lp - last, 0), lp):
+            step(p)
+    for step in (s_z.across, s_z.home, s_db.landed, s_z.landed):
+        for p in range(lp):
+            step(p)
+    save_gy.wait()
+    for copy in saves:
+        copy.wait()
+    s_db.finish()
+    s_z.finish()
+
+
+def behind_kernel(
     nf, nz, npos, fr,
-    db_terms, z_terms, grads, w_in, x, gy, keep, gain1, gain2, x1, a, qkv, ob,
+    grads, w_in, x, gy, keep, gain1, gain2, x1, a, qkv, ob, db_rows, z_rows,
     block_out, rows_grad, total, pair_all,
-    db_own, db_sib, db_rx, db_land, db_sems,
-    z_own, z_sib, z_rx, z_land, z_sems,
-    t_sib, t_rx, t_land, t_sems,
-    sems_gate, sems_up, sems_own, sem_w,
-    w, terms, db_rows, z_rows, dx1, dxb, do, dqkv,
+    t_sib, t_rx, t_land, t_sems, sems_swap, sem_w,
+    w, terms, dx1, dxb, do, dqkv,
 ):
-    d = x.shape[1]
     each = total.shape[0]
-    lrows = db_own.shape[2]
-    nc = nf // 2
+    lp = npos // nz
     f, z = place()
+    load_w = pltpu.make_async_copy(w_in, w, sem_w)
+    load_w.start()
     greet(nf, nz, True)
     backward = range(nz - 1, -1, -1)
 
-    def own_copies(src, own, at):
-        return [
-            pltpu.make_async_copy(
-                src.at[flip(f, 2 * m), flip(z, k)], own.at[k, m], sems_own.at[at, k, m]
-            )
-            for k in backward
-            for m in range(nc)
-        ]
-
-    def scatter(src, own, sib, rx, land, sems):
-        return Scatter(
-            nf, nz, lambda ff, zz: src.at[ff, zz], lambda k, m: own.at[k, m], sib, rx, land, sems
-        )
-
-    s_db = scatter(db_terms, db_own, db_sib, db_rx, db_land, db_sems)
-    s_z = scatter(z_terms, z_own, z_sib, z_rx, z_land, z_sems)
-    for k in backward:
-        s_db.pairs(k)
-    load_db = own_copies(db_terms, db_own, 0)
-    load_z = own_copies(z_terms, z_own, 1)
-    for copy in load_db:
-        copy.start()
-    load_w = pltpu.make_async_copy(w_in, w, sem_w)
-    load_w.start()
-    for copy in load_db:
-        copy.wait()
-    for k in backward:
-        s_db.chips(k)
-    for k in backward:
-        s_z.pairs(k)
-    for copy in load_z:
-        copy.start()
-    for k in backward:
-        s_db.across(k)
-
-    def at_pos(zz):
-        return pl.ds(pl.multiple_of(zz * lrows, lrows), lrows)
-
-    for k in backward:
-        s_db.home(k, db_rows.at[at_pos(z)])
-    gate = Swap(nf, lambda ff: grads.at[ff, 0], lambda ff: pair_all.at[ff, 0], sems_gate)
-    up = Swap(nf, lambda ff: grads.at[ff, 1], lambda ff: pair_all.at[ff, 1], sems_up)
-    for copy in load_z:
-        copy.wait()
-    for k in backward:
-        s_z.chips(k)
-    gate.start()
-    for k in range(1, nz):
-        s_db.landed(k)
-        db_rows[at_pos(flip(z, k)), :] = db_land[k - 1]
+    def part(ref, p):
+        return lambda ff: ref.at[ff, :, p]
+
+    swaps = [Swap(nf, part(grads, p), part(pair_all, p), sems_swap.at[p]) for p in range(lp)]
+    for swap in swaps:
+        swap.start()
     load_w.wait()
     gain2_grad = attention_bwd_in(npos, fr, db_rows, gy, keep, x1, ob, w, gain2, dx1, dxb, do, terms)
-    for k in backward:
-        s_z.across(k)
-    up.start()
     attention_bwd_heads(npos, qkv, do, dqkv)
-    for k in backward:
-        s_z.home(k, z_rows.at[at_pos(z)])
     attention_bwd_weights(a, dqkv, terms)
     gain1_grad = attention_bwd_rows(x, dqkv, w, gain1, dx1, rows_grad)
     gains_into(gain1_grad, gain2_grad, terms)
     src_at = by_row(terms, each, nz)
     s_t = Scatter(
-        nf, nz, src_at, lambda k, m: src_at(flip(f, 2 * m), flip(z, k)), t_sib, t_rx, t_land, t_sems
+        nf,
+        nz,
+        lambda ff, k: src_at(ff, flip(z, k)),
+        lambda k, m: src_at(flip(f, 2 * m), flip(z, k)),
+        t_sib, t_rx, t_sems, t_land,
     )
     for step in (s_t.pairs, s_t.chips):
         for k in backward:
             step(k)
-    for k in range(1, nz):
-        s_z.landed(k)
-        z_rows[at_pos(flip(z, k)), :] = z_land[k - 1]
     back = nn(by_position(npos * fr, npos, fr, True), z_rows[...])
     block_out[...] = (keep[...] * (x1[...] + back)).astype(BF)
     for step in (s_t.across, lambda k: s_t.home(k, total)):
@@ -715,14 +788,24 @@
     for k in range(1, nz):
         s_t.landed(k)
         add_into(total, total, t_land.at[k - 1])
-    for task in (s_db, s_z, s_t, gate, up):
-        task.finish()
-
-
-def unpack_kernel(pair, gate, up):
+    s_t.finish()
+    for swap in swaps:
+        swap.finish()
+
+
+def last_local_kernel(pair, hid, gy, total, gate, up, down, qkv_grad, out_grad, gains):
     nf, _, _, ffs, width = pair.shape
+    d = gy.shape[3]
+
+    @pl.when(pl.program_id(0) == 0)
+    def _():
+        qkv_grad[...] = total[:, : 3 * d]
+        out_grad[...] = total[:, 3 * d : 4 * d]
+        gains[...] = total[:, 4 * d :]
+
     for at, out in enumerate((gate, up)):
         out[0] = pair[:, at, 0].astype(F32).reshape(nf * ffs, width).T
+    down[0] = nn(hid[0], gy[...].reshape(hid.shape[2], d))
 
 
 def rms_norm(values, gain_vector):
@@ -926,114 +1009,134 @@
     fr, npos, d = frame_rows.shape
     rows = fr * npos
     each = qkv_master.shape[0]
+    count = nf * nz * fr
 
     def make(shape, kind=BF):
         return jax.ShapeDtypeStruct(shape, kind)
+
+    def vmem(shape, kind=BF):
+        return pltpu.VMEM(shape, kind)
+
+    def dma(*shape):
+        return pltpu.SemaphoreType.DMA(shape)
 
     x = frame_rows.reshape(rows, d)
     gy = out_cotangent.reshape(rows, d)
     keep = jnp.broadcast_to(frame_mask.astype(F32)[:, None], (fr, npos)).reshape(rows, 1)
     gain1 = gain_attention.reshape(1, d)
     gain2 = gain_feed.reshape(1, d)
-    gather_sems = pltpu.SemaphoreType.DMA(Gather.sem_shape(nf, nz))
-    swap_sems = pltpu.SemaphoreType.DMA(Swap.sem_shape(nf))
-    rows_shape = make((nf, nz, lp * fr, d))
-    pair_shape = make((nf, 2, lp, ffs, dslice))
-    w_all, gy_all, b_all, pair_all, a, qkv, ob, x1 = call(
-        functools.partial(forward_kernel, nf, nz, npos, fr),
+    gather_sems = dma(*Gather.sem_shape(nf, nz))
+    swap_sems = dma(lp, *Swap.sem_shape(nf))
+    pair_shape = (nf, 2, lp, ffs, dslice)
+    row_scratch = RowScatter.scratch(nf, nz, lp, nz * fr, d)
+    w_all, gy_all, grads, hid, a, qkv, ob, x1, db_rows, z_rows = call(
+        functools.partial(ahead_kernel, nf, nz, npos, fr),
         0,
         out_shape=(
-            make((d, 4 * d)),
-            rows_shape,
-            rows_shape,
-            pair_shape,
+            make((4, d, d)),
+            make((lp * count, d)),
+            make(pair_shape),
+            make((lp, ffs, count)),
             make((rows, d)),
             make((rows, 3 * d)),
             make((rows, d)),
             make((rows, d), F32),
+            make((rows, d)),
+            make((rows, d)),
         ),
-        in_specs=[VM] * 7 + [ANY] * 2,
-        out_specs=(ANY,) * 4 + (VM,) * 4,
+        in_specs=[VM] * 7 + [ANY] * 3,
+        out_specs=(ANY,) * 3 + (VM,) * 7,
         scratch_shapes=[
-            pltpu.VMEM((each, 4 * d), BF),
-            pltpu.VMEM((d, 4 * d), BF),
-            pltpu.VMEM((nz, lp * fr, d), BF),
-            pltpu.VMEM((rows, d), BF),
-            pltpu.VMEM(pair_shape.shape, BF),
-            pltpu.VMEM((2, dslice, ff), F32),
+            vmem((4, each, d)),
+            vmem((4, d, d)),
+            vmem((rows, d)),
+            vmem((rows, d)),
+            vmem(pair_shape),
+            vmem((2, dslice, ff), F32),
+            vmem((2, ffs, d), F32),
+            vmem((lp * count, d)),
+            vmem((lp * count, d)),
+            vmem((2, lp, ffs, d)),
+            vmem((count, d)),
+            vmem((count, d)),
+            *row_scratch[:2],
+            *row_scratch[:2],
             gather_sems,
             gather_sems,
             gather_sems,
             swap_sems,
-            swap_sems,
-            pltpu.SemaphoreType.DMA((2,)),
-            pltpu.SemaphoreType.DMA,
+            dma(2),
+            dma(2),
+            dma(lp),
+            dma(2),
+            *row_scratch[2:],
+            *row_scratch[2:],
         ],
-    )(x, gy, keep, gain1, gain2, qkv_master, out_master, gate_master, up_master)
-    rows_block = pl.BlockSpec((nf, nz, fr, d), lambda p: (0, 0, p, 0))
-    pair_block = pl.BlockSpec((nf, 2, 1, ffs, dslice), lambda p: (0, 0, p, 0, 0))
-    down_block = pl.BlockSpec((1, ffs, d), lambda p: (p, 0, 0))
-    local_params = pltpu.CompilerParams(vmem_limit_bytes=56 * 2**20)
-    db_terms, z_terms, grads, down_grad = pl.pallas_call(
-        feed_kernel,
-        grid=(lp,),
-        out_shape=(rows_shape, rows_shape, pair_shape, make((lp, ffs, d), F32)),
-        in_specs=[rows_block, rows_block, pair_block, down_block],
-        out_specs=(rows_block, rows_block, pair_block, down_block),
-        scratch_shapes=[pltpu.VMEM((ffs, d), BF)] * 2,
-        compiler_params=local_params,
-    )(gy_all, b_all, pair_all, down_master)
-    small = (nf, nz, lp * fr, d)
+    )(x, gy, keep, gain1, gain2, qkv_master, out_master, gate_master, up_master, down_master)
     wide = 4 * d + 128
-    own = pltpu.VMEM((nz, nf // 2, lp * fr, d), BF)
     block_out, rows_grad, total, back = call(
-        functools.partial(backward_kernel, nf, nz, npos, fr),
+        functools.partial(behind_kernel, nf, nz, npos, fr),
         1,
         out_shape=(
             make((rows, d)),
             make((rows, d), F32),
             make((each, wide), F32),
-            pair_shape,
+            make(pair_shape),
         ),
-        in_specs=[ANY] * 4 + [VM] * 9,
+        in_specs=[ANY] * 2 + [VM] * 11,
         out_specs=(VM,) * 3 + (ANY,),
         scratch_shapes=[
-            own,
-            *Scatter.scratch(*small),
-            own,
-            *Scatter.scratch(*small),
             *Scatter.scratch(nf, nz, each, wide),
             swap_sems,
-            swap_sems,
-            pltpu.SemaphoreType.DMA((2, nz, nf // 2)),
             pltpu.SemaphoreType.DMA,
-            pltpu.VMEM((d, 4 * d), BF),
-            pltpu.VMEM((d, wide), BF),
-            pltpu.VMEM((rows, d), BF),
-            pltpu.VMEM((rows, d), BF),
-            pltpu.VMEM((rows, d), F32),
-            pltpu.VMEM((rows, d), BF),
-            pltpu.VMEM((rows, d), BF),
-            pltpu.VMEM((rows, 3 * d), BF),
+            vmem((4, d, d)),
+            vmem((d, wide)),
+            vmem((rows, d), F32),
+            vmem((rows, d)),
+            vmem((rows, d)),
+            vmem((rows, 3 * d)),
         ],
-    )(db_terms, z_terms, grads, w_all, x, gy, keep, gain1, gain2, x1, a, qkv, ob)
+    )(grads, w_all, x, gy, keep, gain1, gain2, x1, a, qkv, ob, db_rows, z_rows)
     whole_block = pl.BlockSpec((1, dslice, ff), lambda p: (p, 0, 0))
-    gate_grad, up_grad = pl.pallas_call(
-        unpack_kernel,
+
+    def once(*shape):
+        return pl.BlockSpec(shape, lambda p: (0, 0))
+
+    gate_grad, up_grad, down_grad, qkv_grad, out_grad, gains = pl.pallas_call(
+        last_local_kernel,
         grid=(lp,),
-        out_shape=(make((lp, dslice, ff), F32),) * 2,
-        in_specs=[pair_block],
-        out_specs=(whole_block, whole_block),
-        compiler_params=local_params,
-    )(back)
-    gains = total[:, 4 * d : 4 * d + 2] + total[:, 4 * d + 2 : 4 * d + 4]
+        out_shape=(
+            make((lp, dslice, ff), F32),
+            make((lp, dslice, ff), F32),
+            make((lp, ffs, d), F32),
+            make((each, 3 * d), F32),
+            make((each, d), F32),
+            make((each, 128), F32),
+        ),
+        in_specs=[
+            pl.BlockSpec((nf, 2, 1, ffs, dslice), lambda p: (0, 0, p, 0, 0)),
+            pl.BlockSpec((1, ffs, count), lambda p: (p, 0, 0)),
+            pl.BlockSpec((nf, nz, fr, d), lambda p: (0, 0, p, 0)),
+            once(each, wide),
+        ],
+        out_specs=(
+            whole_block,
+            whole_block,
+            pl.BlockSpec((1, ffs, d), lambda p: (p, 0, 0)),
+            once(each, 3 * d),
+            once(each, d),
+            once(each, 128),
+        ),
+        compiler_params=pltpu.CompilerParams(vmem_limit_bytes=48 * 2**20),
+    )(back, hid, gy_all.reshape(nf, nz, lp * fr, d), total)
+    gains = gains[:, :2] + gains[:, 2:4]
     return (
         block_out.reshape(fr, npos, d),
         rows_grad.reshape(fr, npos, d),
         gains[:, 0],
         gains[:, 1],
-        total[:, : 3 * d],
-        total[:, 3 * d : 4 * d],
+        qkv_grad,
+        out_grad,
         gate_grad,
         up_grad,
         down_grad,

time: 352 us -> 342 us (0.972)
  Pallas kernels: 342 us -> 333 us
    pallas_call x4 -> x3, Pallas kernels: 342 us -> 333 us  [the longest x1 197 us: local_fused(): call(functools.partial(ahead_kernel, nf, nz, npos, fr), 0, out_shape=(mak...]
where the time goes in v4:
time: 342 us; the launch traced here: 341 us
  Pallas kernels  333 us (97%)
  local copies, waits for them, and re-layouts  6.54 us (2%)
    pallas_call x1, Pallas kernels, local_fused(): call(functools.partial(ahead_kernel, nf, nz, npos, fr), 0, out_shape=(mak...  197 us
    pallas_call x1, Pallas kernels, local_fused(): call(functools.partial(behind_kernel, nf, nz, npos, fr), 1, out_shape=(ma...  127 us
    pallas_call x1, Pallas kernels, local_fused(): pl.pallas_call(last_local_kernel, grid=(lp,), out_shape=(make((lp, dslice...  8.95 us

profile of v4, /device:TPU:0, one launch (start us, length us, event | category | flops | bytes accessed | tf_op | source)
XLA Modules:
  0.0 341.4 jit_solution(6301642468889282284)
XLA Ops:
  0.6 0.7 convert_element_type.3
  1.3 0.1 broadcast_in_dim.2
  1.4 0.8 reshape.51.keep
  2.1 197.3 %shard_map.169 = (bf16[4,1024,1024]{2,1,0:T(8,128)(2,1)}, bf16[2048,1024]{1,0:T(8,128)(2,1)}, bf16[8,2,4,352,128]{4,3,2,1,0:T(8,128)(2,1)}, bf16[4,352,512]{2,1,...) custom-call(bf16[256,1024]{1,0:T(8,128)(2,1)} %bitcast.8, ...), custom_call_target="tpu_custom_call" | custom-call | tf_op jit(solution)/shard_map/pallas_call | solution.py:1032
  199.4 0.0 copy-start.1
  199.5 127.2 %shard_map.170 = (bf16[256,1024]{1,0:T(8,128)(2,1)}, f32[256,1024]{1,0:T(8,128)}, f32[32,4224]{1,0:T(8,128)}, bf16[8,2,4,352,128]{4,3,2,1,0:T(8,128)(2,1)}) custom-call(bf16[8,2,4,352,128]{4,3,2,1,0:T(8,128)(2,1)} %get-tuple-element.29.grads, bf16[4,1024,1024]{2,1,0:T(8,128)(2,1)} %get-tuple-element.30.w_in, bf16[256,1024]{1,0:T(8,128)(2,1)} %bitcast.9, ...), custom_call_target="tpu_custom_call" | custom-call | tf_op jit(solution)/shard_map/pallas_call | solution.py:1077
  326.7 0.0 copy-done.1
  326.7 0.0 copy-start
  326.7 2.2 copy-done
  328.9 0.0 copy-start.2
  328.9 1.0 copy-done.2
  329.9 0.0 copy-start.4
  329.9 0.0 copy-start.3
  329.9 9.0 %shard_map.171 = (f32[4,128,2816]{2,1,0:T(8,128)}, f32[4,128,2816]{2,1,0:T(8,128)}, f32[4,352,1024]{2,1,0:T(8,128)}, f32[32,3072]{1,0:T(8,128)}, f32[32,1024]{1,0:T(8,128)}, /*index=5*/f32[32,128]{1,0:T(8,128)S(1)}) custom-call(bf16[8,2,4,352,128]{4,3,2,1,0:T(8,128)(2,1)} %get-tuple-element.39.pair, bf16[4,352,512]{2,1,0:T(8,128)(2,1)S(1)} %copy-done.1, ...), custom_call_target="tpu_custom_call" | custom-call | tf_op jit(solution)/shard_map/pallas_call | solution.py:1105
  338.9 0.1 slice_add_fusion
  339.0 0.7 slice_reduce_fusion
  339.7 0.0 copy-done.4
  339.7 0.8 copy.23
  340.5 0.0 copy-done.3
  340.5 1.0 copy.24
Async XLA Ops:
  199.4 127.2 %copy-start.1 = (bf16[4,352,512]{2,1,0:T(8,128)(2,1)S(1)}, bf16[4,352,512]{2,1,0:T(8,128)(2,1)}, u32[]{:S(2)}) copy-start(bf16[4,352,512]{2,1,0:T(8,128)(2,1)} %get-tuple-element.40.hid) | copy-start | bytes 4325380
  326.7 2.2 copy-start
  328.9 1.0 copy-start.2
  329.9 9.7 %copy-start.4 = (bf16[256,1024]{1,0:T(8,128)(2,1)S(1)}, bf16[256,1024]{1,0:T(8,128)(2,1)}, u32[]{:S(2)}) copy-start(bf16[256,1024]{1,0:T(8,128)(2,1)} %get-tuple-element.37) | copy-start | bytes 1572868
  329.9 10.5 %copy-start.3 = (f32[256,1024]{1,0:T(8,128)S(1)}, f32[256,1024]{1,0:T(8,128)}, u32[]{:S(2)}) copy-start(f32[256,1024]{1,0:T(8,128)} %get-tuple-element.38) | copy-start | bytes 3145732

commit v5 on v4

--- a/solution.py
+++ b/solution.py
@@ -50,75 +50,86 @@
     return copy
 
 
+def arrival(dst, send, recv):
+    f, z = place()
+    pltpu.make_async_remote_copy(
+        src_ref=dst,
+        dst_ref=dst,
+        send_sem=send,
+        recv_sem=recv,
+        device_id=(flip(f, 1), z),
+        device_id_type=MESH,
+    ).wait_recv()
+
+
 def relay_of(k):
     return 1 if k % 2 == 0 else 2
 
 
 class Gather:
-    def __init__(self, nf, nz, src_for, out_at, sems):
+    def __init__(self, nf, nz, src_for, out_at, group_at, sems):
         self.nf, self.nz, self.nc = nf, nz, nf // 2
         self.f, self.z = place()
-        self.src_for, self.out_at, self.sems = src_for, out_at, sems
+        self.src_for, self.out_at, self.group_at, self.sems = src_for, out_at, group_at, sems
         self.sent = []
+        self.own = {}
         self.tree = self.nc == 4
 
     @staticmethod
-    def sem_shape(nf, nz):
-        return (2, 1 + 2 * (nf // 2), nz)
-
-    def push(self, src, dst, hop, k, to):
-        self.sent.append(remote(src, dst, self.sems.at[0, hop, k], self.sems.at[1, hop, k], to))
-
-    def arrive(self, dst, hop, k):
-        pltpu.make_async_remote_copy(
-            src_ref=dst,
-            dst_ref=dst,
-            send_sem=self.sems.at[0, hop, k],
-            recv_sem=self.sems.at[1, hop, k],
-            device_id=(flip(self.f, 1), self.z),
-            device_id_type=MESH,
-        ).wait_recv()
-
-    def begin(self):
+    def sem_shape(nf, nz, parts=1):
+        return (2, nz + nf, parts)
+
+    def push(self, src, dst, hop, c, to):
+        self.sent.append(remote(src, dst, self.sems.at[0, hop, c], self.sems.at[1, hop, c], to))
+
+    def arrive(self, dst, hop, c):
+        arrival(dst, self.sems.at[0, hop, c], self.sems.at[1, hop, c])
+
+    def near(self, m, c):
+        return self.group_at(flip(self.f, 2 * m), c)
+
+    def begin(self, c=0):
         f, z = self.f, self.z
+        for k in range(self.nz - 1, 0, -1):
+            self.push(self.src_for(flip(z, k), c), self.out_at(f, z, c), k, c, (f, flip(z, k)))
+        src, dst = self.src_for(z, c), self.out_at(f, z, c)
+        self.own[c] = pltpu.make_async_copy(src, dst, self.sems.at[0, 0, c])
+        self.own[c].start()
+
+    def along(self, c=0):
+        f, z = self.f, self.z
+        self.own[c].wait()
         for k in range(1, self.nz):
-            self.push(self.src_for(flip(z, k)), self.out_at(f, z), 0, k, (f, flip(z, k)))
-        self.own = pltpu.make_async_copy(self.src_for(z), self.out_at(f, z), self.sems.at[0, 0, 0])
-        self.own.start()
-        self.spread(self.src_for(z), 0)
-
-    def spread(self, src, k):
+            self.arrive(self.out_at(f, flip(z, k), c), k, c)
+        group = self.near(0, c)
+        for m in range(1, self.nc):
+            if not (self.tree and m == 3):
+                self.push(group, group, self.nz + m, c, (flip(f, 2 * m), z))
+        self.push(group, group, self.nz + self.nc, c, (flip(f, 1), z))
+
+    def over(self, m, c):
         f, z = self.f, self.z
-        block = self.out_at(f, flip(z, k))
+        group = self.near(m, c)
+        self.arrive(group, self.nz + m, c)
+        if self.tree and m == relay_of(c):
+            self.push(group, group, self.nz + 3, c, (flip(f, 2 * (3 - m)), z))
+        self.push(group, group, self.nz + self.nc + m, c, (flip(f, 1), z))
+
+    def relay(self, c=0):
+        if self.tree:
+            self.over(relay_of(c), c)
+
+    def rest(self, c=0):
         for m in range(1, self.nc):
-            if self.tree and m == 3:
-                continue
-            self.push(src, block, m, k, (flip(f, 2 * m), z))
-        self.push(src, block, self.nc, k, (flip(f, 1), z))
-
-    def along(self, k):
-        block = self.out_at(self.f, flip(self.z, k))
-        self.arrive(block, 0, k)
-        self.spread(block, k)
-
-    def over(self, m, k):
-        f, z = self.f, self.z
-        block = self.out_at(flip(f, 2 * m), flip(z, k))
-        self.arrive(block, m, k)
-        if self.tree and m == relay_of(k):
-            self.push(block, block, 3, k, (flip(f, 2 * (3 - m)), z))
-        self.push(block, block, self.nc + m, k, (flip(f, 1), z))
-
-    def order(self, k):
-        first = relay_of(k) if self.tree else 1
-        return [first] + [m for m in range(1, self.nc) if m != first]
+            if not (self.tree and m == relay_of(c)):
+                self.over(m, c)
+
+    def whole(self, c=0):
+        for m in range(self.nc):
+            group = self.group_at(flip(self.f, 2 * m + 1), c)
+            self.arrive(group, self.nz + self.nc + m, c)
 
     def finish(self):
-        f, z = self.f, self.z
-        for k in range(self.nz):
-            for m in range(self.nc):
-                self.arrive(self.out_at(flip(f, 2 * m + 1), flip(z, k)), self.nc + m, k)
-        self.own.wait()
         for copy in self.sent:
             copy.wait_send()
 
@@ -176,14 +187,7 @@
         self.sent.append(remote(src, dst, sems.at[0, hop, k], sems.at[1, hop, k], to))
 
     def arrive(self, dst, sems, hop, k):
-        pltpu.make_async_remote_copy(
-            src_ref=dst,
-            dst_ref=dst,
-            send_sem=sems.at[0, hop, k],
-            recv_sem=sems.at[1, hop, k],
-            device_id=(flip(self.f, 1), self.z),
-            device_id_type=MESH,
-        ).wait_recv()
+        arrival(dst, sems.at[0, hop, k], sems.at[1, hop, k])
 
     def first(self, k):
         if self.tree:
@@ -233,56 +237,50 @@
             copy.wait_send()
 
 
-class Scatter(Sums):
-    def __init__(self, nf, nz, src_at, own_at, sib, rx, sems, land):
-        super().__init__(nf, nz, src_at, own_at, sib, rx, sems)
-        self.land = land
-
-    @staticmethod
-    def scratch(nf, nz, rows, columns):
-        sib, rx, sems = Sums.buffers(nf, nz, rows, columns)
-        return [sib, rx, pltpu.VMEM((nz - 1, rows, columns), BF), sems]
-
-    def home(self, k, out):
-        if k == 0:
-            self.total(0, out)
-            return
-        sib = self.sib.at[k, 0]
-        self.total(k, sib)
-        self.push(sib, self.land.at[k - 1], self.sems, 0, k, (self.f, flip(self.z, k)))
-
-    def landed(self, k):
-        self.arrive(self.land.at[k - 1], self.sems, 0, k)
-
-
-class RowScatter(Sums):
+class HomeSums(Sums):
     def __init__(self, nf, nz, src_at, own_at, sib, rx, sems, home_sems, land, each):
         super().__init__(nf, nz, src_at, own_at, sib, rx, sems)
         self.home_sems, self.land, self.each = home_sems, land, each
 
     @staticmethod
-    def scratch(nf, nz, lp, rows, columns):
-        sib, rx, sems = Sums.buffers(nf, lp, rows, columns)
-        return [sib, rx, sems, pltpu.SemaphoreType.DMA((2, nz, lp))]
+    def scratch(nf, nz, parts, rows, columns):
+        sib, rx, sems = Sums.buffers(nf, parts, rows, columns)
+        return [sib, rx, sems, pltpu.SemaphoreType.DMA((2, nz, parts))]
 
     def rows_of(self, ref, at):
         return ref.at[pl.ds(pl.multiple_of(at * self.each, self.each), self.each)]
 
     def home(self, p):
-        f, z, lp = self.f, self.z, self.sib.shape[0]
         whole = self.sib.at[p, 0]
         self.total(p, whole)
-        land = self.rows_of(self.land, z * lp + p)
+        for k in range(self.nz - 1, 0, -1):
+            src = self.rows_of(whole, flip(self.z, k))
+            self.push(src, self.sent_to(k, p), self.home_sems, k, p, (self.f, flip(self.z, k)))
+
+
+class RowSums(HomeSums):
+    def at(self, zz, p):
+        return self.rows_of(self.land, zz * self.sib.shape[0] + p)
+
+    def sent_to(self, k, p):
+        return self.at(self.z, p)
+
+    def landed(self, p):
+        self.at(self.z, p)[...] = self.rows_of(self.sib.at[p, 0], self.z)[...]
         for k in range(1, self.nz):
-            src = self.rows_of(whole, flip(z, k))
-            self.push(src, land, self.home_sems, k, p, (f, flip(z, k)))
-        land[...] = self.rows_of(whole, z)[...]
-
-    def landed(self, p):
-        lp = self.sib.shape[0]
+            self.arrive(self.at(flip(self.z, k), p), self.home_sems, k, p)
+
+
+class BlockSums(HomeSums):
+    def sent_to(self, k, p):
+        return self.land.at[p, k - 1]
+
+    def landed(self, p, out):
+        terms = [self.rows_of(self.sib.at[p, 0], self.z)]
         for k in range(1, self.nz):
-            land = self.rows_of(self.land, flip(self.z, k) * lp + p)
-            self.arrive(land, self.home_sems, k, p)
+            self.arrive(self.land.at[p, k - 1], self.home_sems, k, p)
+            terms.append(self.land.at[p, k - 1])
+        add_into(out, *terms)
 
 
 def add_into(out, *terms):
@@ -310,83 +308,58 @@
     )
 
 
-def run_gathers(gathers, nz):
-    for k in range(nz):
-        for g in gathers:
-            if k > 0:
-                g.along(k)
-        for g in gathers:
-            if g.tree and k > 0:
-                g.over(relay_of(k - 1), k - 1)
-    for g in gathers:
-        if g.tree:
-            g.over(relay_of(nz - 1), nz - 1)
-    for k in range(nz):
-        for g in gathers:
-            for m in range(1, g.nc):
-                if g.tree and m == relay_of(k):
-                    continue
-                g.over(m, k)
+def by_block(nf, nz, src_for, out, sems):
+    return Gather(
+        nf, nz, src_for, lambda ff, zz, c: out.at[ff, zz], lambda ff, c: out.at[ff], sems
+    )
 
 
 def first_kernel(nf, nz, attn, gy, pair, attn_all, gy_all, pair_all, s1, s2, s3):
     greet(nf, nz, True)
-    weights = Gather(nf, nz, lambda zz: attn, lambda ff, zz: attn_all.at[ff, zz], s1)
-    rows = Gather(nf, nz, lambda zz: gy.at[zz], lambda ff, zz: gy_all.at[ff, zz], s2)
+    weights = by_block(nf, nz, lambda zz, c: attn, attn_all, s1)
+    rows = by_block(nf, nz, lambda zz, c: gy.at[zz], gy_all, s2)
     swap = Swap(nf, lambda ff: pair.at[ff], lambda ff: pair_all.at[ff], s3)
-    weights.begin()
-    rows.begin()
-    swap.start()
-    run_gathers([weights, rows], nz)
-    weights.finish()
-    rows.finish()
+    gathers = (weights, rows)
+    for g in gathers:
+        g.begin()
+    for step in ("along", "relay", "rest", "whole", "finish"):
+        for g in gathers:
+            getattr(g, step)()
+        if step == "relay":
+            swap.start()
     swap.finish()
 
 
 def rows_kernel(nf, nz, b, b_all, s1):
     greet(nf, nz, False)
-    rows = Gather(nf, nz, lambda zz: b.at[zz], lambda ff, zz: b_all.at[ff, zz], s1)
-    rows.begin()
-    run_gathers([rows], nz)
-    rows.finish()
-
-
-def in_place(terms):
-    f, z = place()
-    return (
-        lambda ff, k: terms.at[ff, flip(z, k)],
-        lambda k, m: terms.at[flip(f, 2 * m), flip(z, k)],
-    )
-
-
-def back_kernel(nf, nz, terms, out, sib, rx, land, sems):
+    rows = by_block(nf, nz, lambda zz, c: b.at[zz], b_all, s1)
+    for step in (rows.begin, rows.along, rows.relay, rows.rest, rows.whole, rows.finish):
+        step()
+
+
+def chip_terms(terms):
+    f, _ = place()
+    return lambda ff, p: terms.at[p, ff], lambda p, m: terms.at[p, flip(f, 2 * m)]
+
+
+def back_kernel(nf, nz, each, terms, out, sib, rx, sems, home_sems):
     greet(nf, nz, False)
-    s = Scatter(nf, nz, *in_place(terms), sib, rx, sems, land)
-    z = s.z
-    backward = range(nz - 1, -1, -1)
-    for step in (s.pairs, s.chips, s.across, lambda k: s.home(k, out.at[z])):
-        for k in backward:
-            step(k)
-    for k in range(1, nz):
-        s.landed(k)
-        out[flip(z, k)] = land[k - 1]
+    s = RowSums(nf, nz, *chip_terms(terms), sib, rx, sems, home_sems, out, each)
+    for step in (s.pairs, s.chips, s.across, s.home, s.landed):
+        for p in range(terms.shape[0]):
+            step(p)
     s.finish()
 
 
-def last_kernel(nf, nz, terms, pair, out, pair_all, sib, rx, land, sems, s2):
+def last_kernel(nf, nz, terms, pair, out, pair_all, sib, rx, sems, home_sems, land, s2):
     greet(nf, nz, True)
-    s = Scatter(nf, nz, *in_place(terms), sib, rx, sems, land)
+    s = BlockSums(nf, nz, *chip_terms(terms), sib, rx, sems, home_sems, land, out.shape[0])
     swap = Swap(nf, lambda ff: pair.at[ff], lambda ff: pair_all.at[ff], s2)
-    backward = range(nz - 1, -1, -1)
-    for k in backward:
-        s.pairs(k)
+    s.pairs(0)
     swap.start()
-    for step in (s.chips, s.across, lambda k: s.home(k, out)):
-        for k in backward:
-            step(k)
-    for k in range(1, nz):
-        s.landed(k)
-        add_into(out, out, land.at[k - 1])
+    for step in (s.chips, s.across, s.home):
+        step(0)
+    s.landed(0, out)
     s.finish()
     swap.finish()
 
@@ -464,7 +437,20 @@
     b_out[...] = nn(by_position(rows, npos, fr), b).astype(BF)
 
 
-def attention_bwd_in(npos, fr, db_pos, gy, keep, x1_ref, ob, w, gain2, dx1_s, dxb, do_s, terms):
+def weight_terms(left, right, first, out):
+    columns = out.shape[1]
+    step = 512
+
+    def body(i, c):
+        at = pl.ds(pl.multiple_of(i * step, step), step)
+        of = pl.ds(pl.multiple_of(first + i * step, step), step)
+        out[:, at] = tn(left[...], right[:, of]).astype(BF)
+        return c
+
+    lax.fori_loop(0, columns // step, body, 0)
+
+
+def attention_bwd_in(npos, fr, db_pos, gy, keep, x1_ref, ob, gain2, dx1_s, dxb, terms):
     rows, d = x1_ref.shape
     db = nn(by_position(rows, npos, fr, True), db_pos[...])
     x1 = x1_ref[...]
@@ -474,16 +460,7 @@
     dx1 = keep[...] * gy[...].astype(F32) + rinv2 * n2 - x1 * (rinv2 * rinv2 * rinv2 * inner)
     dx1_s[...] = dx1
     dxb[...] = dx1.astype(BF)
-    step = 512
-
-    def weights(i, c):
-        at = pl.ds(pl.multiple_of(i * step, step), step)
-        to = pl.ds(pl.multiple_of(3 * d + i * step, step), step)
-        terms[:, to] = tn(ob[...], dxb[:, at]).astype(BF)
-        return c
-
-    lax.fori_loop(0, d // step, weights, 0)
-    do_s[...] = nt(dxb[...], w[3]).astype(BF)
+    weight_terms(ob, dxb, 0, terms.at[3])
     return jnp.sum(db * x1 * rinv2, axis=0, keepdims=True)
 
 
@@ -514,17 +491,6 @@
     lax.fori_loop(0, d // (2 * HD), heads, 0)
 
 
-def attention_bwd_weights(a, dqkv, terms):
-    step = 512
-
-    def weights(i, c):
-        at = pl.ds(pl.multiple_of(i * step, step), step)
-        terms[:, at] = tn(a[...], dqkv[:, at]).astype(BF)
-        return c
-
-    lax.fori_loop(0, dqkv.shape[1] // step, weights, 0)
-
-
 def attention_bwd_rows(x, dqkv, w, gain1, dx1, rows_out):
     d = x.shape[1]
     da = sum(nt(dqkv[:, t * d : (t + 1) * d], w[t]) for t in range(3))
@@ -545,40 +511,37 @@
     tail = jnp.where(at == 1, high2, tail)
     tail = jnp.where(at == 2, gain1_grad - high1, tail)
     tail = jnp.where(at == 3, gain2_grad - high2, tail)
-    terms[:, 4 * d : 4 * d + 128] = tail.T.astype(BF)
-
-
-def by_row(ref, rows, nz):
-    return lambda ff, zz: ref.at[pl.ds(pl.multiple_of((ff * nz + zz) * rows, rows), rows)]
-
-
-def pack(masters, stage, sems, send, p):
-    nf, _, _, ffs, _ = send.shape
-    copies = [
-        pltpu.make_async_copy(master.at[p], stage.at[i], sems.at[i])
-        for i, master in enumerate(masters)
-    ]
-    for copy in copies:
-        copy.start()
-    for i, copy in enumerate(copies):
-        copy.wait()
-        turned = stage[i].T.astype(BF)
-        for j in range(nf):
-            send[j, i, p] = turned[j * ffs : (j + 1) * ffs]
-
-
-def feed(p, fr, gy_all, b_all, pair, wd, rows_g, rows_b, hid_out, grads, db, z):
+    terms[...] = tail.T.astype(BF)
+
+
+class Packer:
+    def __init__(self, masters, stage, sems, send):
+        self.masters, self.stage, self.sems, self.send = masters, stage, sems, send
+
+    def fetch(self, i, p):
+        return pltpu.make_async_copy(self.masters[i].at[p], self.stage.at[i], self.sems.at[i])
+
+    def begin(self):
+        for i in range(len(self.masters)):
+            self.fetch(i, 0).start()
+
+    def pack(self, p):
+        nf, _, lp, ffs, _ = self.send.shape
+        for i in range(len(self.masters)):
+            self.fetch(i, p).wait()
+            turned = self.stage[i].T.astype(BF)
+            for j in range(nf):
+                self.send[j, i, p] = turned[j * ffs : (j + 1) * ffs]
+            if p + 1 < lp:
+                self.fetch(i, p + 1).start()
+
+
+def feed(p, gy_rows, b_rows, pair, wd, hid_out, grads, db, z):
     nf, _, _, _, width = grads.shape
-    count, d = rows_b.shape
-    blocks = count // fr
-    each = b_all.shape[0] // blocks
-    for i in range(blocks):
-        rows_g[i * fr : (i + 1) * fr] = gy_all[i * each + p * fr : i * each + (p + 1) * fr]
-        rows_b[i * fr : (i + 1) * fr] = b_all[i * each + p * fr : i * each + (p + 1) * fr]
-    b_rows = rows_b[...]
-    gate = nt(pair[0, p], b_rows)
-    up = nt(pair[1, p], b_rows)
-    dhid = nt(wd, rows_g[...])
+    b = b_rows[p]
+    gate = nt(pair[0, p], b)
+    up = nt(pair[1, p], b)
+    dhid = nt(wd, gy_rows[p])
     s = jax.nn.sigmoid(gate)
     silu = gate * s
     hid = (silu * up).astype(BF)
@@ -588,7 +551,7 @@
     db[...] = (tn(dgate, pair[0, p]) + tn(dup, pair[1, p])).astype(BF)
     z[...] = tn(hid, wd).astype(BF)
     for at, term in enumerate((dgate, dup)):
-        grad = nn(term, b_rows).astype(BF)
+        grad = nn(term, b).astype(BF)
         for j in range(nf):
             grads[j, at, p] = grad[:, j * width : (j + 1) * width]
 
@@ -597,7 +560,7 @@
     nf, nz, npos, fr,
     x, gy, keep, gain1, gain2, qkv_w, out_w, gate_w, up_w, down_w,
     w_out, gy_out, grads_out, hid_out, a, qkv, ob, x1, db_rows, z_rows,
-    own_w, w, gy_pos, b_pos, send, stage, down, gy_all, b_all, pair, rows_g, rows_b,
+    own_w, w, gy_pos, b_pos, send, stage, down, gy_all, b_all, pair,
     db_sib, db_rx, z_sib, z_rx,
     sems_w, sems_gy, sems_b, sems_swap, sems_in, sems_out, sems_grads, sems_down,
     sems_db, sems_db_home, sems_z, sems_z_home,
@@ -605,96 +568,106 @@
     d = x.shape[1]
     each = own_w.shape[1]
     lp = npos // nz
-    lrows = lp * fr
     width = send.shape[4]
     f, z = place()
+    packer = Packer((gate_w, up_w), stage, sems_in, send)
+    packer.begin()
     greet(nf, nz, True)
     for i in range(3):
         own_w[i] = qkv_w[:, i * d : (i + 1) * d].astype(BF)
     own_w[3] = out_w[...].astype(BF)
 
-    def w_at(ff, zz):
-        return w.at[:, pl.ds(pl.multiple_of((ff * nz + zz) * each, each), each)]
-
-    def pos_rows(ref):
-        return lambda zz: ref.at[pl.ds(pl.multiple_of(zz * lrows, lrows), lrows)]
-
-    weights = Gather(nf, nz, lambda zz: own_w, w_at, sems_w)
-    weights.begin()
+    def span(at, size):
+        return pl.ds(pl.multiple_of(at * size, size), size)
+
+    weights = Gather(
+        nf, nz,
+        lambda zz, c: own_w.at[c],
+        lambda ff, zz, c: w.at[c, span(ff * nz + zz, each)],
+        lambda ff, c: w.at[c, span(ff, nz * each)],
+        sems_w,
+    )
+
+    def rows_gather(mine, every, sems):
+        return Gather(
+            nf, nz,
+            lambda zz, p: mine.at[span(zz * lp + p, fr)],
+            lambda ff, zz, p: every.at[p, span(ff * nz + zz, fr)],
+            lambda ff, p: every.at[p, span(ff, nz * fr)],
+            sems,
+        )
+
+    for c in range(4):
+        weights.begin(c)
     kept = (gy[...].astype(F32) * keep[...]).astype(BF)
     gy_pos[...] = nn(by_position(npos * fr, npos, fr), kept).astype(BF)
-    grads = Gather(nf, nz, pos_rows(gy_pos), by_row(gy_all, lrows, nz), sems_gy)
-    masters = (gate_w, up_w)
+    grads = rows_gather(gy_pos, gy_all, sems_gy)
+    rows = rows_gather(b_pos, b_all, sems_b)
 
     def pair_at(p):
-        def at(ff):
-            return pair.at[:, p, :, pl.ds(pl.multiple_of(ff * width, width), width)]
-
-        return at
+        return lambda ff: pair.at[:, p, :, span(ff, width)]
 
     def send_at(p):
         return lambda ff: send.at[ff, :, p]
 
     swaps = [Swap(nf, send_at(p), pair_at(p), sems_swap.at[p]) for p in range(lp)]
     half = lp // 2
-    for p in range(half):
-        pack(masters, stage, sems_in, send, p)
-    for k in range(1, nz):
-        weights.along(k)
-    for k in range(nz):
-        weights.over(relay_of(k), k)
-    grads.begin()
-    for p in range(half, lp):
-        pack(masters, stage, sems_in, send, p)
-    for k in range(nz):
-        for m in weights.order(k)[1:]:
-            weights.over(m, k)
-    for k in range(1, nz):
-        grads.along(k)
+    for c in range(4):
+        weights.along(c)
+        if c >= 1:
+            weights.relay(c - 1)
+        if c >= 2:
+            weights.rest(c - 2)
+        if c < lp:
+            packer.pack(c)
+    for p in range(lp):
+        grads.begin(p)
+    for p in range(4, lp):
+        packer.pack(p)
+    weights.relay(3)
+    weights.rest(2)
+    for p in range(lp):
+        grads.along(p)
+    weights.rest(3)
     for p in range(half):
         swaps[p].start()
-    for k in range(nz):
-        grads.over(relay_of(k), k)
+    for p in range(lp):
+        grads.relay(p)
+    for c in range(4):
+        weights.whole(c)
     weights.finish()
     save_w = pltpu.make_async_copy(w, w_out, sems_out.at[0])
     save_w.start()
     attention_fwd(npos, fr, x, gain1, gain2, w, a, qkv, ob, x1, b_pos)
-    rows = Gather(nf, nz, pos_rows(b_pos), by_row(b_all, lrows, nz), sems_b)
-    rows.begin()
-    for k in range(nz):
-        for m in grads.order(k)[1:]:
-            grads.over(m, k)
-    for k in range(1, nz):
-        rows.along(k)
-    for k in range(nz):
-        rows.over(relay_of(k), k)
+    for p in range(lp):
+        rows.begin(p)
+    for p in range(lp):
+        grads.rest(p)
+    for p in range(lp):
+        rows.along(p)
+        if p >= 1:
+            rows.relay(p - 1)
+    rows.relay(lp - 1)
     for p in range(half, lp):
         swaps[p].start()
-    for k in range(nz):
-        for m in rows.order(k)[1:]:
-            rows.over(m, k)
+    for p in range(lp):
+        grads.whole(p)
     grads.finish()
     save_gy = pltpu.make_async_copy(gy_all, gy_out, sems_out.at[1])
     save_gy.start()
-    save_w.wait()
-    rows.finish()
-
-    count = rows_b.shape[0]
+
+    count = b_all.shape[1]
     share = count // nf
 
     def term_at(first, p):
         per = d // count
         return w.at[first + p // per, pl.ds((p % per) * count, count)]
 
-    def part_at(first):
+    def sums(first, sib, rx, sems, home_sems, land):
         def at(ff, p):
-            return term_at(first, p).at[pl.ds(pl.multiple_of(ff * share, share), share)]
-
-        return at
-
-    def sums(first, sib, rx, sems, home_sems, land):
-        at = part_at(first)
-        return RowScatter(
+            return term_at(first, p).at[span(ff, share)]
+
+        return RowSums(
             nf, nz, at, lambda p, m: at(flip(f, 2 * m), p), sib, rx, sems, home_sems, land, fr
         )
 
@@ -706,16 +679,17 @@
 
     saves = []
     fetch(0).start()
+    rows.rest(0)
+    save_w.wait()
     for p in range(lp):
         if p + 1 < lp:
             fetch(p + 1).start()
+            rows.rest(p + 1)
         fetch(p).wait()
         wd = down[p % 2].astype(BF)
+        rows.whole(p)
         swaps[p].finish()
-        feed(
-            p, fr, gy_all, b_all, pair, wd, rows_g, rows_b, hid_out, send,
-            term_at(0, p), term_at(2, p),
-        )
+        feed(p, gy_all, b_all, pair, wd, hid_out, send, term_at(0, p), term_at(2, p))
         saves.append(
             pltpu.make_async_copy(send.at[:, :, p], grads_out.at[:, :, p], sems_grads.at[p])
         )
@@ -735,6 +709,7 @@
     for step in (s_z.across, s_z.home, s_db.landed, s_z.landed):
         for p in range(lp):
             step(p)
+    rows.finish()
     save_gy.wait()
     for copy in saves:
         copy.wait()
@@ -745,17 +720,17 @@
 def behind_kernel(
     nf, nz, npos, fr,
     grads, w_in, x, gy, keep, gain1, gain2, x1, a, qkv, ob, db_rows, z_rows,
-    block_out, rows_grad, total, pair_all,
-    t_sib, t_rx, t_land, t_sems, sems_swap, sem_w,
-    w, terms, dx1, dxb, do, dqkv,
+    block_out, rows_grad, total, gains, pair_all,
+    t_sib, t_rx, t_sems, t_home, g_sib, g_rx, g_sems, g_home, t_land, g_land, sems_swap, sem_w,
+    w, terms, tail, dx1, dxb, do, dqkv,
 ):
-    each = total.shape[0]
+    d = x.shape[1]
+    each = gains.shape[0]
     lp = npos // nz
     f, z = place()
     load_w = pltpu.make_async_copy(w_in, w, sem_w)
     load_w.start()
     greet(nf, nz, True)
-    backward = range(nz - 1, -1, -1)
 
     def part(ref, p):
         return lambda ff: ref.at[ff, :, p]
@@ -763,49 +738,74 @@
     swaps = [Swap(nf, part(grads, p), part(pair_all, p), sems_swap.at[p]) for p in range(lp)]
     for swap in swaps:
         swap.start()
+
+    def span(ff):
+        return pl.ds(pl.multiple_of(ff * nz * each, nz * each), nz * each)
+
+    s_t = BlockSums(
+        nf, nz,
+        lambda ff, c: terms.at[c, span(ff)],
+        lambda c, m: terms.at[c, span(flip(f, 2 * m))],
+        t_sib, t_rx, t_sems, t_home, t_land, each,
+    )
+    s_g = BlockSums(
+        nf, nz,
+        lambda ff, c: tail.at[span(ff)],
+        lambda c, m: tail.at[span(flip(f, 2 * m))],
+        g_sib, g_rx, g_sems, g_home, g_land, each,
+    )
+    gain2_grad = attention_bwd_in(npos, fr, db_rows, gy, keep, x1, ob, gain2, dx1, dxb, terms)
+    s_t.pairs(3)
     load_w.wait()
-    gain2_grad = attention_bwd_in(npos, fr, db_rows, gy, keep, x1, ob, w, gain2, dx1, dxb, do, terms)
+    do[...] = nt(dxb[...], w[3]).astype(BF)
+    s_t.chips(3)
     attention_bwd_heads(npos, qkv, do, dqkv)
-    attention_bwd_weights(a, dqkv, terms)
+    s_t.across(3)
+    weight_terms(a, dqkv, 0, terms.at[0])
+    s_t.pairs(0)
+    weight_terms(a, dqkv, d, terms.at[1])
+    s_t.pairs(1)
+    s_t.chips(0)
+    weight_terms(a, dqkv, 2 * d, terms.at[2])
+    s_t.pairs(2)
+    s_t.chips(1)
     gain1_grad = attention_bwd_rows(x, dqkv, w, gain1, dx1, rows_grad)
-    gains_into(gain1_grad, gain2_grad, terms)
-    src_at = by_row(terms, each, nz)
-    s_t = Scatter(
-        nf,
-        nz,
-        lambda ff, k: src_at(ff, flip(z, k)),
-        lambda k, m: src_at(flip(f, 2 * m), flip(z, k)),
-        t_sib, t_rx, t_sems, t_land,
-    )
-    for step in (s_t.pairs, s_t.chips):
-        for k in backward:
-            step(k)
+    gains_into(gain1_grad, gain2_grad, tail)
+    s_g.pairs(0)
+    s_t.chips(2)
+    s_g.chips(0)
+    s_t.home(3)
     back = nn(by_position(npos * fr, npos, fr, True), z_rows[...])
     block_out[...] = (keep[...] * (x1[...] + back)).astype(BF)
-    for step in (s_t.across, lambda k: s_t.home(k, total)):
-        for k in backward:
-            step(k)
-    for k in range(1, nz):
-        s_t.landed(k)
-        add_into(total, total, t_land.at[k - 1])
+    s_t.across(0)
+    s_t.across(1)
+    s_g.across(0)
+    s_t.home(0)
+    s_t.across(2)
+    s_g.home(0)
+    s_t.home(1)
+    s_t.home(2)
+    for c in (3, 0, 1, 2):
+        s_t.landed(c, total.at[:, pl.ds(c * d, d)])
+    s_g.landed(0, gains)
     s_t.finish()
+    s_g.finish()
     for swap in swaps:
         swap.finish()
 
 
-def last_local_kernel(pair, hid, gy, total, gate, up, down, qkv_grad, out_grad, gains):
+def last_local_kernel(pair, hid, gy, total, gate, up, down, qkv_grad, out_grad):
     nf, _, _, ffs, width = pair.shape
-    d = gy.shape[3]
+    d = gy.shape[2]
 
     @pl.when(pl.program_id(0) == 0)
     def _():
         qkv_grad[...] = total[:, : 3 * d]
-        out_grad[...] = total[:, 3 * d : 4 * d]
-        gains[...] = total[:, 4 * d :]
+        out_grad[...] = total[:, 3 * d :]
 
     for at, out in enumerate((gate, up)):
         out[0] = pair[:, at, 0].astype(F32).reshape(nf * ffs, width).T
-    down[0] = nn(hid[0], gy[...].reshape(hid.shape[2], d))
+    down[0] = nn(hid[0], gy[0])
 
 
 def rms_norm(values, gain_vector):
@@ -866,21 +866,19 @@
         return every.transpose(2, 0, 1, 3, 4).reshape(lp, nf * nz * fr, d)
 
     rows_shape = jax.ShapeDtypeStruct((nf, nz, lp * fr, d), BF)
-    back_shape = jax.ShapeDtypeStruct((nz, lp * fr, d), BF)
+    back_shape = jax.ShapeDtypeStruct((npos * fr, d), BF)
     gather_sems = pltpu.SemaphoreType.DMA(Gather.sem_shape(nf, nz))
     swap_sems = pltpu.SemaphoreType.DMA(Swap.sem_shape(nf))
 
     def scattered(rows, ident):
-        moved = rows.reshape(lp, nf, nz, fr, d).transpose(1, 2, 0, 3, 4)
-        moved = moved.reshape(nf, nz, lp * fr, d)
         back = call(
-            functools.partial(back_kernel, nf, nz),
+            functools.partial(back_kernel, nf, nz, fr),
             ident,
             out_shape=back_shape,
             in_specs=[VM],
             out_specs=VM,
-            scratch_shapes=Scatter.scratch(nf, nz, lp * fr, d),
-        )(moved)
+            scratch_shapes=HomeSums.scratch(nf, nz, lp, nz * fr, d),
+        )(rows.reshape(lp, nf, nz * fr, d))
         return back.reshape(npos, fr, d).transpose(1, 0, 2)
 
     both = jnp.concatenate((qkv_master.astype(BF), out_master.astype(BF)), axis=1)
@@ -961,23 +959,27 @@
     gains = jnp.stack((pulled_one[1], pulled_two[1]), axis=1)
     gains_hi = gains.astype(BF)
     gains_lo = (gains - gains_hi.astype(F32)).astype(BF)
-    tail = jnp.concatenate((gains_hi, gains_lo, jnp.zeros((d, 124), BF)), axis=1)
+    unit = max(128, 2048 // own_rows)
+    spare = -(4 * d + 4) % unit
+    tail = jnp.concatenate((gains_hi, gains_lo, jnp.zeros((d, spare), BF)), axis=1)
     total = jnp.concatenate(
         (qkv_weight_grad.astype(BF), out_weight_grad.astype(BF), tail), axis=1
     )
-    total = total.reshape(nf, nz, own_rows, total.shape[1])
+    block = own_rows * total.shape[1] // 128
     total, grads = call(
         functools.partial(last_kernel, nf, nz),
         4,
         out_shape=(
-            jax.ShapeDtypeStruct(total.shape[2:], F32),
+            jax.ShapeDtypeStruct((block, 128), F32),
             jax.ShapeDtypeStruct(grads.shape, BF),
         ),
         in_specs=[VM, ANY],
         out_specs=(VM, ANY),
-        scratch_shapes=Scatter.scratch(nf, nz, *total.shape[2:]) + [swap_sems],
-    )(total, grads)
+        scratch_shapes=HomeSums.scratch(nf, nz, 1, nz * block, 128)
+        + [pltpu.VMEM((1, nz - 1, block, 128), BF), swap_sems],
+    )(total.reshape(1, nf, nz * block, 128), grads)
     grads = grads.transpose(1, 2, 4, 0, 3).reshape(2, lp, dslice, ff).astype(F32)
+    total = total.reshape(own_rows, 4 * d + 4 + spare)
     gain_grads = total[:, 4 * d : 4 * d + 2] + total[:, 4 * d + 2 : 4 * d + 4]
     return (
         block_out,
@@ -1025,16 +1027,17 @@
     keep = jnp.broadcast_to(frame_mask.astype(F32)[:, None], (fr, npos)).reshape(rows, 1)
     gain1 = gain_attention.reshape(1, d)
     gain2 = gain_feed.reshape(1, d)
-    gather_sems = dma(*Gather.sem_shape(nf, nz))
+    gather_sems = dma(*Gather.sem_shape(nf, nz, 4))
+    rows_sems = dma(*Gather.sem_shape(nf, nz, lp))
     swap_sems = dma(lp, *Swap.sem_shape(nf))
     pair_shape = (nf, 2, lp, ffs, dslice)
-    row_scratch = RowScatter.scratch(nf, nz, lp, nz * fr, d)
+    row_scratch = HomeSums.scratch(nf, nz, lp, nz * fr, d)
     w_all, gy_all, grads, hid, a, qkv, ob, x1, db_rows, z_rows = call(
         functools.partial(ahead_kernel, nf, nz, npos, fr),
         0,
         out_shape=(
             make((4, d, d)),
-            make((lp * count, d)),
+            make((lp, count, d)),
             make(pair_shape),
             make((lp, ffs, count)),
             make((rows, d)),
@@ -1054,16 +1057,14 @@
             vmem(pair_shape),
             vmem((2, dslice, ff), F32),
             vmem((2, ffs, d), F32),
-            vmem((lp * count, d)),
-            vmem((lp * count, d)),
+            vmem((lp, count, d)),
+            vmem((lp, count, d)),
             vmem((2, lp, ffs, d)),
-            vmem((count, d)),
-            vmem((count, d)),
             *row_scratch[:2],
             *row_scratch[:2],
             gather_sems,
-            gather_sems,
-            gather_sems,
+            rows_sems,
+            rows_sems,
             swap_sems,
             dma(2),
             dma(2),
@@ -1073,24 +1074,28 @@
             *row_scratch[2:],
         ],
     )(x, gy, keep, gain1, gain2, qkv_master, out_master, gate_master, up_master, down_master)
-    wide = 4 * d + 128
-    block_out, rows_grad, total, back = call(
+    block_out, rows_grad, total, gains, back = call(
         functools.partial(behind_kernel, nf, nz, npos, fr),
         1,
         out_shape=(
             make((rows, d)),
             make((rows, d), F32),
-            make((each, wide), F32),
+            make((each, 4 * d), F32),
+            make((each, 128), F32),
             make(pair_shape),
         ),
         in_specs=[ANY] * 2 + [VM] * 11,
-        out_specs=(VM,) * 3 + (ANY,),
+        out_specs=(VM,) * 4 + (ANY,),
         scratch_shapes=[
-            *Scatter.scratch(nf, nz, each, wide),
+            *HomeSums.scratch(nf, nz, 4, nz * each, d),
+            *HomeSums.scratch(nf, nz, 1, nz * each, 128),
+            vmem((4, nz - 1, each, d)),
+            vmem((1, nz - 1, each, 128)),
             swap_sems,
             pltpu.SemaphoreType.DMA,
             vmem((4, d, d)),
-            vmem((d, wide)),
+            vmem((4, d, d)),
+            vmem((d, 128)),
             vmem((rows, d), F32),
             vmem((rows, d)),
             vmem((rows, d)),
@@ -1102,7 +1107,7 @@
     def once(*shape):
         return pl.BlockSpec(shape, lambda p: (0, 0))
 
-    gate_grad, up_grad, down_grad, qkv_grad, out_grad, gains = pl.pallas_call(
+    gate_grad, up_grad, down_grad, qkv_grad, out_grad = pl.pallas_call(
         last_local_kernel,
         grid=(lp,),
         out_shape=(
@@ -1111,13 +1116,12 @@
             make((lp, ffs, d), F32),
             make((each, 3 * d), F32),
             make((each, d), F32),
-            make((each, 128), F32),
         ),
         in_specs=[
             pl.BlockSpec((nf, 2, 1, ffs, dslice), lambda p: (0, 0, p, 0, 0)),
             pl.BlockSpec((1, ffs, count), lambda p: (p, 0, 0)),
-            pl.BlockSpec((nf, nz, fr, d), lambda p: (0, 0, p, 0)),
-            once(each, wide),
+            pl.BlockSpec((1, count, d), lambda p: (p, 0, 0)),
+            once(each, 4 * d),
         ],
         out_specs=(
             whole_block,
@@ -1125,10 +1129,9 @@
             pl.BlockSpec((1, ffs, d), lambda p: (p, 0, 0)),
             once(each, 3 * d),
             once(each, d),
-            once(each, 128),
         ),
-        compiler_params=pltpu.CompilerParams(vmem_limit_bytes=48 * 2**20),
-    )(back, hid, gy_all.reshape(nf, nz, lp * fr, d), total)
+        compiler_params=pltpu.CompilerParams(vmem_limit_bytes=60 * 2**20),
+    )(back, hid, gy_all, total)
     gains = gains[:, :2] + gains[:, 2:4]
     return (
         block_out.reshape(fr, npos, d),

time: 342 us -> 346 us (1.012)
  Pallas kernels: 333 us -> 341 us
    pallas_call x1, Pallas kernels: 197 us -> 203 us  [local_fused(): call(functools.partial(ahead_kernel, nf, nz, npos, fr), 0, out_shape=(mak...]
where the time goes in v5:
time: 346 us
  Pallas kernels  341 us (99%)
    pallas_call x1, Pallas kernels, local_fused(): call(functools.partial(ahead_kernel, nf, nz, npos, fr), 0, out_shape=(mak...  203 us
    pallas_call x1, Pallas kernels, local_fused(): call(functools.partial(behind_kernel, nf, nz, npos, fr), 1, out_shape=(ma...  126 us
    pallas_call x1, Pallas kernels, local_fused(): pl.pallas_call(last_local_kernel, grid=(lp,), out_shape=(make((lp, dslice...  11.1 us

profile of v5, /device:TPU:0, one launch (start us, length us, event | category | flops | bytes accessed | tf_op | source)
XLA Modules:
  0.0 346.1 jit_solution(83875941800294686)
XLA Ops:
  0.6 0.7 convert_element_type.3
  1.3 0.1 broadcast_in_dim.2
  1.4 0.8 reshape.47.keep
  2.1 203.2 %shard_map.169 = (bf16[4,1024,1024]{2,1,0:T(8,128)(2,1)}, bf16[4,512,1024]{2,1,0:T(8,128)(2,1)}, bf16[8,2,4,352,128]{4,3,2,1,0:T(8,128)(2,1)}, bf16[4,352,512]{2...) custom-call(bf16[256,1024]{1,0:T(8,128)(2,1)} %bitcast.6, ...), custom_call_target="tpu_custom_call" | custom-call | tf_op jit(solution)/shard_map/pallas_call | solution.py:1035
  205.4 126.3 %shard_map.170 = (bf16[256,1024]{1,0:T(8,128)(2,1)}, f32[256,1024]{1,0:T(8,128)}, f32[32,4096]{1,0:T(8,128)}, f32[32,128]{1,0:T(8,128)}, bf16[8,2,4,352,128]{4,3,2,1,0:T(8,128)(2,1)}) custom-call(bf16[8,2,4,352,128]{4,3,2,1,0:T(8,128)(2,1)} %get-tuple-element.29.grads, bf16[4,1024,1024]{2,1,0:T(8,128)(2,1)} %get-tuple-element.30.w_in, ...), custom_call_target="tpu_custom_call" | custom-call | tf_op jit(solution)/shard_map/pallas_call | solution.py:1077
  331.7 0.9 slice_add_fusion
  332.6 0.7 slice_reduce_fusion
  333.3 0.0 copy-start.1
  333.3 0.0 copy-start
  333.3 11.1 %shard_map.171 = (f32[4,128,2816]{2,1,0:T(8,128)}, f32[4,128,2816]{2,1,0:T(8,128)}, f32[4,352,1024]{2,1,0:T(8,128)}, f32[32,3072]{1,0:T(8,128)}, f32[32,1024]{1,0:T(8,128)}) custom-call(bf16[8,2,4,352,128]{4,3,2,1,0:T(8,128)(2,1)} %get-tuple-element.40.pair, bf16[4,352,512]{2,1,0:T(8,128)(2,1)} %get-tuple-element.41.hid, ...), custom_call_target="tpu_custom_call" | custom-call | tf_op jit(solution)/shard_map/pallas_call | solution.py:1110
  344.4 0.0 copy-done.1
  344.4 0.8 copy.23
  345.2 0.0 copy-done
  345.2 1.0 copy.24
Async XLA Ops:
  333.3 11.1 %copy-start.1 = (bf16[256,1024]{1,0:T(8,128)(2,1)S(1)}, bf16[256,1024]{1,0:T(8,128)(2,1)}, u32[]{:S(2)}) copy-start(bf16[256,1024]{1,0:T(8,128)(2,1)} %get-tuple-element.37) | copy-start | bytes 1572868
  333.3 11.9 %copy-start = (f32[256,1024]{1,0:T(8,128)S(1)}, f32[256,1024]{1,0:T(8,128)}, u32[]{:S(2)}) copy-start(f32[256,1024]{1,0:T(8,128)} %get-tuple-element.38) | copy-start | bytes 3145732

commit v6 on v5

--- a/solution.py
+++ b/solution.py
@@ -13,6 +13,12 @@
 BF = jnp.bfloat16
 F32 = jnp.float32
 MESH = pl.DeviceIdType.MESH
+FILL = (10, 6)
+PUMP = (14, 4, 3, 3)
+LATE = (2, 3)
+EARLY = tuple(c for c in range(4) if c not in LATE)
+LATE_W = (2, 3)
+EARLY_W = tuple(c for c in range(4) if c not in LATE_W)
 ANY = pl.BlockSpec(memory_space=pl.ANY)
 VM = pl.BlockSpec(memory_space=pltpu.VMEM)
 
@@ -134,21 +140,73 @@
             copy.wait_send()
 
 
+class LateGather(Gather):
+    def __init__(self, nf, nz, src_for, out_at, group_at, sems, late_sems):
+        super().__init__(nf, nz, src_for, out_at, group_at, sems)
+        self.late_sems = late_sems
+
+    @staticmethod
+    def late_shape(nf, nz, parts):
+        return (2, nz * (nf // 2), parts)
+
+    def block(self, m, k, c):
+        return self.out_at(flip(self.f, 2 * m), flip(self.z, k), c)
+
+    def begin(self, c=0):
+        f, z = self.f, self.z
+        src, dst = self.src_for(z, c), self.out_at(f, z, c)
+        for m in range(1, self.nc):
+            if not (self.tree and m == 3):
+                self.push(src, dst, self.nz + m, c, (flip(f, 2 * m), z))
+        self.own[c] = pltpu.make_async_copy(src, dst, self.sems.at[0, 0, c])
+        self.own[c].start()
+
+    def relay(self, c=0):
+        if self.tree:
+            m = relay_of(c)
+            block = self.block(m, 0, c)
+            self.arrive(block, self.nz + m, c)
+            to = (flip(self.f, 2 * (3 - m)), self.z)
+            self.push(block, block, self.nz + 3, c, to)
+
+    def along(self, c=0):
+        self.own[c].wait()
+        for m in range(1, self.nc):
+            if not (self.tree and m == relay_of(c)):
+                self.arrive(self.block(m, 0, c), self.nz + m, c)
+        for k in range(self.nz - 1, 0, -1):
+            for m in range(self.nc):
+                block, hop = self.block(m, 0, c), k * self.nc + m
+                send, recv = self.late_sems.at[0, hop, c], self.late_sems.at[1, hop, c]
+                self.sent.append(remote(block, block, send, recv, (self.f, flip(self.z, k))))
+
+    def rest(self, c=0):
+        for m in range(self.nc):
+            for k in range(1, self.nz):
+                hop = k * self.nc + m
+                send, recv = self.late_sems.at[0, hop, c], self.late_sems.at[1, hop, c]
+                arrival(self.block(m, k, c), send, recv)
+            group = self.near(m, c)
+            self.push(group, group, self.nz + self.nc + m, c, (flip(self.f, 1), self.z))
+
+
 class Swap:
     def __init__(self, nf, src_at, out_at, sems):
         self.nf, self.src_at, self.out_at, self.sems = nf, src_at, out_at, sems
         self.f, self.z = place()
         self.sent = []
+        self.own = None
 
     @staticmethod
     def sem_shape(nf):
         return (2, nf)
 
-    def start(self):
+    def start(self, masks=None):
         f, z = self.f, self.z
-        self.own = pltpu.make_async_copy(self.src_at(f), self.out_at(f), self.sems.at[0, 0])
-        self.own.start()
-        for m in range(self.nf - 1, 0, -1):
+        if self.own is None:
+            self.own = pltpu.make_async_copy(self.src_at(f), self.out_at(f), self.sems.at[0, 0])
+            self.own.start()
+        for m in masks or range(self.nf - 1, 0, -1):
             self.sent.append(
                 remote(
                     self.src_at(flip(f, m)),
@@ -280,6 +338,76 @@
         for k in range(1, self.nz):
             self.arrive(self.land.at[p, k - 1], self.home_sems, k, p)
             terms.append(self.land.at[p, k - 1])
+        add_into(out, *terms)
+
+
+class PosSums(Sums):
+    def __init__(self, nf, nz, src_at, own_at, sib, rx, sems, late_sems, zl, each):
+        super().__init__(nf, nz, src_at, own_at, sib, rx, sems)
+        self.late_sems, self.zl, self.each = late_sems, zl, each
+
+    @staticmethod
+    def scratch(nf, nz, parts, each, columns):
+        nc = nf // 2
+        return [
+            pltpu.VMEM((parts, nc, nz * each, columns), BF),
+            pltpu.VMEM((parts, nc - 1, each, columns), BF),
+            pltpu.SemaphoreType.DMA((2, 2 * nc, parts)),
+            pltpu.SemaphoreType.DMA((2, nz * nc, parts)),
+            pltpu.VMEM((parts, nc, nz - 1, each, columns), BF),
+        ]
+
+    def rows_of(self, ref, at):
+        return ref.at[pl.ds(pl.multiple_of(at * self.each, self.each), self.each)]
+
+    def order(self, c):
+        first = self.first(c)
+        return first + [m for m in range(self.nc - 1, -1, -1) if m not in first]
+
+    def along(self, c):
+        for m in self.order(c):
+            sib = self.sib.at[c, m]
+            self.arrive(sib, self.sems, self.nc + m, c)
+            add_into(sib, self.own_at(c, m), sib)
+            for k in range(self.nz - 1, 0, -1):
+                src = self.rows_of(sib, flip(self.z, k))
+                to = (self.f, flip(self.z, k))
+                self.push(src, self.zl.at[c, m, k - 1], self.late_sems, k * self.nc + m, c, to)
+
+    def mine(self, m, c):
+        terms = [self.rows_of(self.sib.at[c, m], self.z)]
+        for k in range(1, self.nz):
+            land = self.zl.at[c, m, k - 1]
+            self.arrive(land, self.late_sems, k * self.nc + m, c)
+            terms.append(land)
+        return terms
+
+    def chips(self, c):
+        for m in self.first(c):
+            terms = self.mine(m, c)
+            add_into(terms[0], *terms)
+            hop, to = m, m
+            if self.tree:
+                hop, to = (2 if m == 3 else 1), relay_of(c)
+            chip = (flip(self.f, 2 * to), self.z)
+            self.push(terms[0], self.rx.at[c, hop - 1], self.sems, hop, c, chip)
+
+    def across(self, c):
+        if not self.tree:
+            return
+        m = 3 - relay_of(c)
+        terms = self.mine(m, c)
+        self.arrive(self.rx.at[c, 1], self.sems, 2, c)
+        add_into(terms[0], *terms, self.rx.at[c, 1])
+        self.push(terms[0], self.rx.at[c, 2], self.sems, 3, c, (flip(self.f, 2 * m), self.z))
+
+    def landed(self, c, out):
+        terms = self.mine(0, c)
+        for m in range(1, self.nc):
+            if self.tree and m == 2:
+                continue
+            self.arrive(self.rx.at[c, m - 1], self.sems, m, c)
+            terms.append(self.rx.at[c, m - 1])
         add_into(out, *terms)
 
 
@@ -401,19 +529,26 @@
 
 GROUP=128
 
-def attention_fwd(npos, fr, x, gain1, gain2, w, a_out, qkv, ob, x1_out, b_out):
-    rows, d = x.shape
+def attention_start(x, gain1, a_out):
     xf = x[...].astype(F32)
     rinv1 = lax.rsqrt(jnp.mean(xf * xf, axis=1, keepdims=True) + 1e-05)
     a_out[...] = (xf * rinv1 * gain1[...]).astype(BF)
+
+
+def columns_of(left, right, first, out):
     step = 512
-    def project(i, c):
+
+    def body(i, c):
         at = pl.ds(pl.multiple_of(i * step, step), step)
-        for t in range(3):
-            to = pl.ds(pl.multiple_of(t * d + i * step, step), step)
-            qkv[:, to] = nn(a_out[...], w[t, :, at]).astype(BF)
+        to = pl.ds(pl.multiple_of(first + i * step, step), step)
+        out[:, to] = nn(left[...], right[:, at]).astype(out.dtype)
         return c
-    lax.fori_loop(0, d // step, project, 0)
+
+    lax.fori_loop(0, right.shape[1] // step, body, 0)
+
+
+def attention_heads(npos, qkv, ob):
+    rows, d = ob.shape
     mask = causal(GROUP, npos)
     low = lax.broadcasted_iota(jnp.int32, (GROUP, 2 * HD), 1) < HD
     def heads(i, c):
@@ -426,12 +561,13 @@
             ob[at, pl.ds(pl.multiple_of(i * 2 * HD, 2 * HD), 2 * HD)] = jnp.where(low, nn(p0, v), nn(p1, v)).astype(BF)
         return c
     lax.fori_loop(0, d // (2 * HD), heads, 0)
-    def out(i, c):
-        at = pl.ds(pl.multiple_of(i * step, step), step)
-        x1_out[:, at] = x[:, at].astype(F32) + nn(ob[...], w[3, :, at])
-        return c
-    lax.fori_loop(0, d // step, out, 0)
-    x1 = x1_out[...]
+
+
+def attention_end(npos, fr, x, gain2, w_out, ob, x1_out, b_out):
+    rows, _ = x.shape
+    columns_of(ob, w_out, 0, x1_out)
+    x1 = x1_out[...] + x[...].astype(F32)
+    x1_out[...] = x1
     rinv2 = lax.rsqrt(jnp.mean(x1 * x1, axis=1, keepdims=True) + 1e-05)
     b = (x1 * rinv2 * gain2[...]).astype(BF)
     b_out[...] = nn(by_position(rows, npos, fr), b).astype(BF)
@@ -562,7 +698,7 @@
     w_out, gy_out, grads_out, hid_out, a, qkv, ob, x1, db_rows, z_rows,
     own_w, w, gy_pos, b_pos, send, stage, down, gy_all, b_all, pair,
     db_sib, db_rx, z_sib, z_rx,
-    sems_w, sems_gy, sems_b, sems_swap, sems_in, sems_out, sems_grads, sems_down,
+    sems_w, sems_late, sems_gy, sems_b, sems_swap, sems_in, sems_out, sems_grads, sems_down,
     sems_db, sems_db_home, sems_z, sems_z_home,
 ):
     d = x.shape[1]
@@ -580,13 +716,13 @@
     def span(at, size):
         return pl.ds(pl.multiple_of(at * size, size), size)
 
-    weights = Gather(
-        nf, nz,
+    places = (
         lambda zz, c: own_w.at[c],
         lambda ff, zz, c: w.at[c, span(ff * nz + zz, each)],
         lambda ff, c: w.at[c, span(ff, nz * each)],
-        sems_w,
     )
+    early = Gather(nf, nz, *places, sems_w)
+    late = LateGather(nf, nz, *places, sems_w, sems_late)
 
     def rows_gather(mine, every, sems):
         return Gather(
@@ -597,8 +733,12 @@
             sems,
         )
 
-    for c in range(4):
-        weights.begin(c)
+    for c in LATE_W:
+        late.begin(c)
+    for c in EARLY_W:
+        early.begin(c)
+    for c in LATE_W:
+        late.relay(c)
     kept = (gy[...].astype(F32) * keep[...]).astype(BF)
     gy_pos[...] = nn(by_position(npos * fr, npos, fr), kept).astype(BF)
     grads = rows_gather(gy_pos, gy_all, sems_gy)
@@ -611,45 +751,64 @@
         return lambda ff: send.at[ff, :, p]
 
     swaps = [Swap(nf, send_at(p), pair_at(p), sems_swap.at[p]) for p in range(lp)]
-    half = lp // 2
-    for c in range(4):
-        weights.along(c)
-        if c >= 1:
-            weights.relay(c - 1)
-        if c >= 2:
-            weights.rest(c - 2)
-        if c < lp:
-            packer.pack(c)
+    pieces = [(p, m) for p in range(lp) for m in range(nf - 1, 0, -1)]
+
+    def pump(count):
+        for p, m in pieces[:count]:
+            swaps[p].start([m])
+        del pieces[:count]
+
     for p in range(lp):
         grads.begin(p)
-    for p in range(4, lp):
-        packer.pack(p)
-    weights.relay(3)
-    weights.rest(2)
+    packer.pack(0)
+    for i, c in enumerate(EARLY_W):
+        early.along(c)
+        if i == 0:
+            for at in LATE_W:
+                late.along(at)
+        else:
+            early.relay(EARLY_W[i - 1])
+        if i + 1 < lp:
+            packer.pack(i + 1)
+    early.relay(EARLY_W[-1])
+    for c in EARLY_W:
+        early.rest(c)
     for p in range(lp):
         grads.along(p)
-    weights.rest(3)
-    for p in range(half):
-        swaps[p].start()
+    for p in range(len(EARLY_W) + 1, lp):
+        packer.pack(p)
+    attention_start(x, gain1, a)
+    for c in range(3):
+        if c in LATE_W:
+            for p in range(lp if c == LATE_W[0] else 0):
+                grads.relay(p)
+            pump(FILL[0] if c == LATE_W[0] else 0)
+            late.rest(c)
+        (late if c in LATE_W else early).whole(c)
+        columns_of(a, w.at[c], c * d, qkv)
+    if LATE_W == (3,):
+        for p in range(lp):
+            grads.relay(p)
+        pump(FILL[0])
+    attention_heads(npos, qkv, ob)
+    pump(FILL[1])
+    late.rest(3)
+    late.whole(3)
+    attention_end(npos, fr, x, gain2, w.at[3], ob, x1, b_pos)
     for p in range(lp):
-        grads.relay(p)
-    for c in range(4):
-        weights.whole(c)
-    weights.finish()
+        rows.begin(p)
+    early.finish()
+    late.finish()
     save_w = pltpu.make_async_copy(w, w_out, sems_out.at[0])
     save_w.start()
-    attention_fwd(npos, fr, x, gain1, gain2, w, a, qkv, ob, x1, b_pos)
-    for p in range(lp):
-        rows.begin(p)
-    for p in range(lp):
-        grads.rest(p)
     for p in range(lp):
         rows.along(p)
         if p >= 1:
             rows.relay(p - 1)
     rows.relay(lp - 1)
-    for p in range(half, lp):
-        swaps[p].start()
+    pump(len(pieces))
+    for p in range(lp):
+        grads.rest(p)
     for p in range(lp):
         grads.whole(p)
     grads.finish()
@@ -676,6 +835,11 @@
 
     def fetch(p):
         return pltpu.make_async_copy(down_w.at[p], down.at[p % 2], sems_down.at[p % 2])
+
+    def steps(name, p):
+        if p >= 0:
+            for each_sum in (s_db, s_z):
+                getattr(each_sum, name)(p)
 
     saves = []
     fetch(0).start()
@@ -694,21 +858,13 @@
             pltpu.make_async_copy(send.at[:, :, p], grads_out.at[:, :, p], sems_grads.at[p])
         )
         saves[-1].start()
-        s_db.pairs(p)
-        if p >= 1:
-            s_db.chips(p - 1)
-        s_z.pairs(p)
-        if p >= 2:
-            s_db.across(p - 2)
-        if p >= 3:
-            s_db.home(p - 3)
-            s_z.chips(p - 3)
-    for step, last in ((s_db.chips, 1), (s_db.across, 2), (s_db.home, 3), (s_z.chips, 3)):
+        steps("pairs", p)
+        steps("chips", p - 1)
+        steps("across", p - 2)
+        steps("home", p - 3)
+    for name, last in (("chips", 1), ("across", 2), ("home", 3), ("landed", lp)):
         for p in range(max(lp - last, 0), lp):
-            step(p)
-    for step in (s_z.across, s_z.home, s_db.landed, s_z.landed):
-        for p in range(lp):
-            step(p)
+            steps(name, p)
     rows.finish()
     save_gy.wait()
     for copy in saves:
@@ -721,7 +877,8 @@
     nf, nz, npos, fr,
     grads, w_in, x, gy, keep, gain1, gain2, x1, a, qkv, ob, db_rows, z_rows,
     block_out, rows_grad, total, gains, pair_all,
-    t_sib, t_rx, t_sems, t_home, g_sib, g_rx, g_sems, g_home, t_land, g_land, sems_swap, sem_w,
+    t_sib, t_rx, t_sems, t_home, g_sib, g_rx, g_sems, g_home, t_land, g_land,
+    l_sib, l_rx, l_sems, l_late, l_zl, sems_swap, sem_w,
     w, terms, tail, dx1, dxb, do, dqkv,
 ):
     d = x.shape[1]
@@ -736,60 +893,82 @@
         return lambda ff: ref.at[ff, :, p]
 
     swaps = [Swap(nf, part(grads, p), part(pair_all, p), sems_swap.at[p]) for p in range(lp)]
-    for swap in swaps:
-        swap.start()
+    pieces = [(p, m) for p in range(lp) for m in range(nf - 1, 0, -1)]
+
+    def pump(count):
+        for p, m in pieces[:count]:
+            swaps[p].start([m])
+        del pieces[:count]
+
+    pump(PUMP[0])
 
     def span(ff):
         return pl.ds(pl.multiple_of(ff * nz * each, nz * each), nz * each)
 
-    s_t = BlockSums(
-        nf, nz,
-        lambda ff, c: terms.at[c, span(ff)],
-        lambda c, m: terms.at[c, span(flip(f, 2 * m))],
-        t_sib, t_rx, t_sems, t_home, t_land, each,
-    )
+    def terms_of(table):
+        return (
+            lambda ff, c: terms.at[table[c], span(ff)],
+            lambda c, m: terms.at[table[c], span(flip(f, 2 * m))],
+        )
+
+    s_t = BlockSums(nf, nz, *terms_of(EARLY), t_sib, t_rx, t_sems, t_home, t_land, each)
+    s_l = PosSums(nf, nz, *terms_of(LATE), l_sib, l_rx, l_sems, l_late, l_zl, each)
     s_g = BlockSums(
         nf, nz,
         lambda ff, c: tail.at[span(ff)],
         lambda c, m: tail.at[span(flip(f, 2 * m))],
         g_sib, g_rx, g_sems, g_home, g_land, each,
     )
+
+    def both(step, c):
+        sums, at = (s_l, LATE.index(c)) if c in LATE else (s_t, EARLY.index(c))
+        if hasattr(sums, step):
+            getattr(sums, step)(at)
+
     gain2_grad = attention_bwd_in(npos, fr, db_rows, gy, keep, x1, ob, gain2, dx1, dxb, terms)
-    s_t.pairs(3)
+    both("pairs", 3)
     load_w.wait()
     do[...] = nt(dxb[...], w[3]).astype(BF)
-    s_t.chips(3)
+    both("along" if 3 in LATE else "chips", 3)
     attention_bwd_heads(npos, qkv, do, dqkv)
-    s_t.across(3)
+    if 3 not in LATE:
+        both("across", 3)
+    weight_terms(a, dqkv, 2 * d, terms.at[2])
+    both("pairs", 2)
+    pump(PUMP[1])
     weight_terms(a, dqkv, 0, terms.at[0])
-    s_t.pairs(0)
+    both("pairs", 0)
+    both("along" if 2 in LATE else "chips", 2)
     weight_terms(a, dqkv, d, terms.at[1])
-    s_t.pairs(1)
-    s_t.chips(0)
-    weight_terms(a, dqkv, 2 * d, terms.at[2])
-    s_t.pairs(2)
-    s_t.chips(1)
+    both("pairs", 1)
+    both("chips", 0)
     gain1_grad = attention_bwd_rows(x, dqkv, w, gain1, dx1, rows_grad)
     gains_into(gain1_grad, gain2_grad, tail)
     s_g.pairs(0)
-    s_t.chips(2)
+    both("chips", 1)
     s_g.chips(0)
-    s_t.home(3)
+    pump(PUMP[2])
+    order = [c for c in (2, 0, 1) if c in EARLY]
+    for c in order:
+        both("across", c)
+    s_g.across(0)
+    for c in LATE:
+        both("chips", c)
+    pump(PUMP[3])
+    for c in ([3] if 3 in EARLY else []) + order:
+        both("home", c)
+    s_g.home(0)
+    for c in LATE:
+        both("across", c)
+    pump(len(pieces))
     back = nn(by_position(npos * fr, npos, fr, True), z_rows[...])
     block_out[...] = (keep[...] * (x1[...] + back)).astype(BF)
-    s_t.across(0)
-    s_t.across(1)
-    s_g.across(0)
-    s_t.home(0)
-    s_t.across(2)
-    s_g.home(0)
-    s_t.home(1)
-    s_t.home(2)
-    for c in (3, 0, 1, 2):
-        s_t.landed(c, total.at[:, pl.ds(c * d, d)])
+    for sums, table in ((s_t, EARLY), (s_l, LATE)):
+        for at, c in enumerate(table):
+            sums.landed(at, total.at[:, pl.ds(c * d, d)])
     s_g.landed(0, gains)
-    s_t.finish()
-    s_g.finish()
+    for sums in (s_t, s_l, s_g):
+        sums.finish()
     for swap in swaps:
         swap.finish()
 
@@ -1063,6 +1242,7 @@
             *row_scratch[:2],
             *row_scratch[:2],
             gather_sems,
+            dma(*LateGather.late_shape(nf, nz, 4)),
             rows_sems,
             rows_sems,
             swap_sems,
@@ -1087,10 +1267,11 @@
         in_specs=[ANY] * 2 + [VM] * 11,
         out_specs=(VM,) * 4 + (ANY,),
         scratch_shapes=[
-            *HomeSums.scratch(nf, nz, 4, nz * each, d),
+            *HomeSums.scratch(nf, nz, len(EARLY), nz * each, d),
             *HomeSums.scratch(nf, nz, 1, nz * each, 128),
-            vmem((4, nz - 1, each, d)),
+            vmem((len(EARLY), nz - 1, each, d)),
             vmem((1, nz - 1, each, 128)),
+            *PosSums.scratch(nf, nz, len(LATE), each, d),
             swap_sems,
             pltpu.SemaphoreType.DMA,
             vmem((4, d, d)),

time: 346 us -> 304 us (0.88)
  Pallas kernels: 341 us -> 299 us
    pallas_call x1, Pallas kernels: 126 us -> 94 us  [local_fused(): call(functools.partial(behind_kernel, nf, nz, npos, fr), 1, out_shape=(ma...]
    pallas_call x1, Pallas kernels: 203 us -> 194 us  [local_fused(): call(functools.partial(ahead_kernel, nf, nz, npos, fr), 0, out_shape=(mak...]
where the time goes in v6:
time: 304 us
  Pallas kernels  299 us (98%)
  local copies, waits for them, and re-layouts  3.3 us (1%)
    pallas_call x1, Pallas kernels, local_fused(): call(functools.partial(ahead_kernel, nf, nz, npos, fr), 0, out_shape=(mak...  194 us
    pallas_call x1, Pallas kernels, local_fused(): call(functools.partial(behind_kernel, nf, nz, npos, fr), 1, out_shape=(ma...  94 us
    pallas_call x1, Pallas kernels, local_fused(): pl.pallas_call(last_local_kernel, grid=(lp,), out_shape=(make((lp, dslice...  11.1 us

profile of v6, /device:TPU:0, one launch (start us, length us, event | category | flops | bytes accessed | tf_op | source)
XLA Modules:
  0.0 304.1 jit_solution(3223715848964021450)
XLA Ops:
  0.6 0.7 convert_element_type.3
  1.3 0.1 broadcast_in_dim.2
  1.4 0.8 reshape.47.keep
  2.1 193.6 %shard_map.169 = (bf16[4,1024,1024]{2,1,0:T(8,128)(2,1)}, bf16[4,512,1024]{2,1,0:T(8,128)(2,1)}, bf16[8,2,4,352,128]{4,3,2,1,0:T(8,128)(2,1)}, bf16[4,352,512]{2...) custom-call(bf16[256,1024]{1,0:T(8,128)(2,1)} %bitcast.6, ...), custom_call_target="tpu_custom_call" | custom-call | tf_op jit(solution)/shard_map/pallas_call | solution.py:1214
  195.8 94.0 %shard_map.170 = (bf16[256,1024]{1,0:T(8,128)(2,1)}, f32[256,1024]{1,0:T(8,128)}, f32[32,4096]{1,0:T(8,128)}, f32[32,128]{1,0:T(8,128)}, bf16[8,2,4,352,128]{4,3,2,1,0:T(8,128)(2,1)}) custom-call(bf16[8,2,4,352,128]{4,3,2,1,0:T(8,128)(2,1)} %get-tuple-element.29.grads, bf16[4,1024,1024]{2,1,0:T(8,128)(2,1)} %get-tuple-element.30.w_in, ...), custom_call_target="tpu_custom_call" | custom-call | tf_op jit(solution)/shard_map/pallas_call | solution.py:1257
  289.7 0.9 slice_add_fusion
  290.6 0.7 slice_reduce_fusion
  291.3 0.0 copy-start.1
  291.3 0.0 copy-start
  291.3 11.1 %shard_map.171 = (f32[4,128,2816]{2,1,0:T(8,128)}, f32[4,128,2816]{2,1,0:T(8,128)}, f32[4,352,1024]{2,1,0:T(8,128)}, f32[32,3072]{1,0:T(8,128)}, f32[32,1024]{1,0:T(8,128)}) custom-call(bf16[8,2,4,352,128]{4,3,2,1,0:T(8,128)(2,1)} %get-tuple-element.40.pair, bf16[4,352,512]{2,1,0:T(8,128)(2,1)} %get-tuple-element.41.hid, ...), custom_call_target="tpu_custom_call" | custom-call | tf_op jit(solution)/shard_map/pallas_call | solution.py:1291
  302.4 0.0 copy-done.1
  302.4 0.8 copy.23
  303.2 0.0 copy-done
  303.2 1.0 copy.24
Async XLA Ops:
  291.3 11.1 %copy-start.1 = (bf16[256,1024]{1,0:T(8,128)(2,1)S(1)}, bf16[256,1024]{1,0:T(8,128)(2,1)}, u32[]{:S(2)}) copy-start(bf16[256,1024]{1,0:T(8,128)(2,1)} %get-tuple-element.37) | copy-start | bytes 1572868
  291.3 11.9 %copy-start = (f32[256,1024]{1,0:T(8,128)S(1)}, f32[256,1024]{1,0:T(8,128)}, u32[]{:S(2)}) copy-start(f32[256,1024]{1,0:T(8,128)} %get-tuple-element.38) | copy-start | bytes 3145732

commit v7 on v6

--- a/solution.py
+++ b/solution.py
@@ -13,8 +13,9 @@
 BF = jnp.bfloat16
 F32 = jnp.float32
 MESH = pl.DeviceIdType.MESH
-FILL = (10, 6)
-PUMP = (14, 4, 3, 3)
+MASKS = (1, 2, 4, 3, 5, 6, 7)
+FILL = (7, 9, 4)
+PUMP = (7, 0, 12, 4, 2, 2)
 LATE = (2, 3)
 EARLY = tuple(c for c in range(4) if c not in LATE)
 LATE_W = (2, 3)
@@ -86,7 +87,8 @@
         return (2, nz + nf, parts)
 
     def push(self, src, dst, hop, c, to):
-        self.sent.append(remote(src, dst, self.sems.at[0, hop, c], self.sems.at[1, hop, c], to))
+        copy = remote(src, dst, self.sems.at[0, hop, c], self.sems.at[1, hop, c], to)
+        self.sent.append((c, copy))
 
     def arrive(self, dst, hop, c):
         arrival(dst, self.sems.at[0, hop, c], self.sems.at[1, hop, c])
@@ -135,9 +137,11 @@
             group = self.group_at(flip(self.f, 2 * m + 1), c)
             self.arrive(group, self.nz + self.nc + m, c)
 
-    def finish(self):
-        for copy in self.sent:
-            copy.wait_send()
+    def finish(self, part=None):
+        for c, copy in self.sent:
+            if part is None or c == part:
+                copy.wait_send()
+        self.sent = [(c, copy) for c, copy in self.sent if part is not None and c != part]
 
 
 class LateGather(Gather):
@@ -178,7 +182,8 @@
             for m in range(self.nc):
                 block, hop = self.block(m, 0, c), k * self.nc + m
                 send, recv = self.late_sems.at[0, hop, c], self.late_sems.at[1, hop, c]
-                self.sent.append(remote(block, block, send, recv, (self.f, flip(self.z, k))))
+                copy = remote(block, block, send, recv, (self.f, flip(self.z, k)))
+                self.sent.append((c, copy))
 
     def rest(self, c=0):
         for m in range(self.nc):
@@ -430,7 +435,7 @@
     return pl.pallas_call(
         kernel,
         compiler_params=pltpu.CompilerParams(
-            collective_id=ident, has_side_effects=True, vmem_limit_bytes=60 * 2**20
+            collective_id=ident, has_side_effects=True, vmem_limit_bytes=63 * 2**20
         ),
         **kw,
     )
@@ -674,40 +679,49 @@
 
 def feed(p, gy_rows, b_rows, pair, wd, hid_out, grads, db, z):
     nf, _, _, _, width = grads.shape
-    b = b_rows[p]
+    b = b_rows[...]
     gate = nt(pair[0, p], b)
     up = nt(pair[1, p], b)
-    dhid = nt(wd, gy_rows[p])
+    dhid = nt(wd[...], gy_rows[...])
     s = jax.nn.sigmoid(gate)
     silu = gate * s
     hid = (silu * up).astype(BF)
     dgate = (dhid * up * s * (1.0 + gate * (1.0 - s))).astype(BF)
     dup = (dhid * silu).astype(BF)
-    hid_out[p] = hid
-    db[...] = (tn(dgate, pair[0, p]) + tn(dup, pair[1, p])).astype(BF)
-    z[...] = tn(hid, wd).astype(BF)
+    hid_out[...] = hid
+    z[...] = tn(hid, wd[...]).astype(BF)
     for at, term in enumerate((dgate, dup)):
-        grad = nn(term, b).astype(BF)
+        grad = nn(term, b_rows[...]).astype(BF)
         for j in range(nf):
             grads[j, at, p] = grad[:, j * width : (j + 1) * width]
-
-
-def ahead_kernel(
+    db[...] = (tn(dgate, pair[0, p]) + tn(dup, pair[1, p])).astype(BF)
+
+
+def layer_kernel(
     nf, nz, npos, fr,
     x, gy, keep, gain1, gain2, qkv_w, out_w, gate_w, up_w, down_w,
-    w_out, gy_out, grads_out, hid_out, a, qkv, ob, x1, db_rows, z_rows,
-    own_w, w, gy_pos, b_pos, send, stage, down, gy_all, b_all, pair,
+    block_out, rows_grad, total, gains, gy_out, hid_out, back,
+    own_w, w, gy_pos, b_pos, send, stage, down, wd, hid, big, pair,
+    a, qkv, ob, x1, db_rows, z_rows, tail,
     db_sib, db_rx, z_sib, z_rx,
-    sems_w, sems_late, sems_gy, sems_b, sems_swap, sems_in, sems_out, sems_grads, sems_down,
+    t_sib, t_rx, t_sems, t_home, g_sib, g_rx, g_sems, g_home, t_land, g_land,
+    l_sib, l_rx, l_sems, l_late, l_zl,
+    sems_w, sems_late, sems_gy, sems_b, sems_swap, sems_back, sems_in, sems_out, sems_hid, sem_down,
     sems_db, sems_db_home, sems_z, sems_z_home,
 ):
     d = x.shape[1]
     each = own_w.shape[1]
     lp = npos // nz
     width = send.shape[4]
+    count = nf * nz * fr
     f, z = place()
     packer = Packer((gate_w, up_w), stage, sems_in, send)
     packer.begin()
+
+    def fetch(p):
+        return pltpu.make_async_copy(down_w.at[p], down, sem_down)
+
+    fetch(0).start()
     greet(nf, nz, True)
     for i in range(3):
         own_w[i] = qkv_w[:, i * d : (i + 1) * d].astype(BF)
@@ -715,6 +729,11 @@
 
     def span(at, size):
         return pl.ds(pl.multiple_of(at * size, size), size)
+
+    per = d // count
+
+    def rows_at(first, p):
+        return big.at[first + p // per, pl.ds((p % per) * count, count)]
 
     places = (
         lambda zz, c: own_w.at[c],
@@ -728,8 +747,8 @@
         return Gather(
             nf, nz,
             lambda zz, p: mine.at[span(zz * lp + p, fr)],
-            lambda ff, zz, p: every.at[p, span(ff * nz + zz, fr)],
-            lambda ff, p: every.at[p, span(ff, nz * fr)],
+            lambda ff, zz, p: every(p).at[span(ff * nz + zz, fr)],
+            lambda ff, p: every(p).at[span(ff, nz * fr)],
             sems,
         )
 
@@ -737,12 +756,10 @@
         late.begin(c)
     for c in EARLY_W:
         early.begin(c)
-    for c in LATE_W:
-        late.relay(c)
     kept = (gy[...].astype(F32) * keep[...]).astype(BF)
     gy_pos[...] = nn(by_position(npos * fr, npos, fr), kept).astype(BF)
-    grads = rows_gather(gy_pos, gy_all, sems_gy)
-    rows = rows_gather(b_pos, b_all, sems_b)
+    grads = rows_gather(gy_pos, lambda p: rows_at(0, p), sems_gy)
+    rows = rows_gather(b_pos, lambda p: rows_at(2, p), sems_b)
 
     def pair_at(p):
         return lambda ff: pair.at[:, p, :, span(ff, width)]
@@ -751,7 +768,7 @@
         return lambda ff: send.at[ff, :, p]
 
     swaps = [Swap(nf, send_at(p), pair_at(p), sems_swap.at[p]) for p in range(lp)]
-    pieces = [(p, m) for p in range(lp) for m in range(nf - 1, 0, -1)]
+    pieces = [(p, m) for p in range(lp) for m in MASKS]
 
     def pump(count):
         for p, m in pieces[:count]:
@@ -761,6 +778,9 @@
     for p in range(lp):
         grads.begin(p)
     packer.pack(0)
+    pump(FILL[0])
+    for c in LATE_W:
+        late.relay(c)
     for i, c in enumerate(EARLY_W):
         early.along(c)
         if i == 0:
@@ -782,16 +802,12 @@
         if c in LATE_W:
             for p in range(lp if c == LATE_W[0] else 0):
                 grads.relay(p)
-            pump(FILL[0] if c == LATE_W[0] else 0)
+            pump(FILL[1] if c == LATE_W[0] else 0)
             late.rest(c)
         (late if c in LATE_W else early).whole(c)
         columns_of(a, w.at[c], c * d, qkv)
-    if LATE_W == (3,):
-        for p in range(lp):
-            grads.relay(p)
-        pump(FILL[0])
     attention_heads(npos, qkv, ob)
-    pump(FILL[1])
+    pump(FILL[2])
     late.rest(3)
     late.whole(3)
     attention_end(npos, fr, x, gain2, w.at[3], ob, x1, b_pos)
@@ -799,8 +815,8 @@
         rows.begin(p)
     early.finish()
     late.finish()
-    save_w = pltpu.make_async_copy(w, w_out, sems_out.at[0])
-    save_w.start()
+    for p in range(lp):
+        grads.rest(p)
     for p in range(lp):
         rows.along(p)
         if p >= 1:
@@ -808,138 +824,118 @@
     rows.relay(lp - 1)
     pump(len(pieces))
     for p in range(lp):
-        grads.rest(p)
-    for p in range(lp):
         grads.whole(p)
     grads.finish()
-    save_gy = pltpu.make_async_copy(gy_all, gy_out, sems_out.at[1])
+    save_gy = pltpu.make_async_copy(big.at[: 2], gy_out, sems_out.at[0])
     save_gy.start()
-
-    count = b_all.shape[1]
     share = count // nf
-
-    def term_at(first, p):
-        per = d // count
-        return w.at[first + p // per, pl.ds((p % per) * count, count)]
 
     def sums(first, sib, rx, sems, home_sems, land):
         def at(ff, p):
-            return term_at(first, p).at[span(ff, share)]
+            return rows_at(first, p).at[span(ff, share)]
 
         return RowSums(
             nf, nz, at, lambda p, m: at(flip(f, 2 * m), p), sib, rx, sems, home_sems, land, fr
         )
 
-    s_db = sums(0, db_sib, db_rx, sems_db, sems_db_home, db_rows)
-    s_z = sums(2, z_sib, z_rx, sems_z, sems_z_home, z_rows)
-
-    def fetch(p):
-        return pltpu.make_async_copy(down_w.at[p], down.at[p % 2], sems_down.at[p % 2])
-
-    def steps(name, p):
-        if p >= 0:
-            for each_sum in (s_db, s_z):
-                getattr(each_sum, name)(p)
-
-    saves = []
-    fetch(0).start()
+    s_db = sums(2, db_sib, db_rx, sems_db, sems_db_home, db_rows)
+    s_z = sums(0, z_sib, z_rx, sems_z, sems_z_home, z_rows)
+
+    def back_at(p):
+        return lambda ff: back.at[ff, :, p]
+
+    backs = [Swap(nf, send_at(p), back_at(p), sems_back.at[p]) for p in range(lp)]
+    grad_pieces = [(p, m) for p in range(lp) for m in MASKS]
+
+    def pump_back(size):
+        for p, m in grad_pieces[:size]:
+            backs[p].start([m])
+        del grad_pieces[:size]
+
+    def save_hid(p):
+        return pltpu.make_async_copy(hid.at[p % 2], hid_out.at[p], sems_hid.at[p % 2])
+
     rows.rest(0)
-    save_w.wait()
+    save_gy.wait()
     for p in range(lp):
         if p + 1 < lp:
-            fetch(p + 1).start()
             rows.rest(p + 1)
         fetch(p).wait()
-        wd = down[p % 2].astype(BF)
+        wd[...] = down[...].astype(BF)
+        if p + 1 < lp:
+            fetch(p + 1).start()
         rows.whole(p)
+        rows.finish(p)
         swaps[p].finish()
-        feed(p, gy_all, b_all, pair, wd, hid_out, send, term_at(0, p), term_at(2, p))
-        saves.append(
-            pltpu.make_async_copy(send.at[:, :, p], grads_out.at[:, :, p], sems_grads.at[p])
-        )
-        saves[-1].start()
-        steps("pairs", p)
-        steps("chips", p - 1)
-        steps("across", p - 2)
-        steps("home", p - 3)
-    for name, last in (("chips", 1), ("across", 2), ("home", 3), ("landed", lp)):
+        if p >= 2:
+            save_hid(p - 2).wait()
+        gy_rows, b_rows = rows_at(0, p), rows_at(2, p)
+        feed(p, gy_rows, b_rows, pair, wd, hid.at[p % 2], send, b_rows, gy_rows)
+        save_hid(p).start()
+        s_db.pairs(p)
+        if p >= 1:
+            s_db.chips(p - 1)
+        if p >= 2:
+            s_db.across(p - 2)
+        if p >= 3:
+            s_db.home(p - 3)
+        s_z.pairs(p)
+    for name, last in (("chips", 1), ("across", 2)):
         for p in range(max(lp - last, 0), lp):
-            steps(name, p)
-    rows.finish()
-    save_gy.wait()
-    for copy in saves:
-        copy.wait()
+            getattr(s_db, name)(p)
+        if name == "chips":
+            s_z.chips(0)
+            s_z.chips(1)
+    pump_back(PUMP[0])
+    for p in range(max(lp - 3, 0), lp):
+        s_db.home(p)
+    for p in range(2, lp):
+        s_z.chips(p)
+    for p in range(2):
+        s_z.across(p)
+    pump_back(PUMP[1])
+    for p in range(lp):
+        s_db.landed(p)
     s_db.finish()
-    s_z.finish()
-
-
-def behind_kernel(
-    nf, nz, npos, fr,
-    grads, w_in, x, gy, keep, gain1, gain2, x1, a, qkv, ob, db_rows, z_rows,
-    block_out, rows_grad, total, gains, pair_all,
-    t_sib, t_rx, t_sems, t_home, g_sib, g_rx, g_sems, g_home, t_land, g_land,
-    l_sib, l_rx, l_sems, l_late, l_zl, sems_swap, sem_w,
-    w, terms, tail, dx1, dxb, do, dqkv,
-):
-    d = x.shape[1]
-    each = gains.shape[0]
-    lp = npos // nz
-    f, z = place()
-    load_w = pltpu.make_async_copy(w_in, w, sem_w)
-    load_w.start()
-    greet(nf, nz, True)
-
-    def part(ref, p):
-        return lambda ff: ref.at[ff, :, p]
-
-    swaps = [Swap(nf, part(grads, p), part(pair_all, p), sems_swap.at[p]) for p in range(lp)]
-    pieces = [(p, m) for p in range(lp) for m in range(nf - 1, 0, -1)]
-
-    def pump(count):
-        for p, m in pieces[:count]:
-            swaps[p].start([m])
-        del pieces[:count]
-
-    pump(PUMP[0])
-
-    def span(ff):
-        return pl.ds(pl.multiple_of(ff * nz * each, nz * each), nz * each)
 
     def terms_of(table):
         return (
-            lambda ff, c: terms.at[table[c], span(ff)],
-            lambda c, m: terms.at[table[c], span(flip(f, 2 * m))],
+            lambda ff, c: big.at[table[c], span(ff, nz * each)],
+            lambda c, m: big.at[table[c], span(flip(f, 2 * m), nz * each)],
         )
 
     s_t = BlockSums(nf, nz, *terms_of(EARLY), t_sib, t_rx, t_sems, t_home, t_land, each)
     s_l = PosSums(nf, nz, *terms_of(LATE), l_sib, l_rx, l_sems, l_late, l_zl, each)
     s_g = BlockSums(
         nf, nz,
-        lambda ff, c: tail.at[span(ff)],
-        lambda c, m: tail.at[span(flip(f, 2 * m))],
+        lambda ff, c: tail.at[span(ff, nz * each)],
+        lambda c, m: tail.at[span(flip(f, 2 * m), nz * each)],
         g_sib, g_rx, g_sems, g_home, g_land, each,
     )
 
     def both(step, c):
-        sums, at = (s_l, LATE.index(c)) if c in LATE else (s_t, EARLY.index(c))
-        if hasattr(sums, step):
-            getattr(sums, step)(at)
-
-    gain2_grad = attention_bwd_in(npos, fr, db_rows, gy, keep, x1, ob, gain2, dx1, dxb, terms)
+        group, at = (s_l, LATE.index(c)) if c in LATE else (s_t, EARLY.index(c))
+        getattr(group, step)(at)
+
+    dx1, dxb, do, dqkv = rows_grad, b_pos, gy_pos, qkv
+    gain2_grad = attention_bwd_in(npos, fr, db_rows, gy, keep, x1, ob, gain2, dx1, dxb, big)
     both("pairs", 3)
-    load_w.wait()
     do[...] = nt(dxb[...], w[3]).astype(BF)
-    both("along" if 3 in LATE else "chips", 3)
+    both("along", 3)
+    for p in range(2, lp):
+        s_z.across(p)
+    pump_back(PUMP[2])
     attention_bwd_heads(npos, qkv, do, dqkv)
-    if 3 not in LATE:
-        both("across", 3)
-    weight_terms(a, dqkv, 2 * d, terms.at[2])
+    weight_terms(a, dqkv, 2 * d, big.at[2])
     both("pairs", 2)
-    pump(PUMP[1])
-    weight_terms(a, dqkv, 0, terms.at[0])
+    for p in range(lp):
+        s_z.home(p)
+    s_z.finish()
+    pump_back(PUMP[3])
+    weight_terms(a, dqkv, 0, big.at[0])
     both("pairs", 0)
-    both("along" if 2 in LATE else "chips", 2)
-    weight_terms(a, dqkv, d, terms.at[1])
+    both("along", 2)
+    weight_terms(a, dqkv, d, big.at[1])
     both("pairs", 1)
     both("chips", 0)
     gain1_grad = attention_bwd_rows(x, dqkv, w, gain1, dx1, rows_grad)
@@ -947,29 +943,32 @@
     s_g.pairs(0)
     both("chips", 1)
     s_g.chips(0)
-    pump(PUMP[2])
-    order = [c for c in (2, 0, 1) if c in EARLY]
-    for c in order:
-        both("across", c)
+    pump_back(PUMP[4])
+    both("across", 0)
+    both("across", 1)
     s_g.across(0)
     for c in LATE:
         both("chips", c)
-    pump(PUMP[3])
-    for c in ([3] if 3 in EARLY else []) + order:
-        both("home", c)
+    pump_back(PUMP[5])
+    both("home", 0)
+    both("home", 1)
     s_g.home(0)
     for c in LATE:
         both("across", c)
-    pump(len(pieces))
-    back = nn(by_position(npos * fr, npos, fr, True), z_rows[...])
-    block_out[...] = (keep[...] * (x1[...] + back)).astype(BF)
-    for sums, table in ((s_t, EARLY), (s_l, LATE)):
+    pump_back(len(grad_pieces))
+    for p in range(lp):
+        s_z.landed(p)
+    turned = nn(by_position(npos * fr, npos, fr, True), z_rows[...])
+    block_out[...] = (keep[...] * (x1[...] + turned)).astype(BF)
+    for group, table in ((s_t, EARLY), (s_l, LATE)):
         for at, c in enumerate(table):
-            sums.landed(at, total.at[:, pl.ds(c * d, d)])
+            group.landed(at, total.at[:, pl.ds(c * d, d)])
     s_g.landed(0, gains)
-    for sums in (s_t, s_l, s_g):
-        sums.finish()
-    for swap in swaps:
+    for p in range(max(lp - 2, 0), lp):
+        save_hid(p).wait()
+    for group in (s_t, s_l, s_g):
+        group.finish()
+    for swap in backs:
         swap.finish()
 
 
@@ -1211,23 +1210,20 @@
     swap_sems = dma(lp, *Swap.sem_shape(nf))
     pair_shape = (nf, 2, lp, ffs, dslice)
     row_scratch = HomeSums.scratch(nf, nz, lp, nz * fr, d)
-    w_all, gy_all, grads, hid, a, qkv, ob, x1, db_rows, z_rows = call(
-        functools.partial(ahead_kernel, nf, nz, npos, fr),
+    block_out, rows_grad, total, gains, gy_all, hid, back = call(
+        functools.partial(layer_kernel, nf, nz, npos, fr),
         0,
         out_shape=(
-            make((4, d, d)),
-            make((lp, count, d)),
-            make(pair_shape),
-            make((lp, ffs, count)),
-            make((rows, d)),
-            make((rows, 3 * d)),
             make((rows, d)),
             make((rows, d), F32),
-            make((rows, d)),
-            make((rows, d)),
+            make((each, 4 * d), F32),
+            make((each, 128), F32),
+            make((2, d, d)),
+            make((lp, ffs, count)),
+            make(pair_shape),
         ),
         in_specs=[VM] * 7 + [ANY] * 3,
-        out_specs=(ANY,) * 3 + (VM,) * 7,
+        out_specs=(VM,) * 4 + (ANY,) * 3,
         scratch_shapes=[
             vmem((4, each, d)),
             vmem((4, d, d)),
@@ -1235,54 +1231,40 @@
             vmem((rows, d)),
             vmem(pair_shape),
             vmem((2, dslice, ff), F32),
-            vmem((2, ffs, d), F32),
-            vmem((lp, count, d)),
-            vmem((lp, count, d)),
+            vmem((ffs, d), F32),
+            vmem((ffs, d)),
+            vmem((2, ffs, count)),
+            vmem((4, d, d)),
             vmem((2, lp, ffs, d)),
+            vmem((rows, d)),
+            vmem((rows, 3 * d)),
+            vmem((rows, d)),
+            vmem((rows, d), F32),
+            vmem((rows, d)),
+            vmem((rows, d)),
+            vmem((d, 128)),
             *row_scratch[:2],
             *row_scratch[:2],
+            *HomeSums.scratch(nf, nz, len(EARLY), nz * each, d),
+            *HomeSums.scratch(nf, nz, 1, nz * each, 128),
+            vmem((len(EARLY), nz - 1, each, d)),
+            vmem((1, nz - 1, each, 128)),
+            *PosSums.scratch(nf, nz, len(LATE), each, d),
             gather_sems,
             dma(*LateGather.late_shape(nf, nz, 4)),
             rows_sems,
             rows_sems,
             swap_sems,
+            swap_sems,
             dma(2),
+            dma(1),
             dma(2),
-            dma(lp),
-            dma(2),
+            pltpu.SemaphoreType.DMA,
             *row_scratch[2:],
             *row_scratch[2:],
         ],
     )(x, gy, keep, gain1, gain2, qkv_master, out_master, gate_master, up_master, down_master)
-    block_out, rows_grad, total, gains, back = call(
-        functools.partial(behind_kernel, nf, nz, npos, fr),
-        1,
-        out_shape=(
-            make((rows, d)),
-            make((rows, d), F32),
-            make((each, 4 * d), F32),
-            make((each, 128), F32),
-            make(pair_shape),
-        ),
-        in_specs=[ANY] * 2 + [VM] * 11,
-        out_specs=(VM,) * 4 + (ANY,),
-        scratch_shapes=[
-            *HomeSums.scratch(nf, nz, len(EARLY), nz * each, d),
-            *HomeSums.scratch(nf, nz, 1, nz * each, 128),
-            vmem((len(EARLY), nz - 1, each, d)),
-            vmem((1, nz - 1, each, 128)),
-            *PosSums.scratch(nf, nz, len(LATE), each, d),
-            swap_sems,
-            pltpu.SemaphoreType.DMA,
-            vmem((4, d, d)),
-            vmem((4, d, d)),
-            vmem((d, 128)),
-            vmem((rows, d), F32),
-            vmem((rows, d)),
-            vmem((rows, d)),
-            vmem((rows, 3 * d)),
-        ],
-    )(grads, w_all, x, gy, keep, gain1, gain2, x1, a, qkv, ob, db_rows, z_rows)
+    gy_all = gy_all.reshape(lp, count, d)
     whole_block = pl.BlockSpec((1, dslice, ff), lambda p: (p, 0, 0))
 
     def once(*shape):
@@ -1329,7 +1311,8 @@
 
 def local(*args):
     _, dslice, _ = args[6].shape
-    if lax.axis_size("frames") == 8 and dslice % 128 == 0:
+    sizes = lax.axis_size("frames"), lax.axis_size("pos")
+    if sizes == (8, 4) and dslice % 128 == 0:
         return local_fused(*args)
     return local_general(*args)
 

time: 304 us -> 279 us (0.918); the launches traced: 304 us -> 276 us
  Pallas kernels: 299 us -> 270 us
    pallas_call x2 -> x1, Pallas kernels: 288 us -> 259 us  [local_fused(): call(functools.partial(layer_kernel, nf, nz, npos, fr), 0, out_shape=(mak...]
where the time goes in v7:
time: 279 us; the launch traced here: 276 us
  Pallas kernels  270 us (97%)
  local copies, waits for them, and re-layouts  3.3 us (1%)
    pallas_call x1, Pallas kernels, local_fused(): call(functools.partial(layer_kernel, nf, nz, npos, fr), 0, out_shape=(mak...  259 us
    pallas_call x1, Pallas kernels, local_fused(): pl.pallas_call(last_local_kernel, grid=(lp,), out_shape=(make((lp, dslice...  11.1 us

profile of v7, /device:TPU:0, one launch (start us, length us, event | category | flops | bytes accessed | tf_op | source)
XLA Modules:
  0.0 275.5 jit_solution(13847024075030063936)
XLA Ops:
  0.6 0.7 convert_element_type.3
  1.3 0.1 broadcast_in_dim.2
  1.4 0.8 reshape.51.keep
  2.1 259.0 %shard_map.169 = (bf16[256,1024]{1,0:T(8,128)(2,1)}, f32[256,1024]{1,0:T(8,128)}, f32[32,4096]{1,0:T(8,128)}, f32[32,128]{1,0:T(8,128)}, bf16[2,1024,1024]{2,1,0...) custom-call(bf16[256,1024]{1,0:T(8,128)(2,1)} %bitcast.9, bf16[256,1024]{1,0:T(8,128)(2,1)} %bitcast.10, ...), custom_call_target="tpu_custom_call" | custom-call | tf_op jit(solution)/shard_map/pallas_call | solution.py:1213
  261.1 0.9 slice_add_fusion
  262.0 0.7 slice_reduce_fusion
  262.7 0.0 copy-start.1
  262.7 0.0 copy-start
  262.7 11.1 %shard_map.170 = (f32[4,128,2816]{2,1,0:T(8,128)}, f32[4,128,2816]{2,1,0:T(8,128)}, f32[4,352,1024]{2,1,0:T(8,128)}, f32[32,3072]{1,0:T(8,128)}, f32[32,1024]{1,0:T(8,128)}) custom-call(bf16[8,2,4,352,128]{4,3,2,1,0:T(8,128)(2,1)} %get-tuple-element.24.pair, bf16[4,352,512]{2,1,0:T(8,128)(2,1)} %get-tuple-element.25.hid, bf16[4,512,1024]{2,1,0:T(8,128)(2,1)} %bitcast.7, ...), custom_call_target="tpu_custom_call" | custom-call | tf_op jit(solution)/shard_map/pallas_call | solution.py:1273
  273.8 0.0 copy-done.1
  273.8 0.8 copy.22
  274.6 0.0 copy-done
  274.6 1.0 copy.23
Async XLA Ops:
  262.7 11.1 %copy-start.1 = (bf16[256,1024]{1,0:T(8,128)(2,1)S(1)}, bf16[256,1024]{1,0:T(8,128)(2,1)}, u32[]{:S(2)}) copy-start(bf16[256,1024]{1,0:T(8,128)(2,1)} %get-tuple-element.21) | copy-start | bytes 1572868
  262.7 11.9 %copy-start = (f32[256,1024]{1,0:T(8,128)S(1)}, f32[256,1024]{1,0:T(8,128)}, u32[]{:S(2)}) copy-start(f32[256,1024]{1,0:T(8,128)} %get-tuple-element.22) | copy-start | bytes 3145732

commit v8 on v7

--- a/solution.py
+++ b/solution.py
@@ -699,9 +699,9 @@
 
 def layer_kernel(
     nf, nz, npos, fr,
-    x, gy, keep, gain1, gain2, qkv_w, out_w, gate_w, up_w, down_w,
+    x, gy, mask, gain1, gain2, qkv_w, out_w, gate_w, up_w, down_w,
     block_out, rows_grad, total, gains, gy_out, hid_out, back,
-    own_w, w, gy_pos, b_pos, send, stage, down, wd, hid, big, pair,
+    keep, own_w, w, gy_pos, b_pos, send, stage, down, wd, hid, big, pair,
     a, qkv, ob, x1, db_rows, z_rows, tail,
     db_sib, db_rx, z_sib, z_rx,
     t_sib, t_rx, t_sems, t_home, g_sib, g_rx, g_sems, g_home, t_land, g_land,
@@ -756,6 +756,10 @@
         late.begin(c)
     for c in EARLY_W:
         early.begin(c)
+    frame = lax.broadcasted_iota(jnp.int32, (npos * fr, fr), 0) // npos
+    chosen = frame == lax.broadcasted_iota(jnp.int32, (npos * fr, fr), 1)
+    alive = jnp.where(chosen, mask[...].astype(F32), 0.0)
+    keep[...] = jnp.sum(alive, axis=1, keepdims=True)
     kept = (gy[...].astype(F32) * keep[...]).astype(BF)
     gy_pos[...] = nn(by_position(npos * fr, npos, fr), kept).astype(BF)
     grads = rows_gather(gy_pos, lambda p: rows_at(0, p), sems_gy)
@@ -972,7 +976,10 @@
         swap.finish()
 
 
-def last_local_kernel(pair, hid, gy, total, gate, up, down, qkv_grad, out_grad):
+def last_local_kernel(
+    pair, hid, gy, total, gains, block_out, rows_grad,
+    gate, up, down, qkv_grad, out_grad, gain1_grad, gain2_grad, y, dx,
+):
     nf, _, _, ffs, width = pair.shape
     d = gy.shape[2]
 
@@ -980,7 +987,12 @@
     def _():
         qkv_grad[...] = total[:, : 3 * d]
         out_grad[...] = total[:, 3 * d :]
-
+        turned = gains[...].T
+        gain1_grad[...] = turned[0] + turned[2]
+        gain2_grad[...] = turned[1] + turned[3]
+
+    y[...] = block_out[...]
+    dx[...] = rows_grad[...]
     for at, out in enumerate((gate, up)):
         out[0] = pair[:, at, 0].astype(F32).reshape(nf * ffs, width).T
     down[0] = nn(hid[0], gy[0])
@@ -1202,7 +1214,7 @@
 
     x = frame_rows.reshape(rows, d)
     gy = out_cotangent.reshape(rows, d)
-    keep = jnp.broadcast_to(frame_mask.astype(F32)[:, None], (fr, npos)).reshape(rows, 1)
+    mask = frame_mask.reshape(1, fr)
     gain1 = gain_attention.reshape(1, d)
     gain2 = gain_feed.reshape(1, d)
     gather_sems = dma(*Gather.sem_shape(nf, nz, 4))
@@ -1225,6 +1237,7 @@
         in_specs=[VM] * 7 + [ANY] * 3,
         out_specs=(VM,) * 4 + (ANY,) * 3,
         scratch_shapes=[
+            vmem((rows, 1), F32),
             vmem((4, each, d)),
             vmem((4, d, d)),
             vmem((rows, d)),
@@ -1263,14 +1276,16 @@
             *row_scratch[2:],
             *row_scratch[2:],
         ],
-    )(x, gy, keep, gain1, gain2, qkv_master, out_master, gate_master, up_master, down_master)
+    )(x, gy, mask, gain1, gain2, qkv_master, out_master, gate_master, up_master, down_master)
     gy_all = gy_all.reshape(lp, count, d)
     whole_block = pl.BlockSpec((1, dslice, ff), lambda p: (p, 0, 0))
 
     def once(*shape):
         return pl.BlockSpec(shape, lambda p: (0, 0))
 
-    gate_grad, up_grad, down_grad, qkv_grad, out_grad = pl.pallas_call(
+    part_block = pl.BlockSpec((rows // lp, d), lambda p: (p, 0))
+    one = pl.BlockSpec((each,), lambda p: (0,))
+    gate_grad, up_grad, down_grad, qkv_grad, out_grad, gain1_grad, gain2_grad, y, dx = pl.pallas_call(
         last_local_kernel,
         grid=(lp,),
         out_shape=(
@@ -1279,12 +1294,19 @@
             make((lp, ffs, d), F32),
             make((each, 3 * d), F32),
             make((each, d), F32),
+            make((each,), F32),
+            make((each,), F32),
+            make((rows, d)),
+            make((rows, d), F32),
         ),
         in_specs=[
             pl.BlockSpec((nf, 2, 1, ffs, dslice), lambda p: (0, 0, p, 0, 0)),
             pl.BlockSpec((1, ffs, count), lambda p: (p, 0, 0)),
             pl.BlockSpec((1, count, d), lambda p: (p, 0, 0)),
             once(each, 4 * d),
+            once(each, 128),
+            part_block,
+            part_block,
         ],
         out_specs=(
             whole_block,
@@ -1292,15 +1314,18 @@
             pl.BlockSpec((1, ffs, d), lambda p: (p, 0, 0)),
             once(each, 3 * d),
             once(each, d),
+            one,
+            one,
+            part_block,
+            part_block,
         ),
         compiler_params=pltpu.CompilerParams(vmem_limit_bytes=60 * 2**20),
-    )(back, hid, gy_all, total)
-    gains = gains[:, :2] + gains[:, 2:4]
+    )(back, hid, gy_all, total, gains, block_out, rows_grad)
     return (
-        block_out.reshape(fr, npos, d),
-        rows_grad.reshape(fr, npos, d),
-        gains[:, 0],
-        gains[:, 1],
+        y.reshape(fr, npos, d),
+        dx.reshape(fr, npos, d),
+        gain1_grad,
+        gain2_grad,
         qkv_grad,
         out_grad,
         gate_grad,

time: 279 us -> 275 us (0.986)
  local copies, waits for them, and re-layouts: 3.3 us -> 0 us
where the time goes in v8:
time: 275 us; the launch traced here: 272 us
  Pallas kernels  271 us (99%)
    pallas_call x1, Pallas kernels, local_fused(): call(functools.partial(layer_kernel, nf, nz, npos, fr), 0, out_shape=(mak...  259 us
    pallas_call x1, Pallas kernels, local_fused(): pl.pallas_call(last_local_kernel, grid=(lp,), out_shape=(make((lp, dslice...  12.2 us

profile of v8, /device:TPU:0, one launch (start us, length us, event | category | flops | bytes accessed | tf_op | source)
XLA Modules:
  0.0 272.0 jit_solution(6526455578810767357)
XLA Ops:
  0.6 259.0 %shard_map.169 = (bf16[256,1024]{1,0:T(8,128)(2,1)}, f32[256,1024]{1,0:T(8,128)}, f32[32,4096]{1,0:T(8,128)}, f32[32,128]{1,0:T(8,128)}, bf16[2,1024,1024]{2,1,0...) custom-call(bf16[256,1024]{1,0:T(8,128)(2,1)} %bitcast.9, bf16[256,1024]{1,0:T(8,128)(2,1)} %bitcast.10, ...), custom_call_target="tpu_custom_call" | custom-call | tf_op jit(solution)/shard_map/pallas_call | solution.py:1225
  259.6 12.2 %shard_map.170 = (f32[4,128,2816]{2,1,0:T(8,128)}, f32[4,128,2816]{2,1,0:T(8,128)}, f32[4,352,1024]{2,1,0:T(8,128)}, f32[32,3072]{1,0:T(8,128)}, f32[32,1024]{1,...) custom-call(bf16[8,2,4,352,128]{4,3,2,1,0:T(8,128)(2,1)} %get-tuple-element.25.pair, ...), custom_call_target="tpu_custom_call" | custom-call | tf_op jit(solution)/shard_map/pallas_call | solution.py:1288

commit v9 on v8

--- a/solution.py
+++ b/solution.py
@@ -15,7 +15,7 @@
 MESH = pl.DeviceIdType.MESH
 MASKS = (1, 2, 4, 3, 5, 6, 7)
 FILL = (7, 9, 4)
-PUMP = (7, 0, 12, 4, 2, 2)
+PUMP = (8, 0, 12, 4, 2, 1)
 LATE = (2, 3)
 EARLY = tuple(c for c in range(4) if c not in LATE)
 LATE_W = (2, 3)
@@ -601,7 +601,7 @@
     dx1 = keep[...] * gy[...].astype(F32) + rinv2 * n2 - x1 * (rinv2 * rinv2 * rinv2 * inner)
     dx1_s[...] = dx1
     dxb[...] = dx1.astype(BF)
-    weight_terms(ob, dxb, 0, terms.at[3])
+    weight_terms(ob, dxb, 0, terms)
     return jnp.sum(db * x1 * rinv2, axis=0, keepdims=True)
 
 
@@ -677,7 +677,7 @@
                 self.fetch(i, p + 1).start()
 
 
-def feed(p, gy_rows, b_rows, pair, wd, hid_out, grads, db, z):
+def feed(p, gy_rows, b_rows, pair, wd, hid_out, grads, db, send_db, z):
     nf, _, _, _, width = grads.shape
     b = b_rows[...]
     gate = nt(pair[0, p], b)
@@ -685,16 +685,17 @@
     dhid = nt(wd[...], gy_rows[...])
     s = jax.nn.sigmoid(gate)
     silu = gate * s
-    hid = (silu * up).astype(BF)
     dgate = (dhid * up * s * (1.0 + gate * (1.0 - s))).astype(BF)
     dup = (dhid * silu).astype(BF)
+    hid = (silu * up).astype(BF)
+    db[...] = (tn(dgate, pair[0, p]) + tn(dup, pair[1, p])).astype(BF)
+    send_db()
     hid_out[...] = hid
-    z[...] = tn(hid, wd[...]).astype(BF)
     for at, term in enumerate((dgate, dup)):
         grad = nn(term, b_rows[...]).astype(BF)
         for j in range(nf):
             grads[j, at, p] = grad[:, j * width : (j + 1) * width]
-    db[...] = (tn(dgate, pair[0, p]) + tn(dup, pair[1, p])).astype(BF)
+    z[...] = tn(hid, wd[...]).astype(BF)
 
 
 def layer_kernel(
@@ -842,8 +843,8 @@
             nf, nz, at, lambda p, m: at(flip(f, 2 * m), p), sib, rx, sems, home_sems, land, fr
         )
 
-    s_db = sums(2, db_sib, db_rx, sems_db, sems_db_home, db_rows)
-    s_z = sums(0, z_sib, z_rx, sems_z, sems_z_home, z_rows)
+    s_db = sums(0, db_sib, db_rx, sems_db, sems_db_home, db_rows)
+    s_z = sums(2, z_sib, z_rx, sems_z, sems_z_home, z_rows)
 
     def back_at(p):
         return lambda ff: back.at[ff, :, p]
@@ -874,9 +875,9 @@
         if p >= 2:
             save_hid(p - 2).wait()
         gy_rows, b_rows = rows_at(0, p), rows_at(2, p)
-        feed(p, gy_rows, b_rows, pair, wd, hid.at[p % 2], send, b_rows, gy_rows)
+        send_db = functools.partial(s_db.pairs, p)
+        feed(p, gy_rows, b_rows, pair, wd, hid.at[p % 2], send, gy_rows, send_db, b_rows)
         save_hid(p).start()
-        s_db.pairs(p)
         if p >= 1:
             s_db.chips(p - 1)
         if p >= 2:
@@ -902,10 +903,13 @@
         s_db.landed(p)
     s_db.finish()
 
+    def slot(c):
+        return big.at[(c + 2) % 4]
+
     def terms_of(table):
         return (
-            lambda ff, c: big.at[table[c], span(ff, nz * each)],
-            lambda c, m: big.at[table[c], span(flip(f, 2 * m), nz * each)],
+            lambda ff, c: slot(table[c]).at[span(ff, nz * each)],
+            lambda c, m: slot(table[c]).at[span(flip(f, 2 * m), nz * each)],
         )
 
     s_t = BlockSums(nf, nz, *terms_of(EARLY), t_sib, t_rx, t_sems, t_home, t_land, each)
@@ -922,7 +926,7 @@
         getattr(group, step)(at)
 
     dx1, dxb, do, dqkv = rows_grad, b_pos, gy_pos, qkv
-    gain2_grad = attention_bwd_in(npos, fr, db_rows, gy, keep, x1, ob, gain2, dx1, dxb, big)
+    gain2_grad = attention_bwd_in(npos, fr, db_rows, gy, keep, x1, ob, gain2, dx1, dxb, slot(3))
     both("pairs", 3)
     do[...] = nt(dxb[...], w[3]).astype(BF)
     both("along", 3)
@@ -930,16 +934,16 @@
         s_z.across(p)
     pump_back(PUMP[2])
     attention_bwd_heads(npos, qkv, do, dqkv)
-    weight_terms(a, dqkv, 2 * d, big.at[2])
+    weight_terms(a, dqkv, 2 * d, slot(2))
     both("pairs", 2)
     for p in range(lp):
         s_z.home(p)
     s_z.finish()
     pump_back(PUMP[3])
-    weight_terms(a, dqkv, 0, big.at[0])
+    weight_terms(a, dqkv, 0, slot(0))
     both("pairs", 0)
     both("along", 2)
-    weight_terms(a, dqkv, d, big.at[1])
+    weight_terms(a, dqkv, d, slot(1))
     both("pairs", 1)
     both("chips", 0)
     gain1_grad = attention_bwd_rows(x, dqkv, w, gain1, dx1, rows_grad)

time: 275 us -> 272 us (0.989); the launches traced: 272 us -> 272 us
  no operation moved by 1% of the time
where the time goes in v9:
time: 272 us
  Pallas kernels  271 us (100%)
    pallas_call x1, Pallas kernels, local_fused(): call(functools.partial(layer_kernel, nf, nz, npos, fr), 0, out_shape=(mak...  259 us
    pallas_call x1, Pallas kernels, local_fused(): pl.pallas_call(last_local_kernel, grid=(lp,), out_shape=(make((lp, dslice...  12.2 us

profile of v9, /device:TPU:0, one launch (start us, length us, event | category | flops | bytes accessed | tf_op | source)
XLA Modules:
  0.0 272.0 jit_solution(13795061571988764783)
XLA Ops:
  0.6 259.0 %shard_map.169 = (bf16[256,1024]{1,0:T(8,128)(2,1)}, f32[256,1024]{1,0:T(8,128)}, f32[32,4096]{1,0:T(8,128)}, f32[32,128]{1,0:T(8,128)}, bf16[2,1024,1024]{2,1,0...) custom-call(bf16[256,1024]{1,0:T(8,128)(2,1)} %bitcast.9, bf16[256,1024]{1,0:T(8,128)(2,1)} %bitcast.10, ...), custom_call_target="tpu_custom_call" | custom-call | tf_op jit(solution)/shard_map/pallas_call | solution.py:1229
  259.6 12.2 %shard_map.170 = (f32[4,128,2816]{2,1,0:T(8,128)}, f32[4,128,2816]{2,1,0:T(8,128)}, f32[4,352,1024]{2,1,0:T(8,128)}, f32[32,3072]{1,0:T(8,128)}, f32[32,1024]{1,...) custom-call(bf16[8,2,4,352,128]{4,3,2,1,0:T(8,128)(2,1)} %get-tuple-element.25.pair, ...), custom_call_target="tpu_custom_call" | custom-call | tf_op jit(solution)/shard_map/pallas_call | solution.py:1292

commit v10 on v9

--- a/solution.py
+++ b/solution.py
@@ -565,7 +565,7 @@
             p1 = soft(jnp.where(low, zero, q), k, mask).astype(BF)
             ob[at, pl.ds(pl.multiple_of(i * 2 * HD, 2 * HD), 2 * HD)] = jnp.where(low, nn(p0, v), nn(p1, v)).astype(BF)
         return c
-    lax.fori_loop(0, d // (2 * HD), heads, 0)
+    lax.fori_loop(0, d // (2 * HD), heads, 0, unroll=2)
 
 
 def attention_end(npos, fr, x, gain2, w_out, ob, x1_out, b_out):
@@ -629,7 +629,7 @@
                 dqkv[at, lanes[t]] = jnp.where(low, parts[0][t], parts[1][t]).astype(BF)
         return c
 
-    lax.fori_loop(0, d // (2 * HD), heads, 0)
+    lax.fori_loop(0, d // (2 * HD), heads, 0, unroll=2)
 
 
 def attention_bwd_rows(x, dqkv, w, gain1, dx1, rows_out):

time: 272 us -> 272 us (level)
  no operation moved by 1% of the time
where the time goes in v10:
time: 272 us
  Pallas kernels  271 us (100%)
    pallas_call x1, Pallas kernels, local_fused(): call(functools.partial(layer_kernel, nf, nz, npos, fr), 0, out_shape=(mak...  258 us
    pallas_call x1, Pallas kernels, local_fused(): pl.pallas_call(last_local_kernel, grid=(lp,), out_shape=(make((lp, dslice...  12.2 us

profile of v10, /device:TPU:0, one launch (start us, length us, event | category | flops | bytes accessed | tf_op | source)
XLA Modules:
  0.0 271.5 jit_solution(13298510259907440299)
XLA Ops:
  0.6 258.5 %shard_map.169 = (bf16[256,1024]{1,0:T(8,128)(2,1)}, f32[256,1024]{1,0:T(8,128)}, f32[32,4096]{1,0:T(8,128)}, f32[32,128]{1,0:T(8,128)}, bf16[2,1024,1024]{2,1,0...) custom-call(bf16[256,1024]{1,0:T(8,128)(2,1)} %bitcast.9, bf16[256,1024]{1,0:T(8,128)(2,1)} %bitcast.10, ...), custom_call_target="tpu_custom_call" | custom-call | tf_op jit(solution)/shard_map/pallas_call | solution.py:1229
  259.1 12.2 %shard_map.170 = (f32[4,128,2816]{2,1,0:T(8,128)}, f32[4,128,2816]{2,1,0:T(8,128)}, f32[4,352,1024]{2,1,0:T(8,128)}, f32[32,3072]{1,0:T(8,128)}, f32[32,1024]{1,...) custom-call(bf16[8,2,4,352,128]{4,3,2,1,0:T(8,128)(2,1)} %get-tuple-element.25.pair, ...), custom_call_target="tpu_custom_call" | custom-call | tf_op jit(solution)/shard_map/pallas_call | solution.py:1292
